TPU v7x, 128 devices: a whole 4x4x4 slice. The times are simulated.
128 devices in a mesh: grid: 8 (over z, core), line: 16 (over x, y).
Axes of the slice: x: 4, y: 4, z: 4, core: 2. Of those that a mesh axis runs over, the one named last changes fastest.
Arguments:
- les: float32 [24, 8, 2048], P(None, 'grid', 'line'), may hold values from -6 to 6
- lines: float32 [8, 16, 128, 24, 128], P('grid', 'line'), may hold values from -6 to 6
- triplet_start: int32 [2, 8, 16, 128], P(None, 'grid', 'line'), may hold values from 0 to 80
- splice_owner: int32 [2, 8, 16, 128, 1], P(None, 'grid', 'line'), may hold values from 0 to 127; in each aligned block of 128 rows (0 to 127, 128 to 255, ..., all dimensions but the last counted through in order) at most 2 rows name the same one
- splice_line: int32 [2, 8, 16, 128], P(None, 'grid', 'line'), may hold values from 0 to 127
- splice_from: int32 [2, 8, 16, 128], P(None, 'grid', 'line'), may hold values from 0 to 7
- splice_to: int32 [2, 8, 16, 128], P(None, 'grid', 'line'), may hold values from 0 to 7
- chem_counts: int32 [8, 16, 128], P('grid', 'line'), may hold values from 1 to 6, as said below
- diffusivity: float32 [24], replicated, may hold values from 0.5 to 20
- rates: float32 [24, 24], replicated, may hold values from -1.25 to 1.25
- frozen_inverse: float32 [24, 24], replicated, may hold values from -0.3 to 0.5
Outputs:
- les_out: float32 [24, 8, 2048], P(None, 'grid', 'line')
- lines_out: float32 [8, 16, 128, 24, 128], P('grid', 'line')
Inputs may be any that keep to these rules, and one draw needn't show every extreme that they name: `splice_owner`: in the rows of one device and one step no owner is named more than 2 times, a bound that some block reaches. `chem_counts`: some line has 6 substeps.
All inputs are finite; a program needn't handle non-finite values.
Results may differ from a plain program's by a relative error of at most 0.0003.
Values sent between devices are 32-bit elements; how exact they have to be, the bound alone decides.
No kernel may reach another device: no remote copies, remote signals or barrier semaphores. Data moves between devices by JAX's collectives and lax.ppermute only.
A program may use at most 64 MiB of HBM per device.

v0:
```python
import jax
import jax.numpy as jnp
import numpy as np
from jax import lax
from jax.experimental import pallas as pl
from jax.experimental.pallas import tpu as pltpu
from jax.sharding import PartitionSpec as P

SEG = 16
TRIP = 48
KMAX = 6
STEPS = 2
LES_RATE = 0.2
SPECIES = 24
POINTS = 128
LINES = 128
OWNERS = 128
ROWS = 8
F32 = jnp.float32
BF16 = jnp.bfloat16


def cosine_tables():
    k = np.arange(POINTS)[:, None]
    p = np.arange(POINTS)[None, :]
    basis = np.sqrt(2.0 / POINTS) * np.cos(np.pi * k * (2 * p + 1) / (2 * POINTS))
    basis[0] = 1.0 / np.sqrt(POINTS)
    tables = []
    for table in (basis.T, basis):
        high = table.astype(BF16)
        low = (table - high.astype(np.float64)).astype(BF16)
        half = np.concatenate([high, low], axis=1)
        tables.append(np.concatenate([half, half], axis=0))
    eigen = 4.0 * np.sin(np.pi * np.arange(POINTS) / (2 * POINTS)) ** 2
    return tables[0], tables[1], eigen.astype(np.float32)[None, :]


def halves(value):
    high = value.astype(BF16)
    return high, (value - high.astype(F32)).astype(BF16)


def dot(a, b):
    return jnp.dot(a, b, preferred_element_type=F32)


def iota(axis, shape=(LINES, POINTS)):
    return lax.broadcasted_iota(jnp.int32, shape, axis)


def column(row):
    return jnp.transpose(jnp.broadcast_to(row.astype(F32), (LINES, POINTS)))


def lane_pick(value, index):
    return jnp.take_along_axis(value, index, axis=1, mode="promise_in_bounds")


def mix_tables(rates, frozen, high_ref, low_ref):
    exact = dict(precision=lax.Precision.HIGHEST, preferred_element_type=F32)
    matrix = jnp.dot(frozen, rates, **exact)
    side = SPECIES * 8
    spread = (iota(0, (side, SPECIES)) // 8 == iota(1, (side, SPECIES))).astype(F32)
    gather = (iota(0, (SPECIES, side)) == iota(1, (SPECIES, side)) // 8).astype(F32)
    wide = jnp.dot(jnp.dot(spread, matrix, **exact), gather, **exact)
    same = iota(0, (side, side)) % 8 == iota(1, (side, side)) % 8
    high, low = halves(jnp.where(same, wide, 0.0))
    high_ref[...] = high
    low_ref[...] = low


def middle(les, north, south, west, east):
    lane = iota(1, (SPECIES, LINES))
    left = jnp.where(lane == 0, pltpu.roll(west, 1, 1), pltpu.roll(les, 1, 1))
    right = jnp.where(lane == LINES - 1, pltpu.roll(east, LINES - 1, 1), pltpu.roll(les, LINES - 1, 1))
    return les + LES_RATE * (north + south + left + right - 4.0 * les)


def turned(value):
    pad = jnp.zeros((POINTS - SPECIES, LINES), F32)
    return jnp.transpose(jnp.concatenate([value, pad], axis=0))


def triplet_index(start):
    place = iota(1)
    start = start.astype(jnp.int32)
    rel = place - start
    third = TRIP // 3
    source = jnp.where(
        rel < third,
        3 * rel,
        jnp.where(rel < 2 * third, 3 * (2 * third - 1 - rel) + 1, 3 * (rel - 2 * third) + 2),
    )
    return jnp.where((rel >= 0) & (rel < TRIP), source + start, place)


def mixing(read, start_row, mid, diffusivity_ref, eigen_ref, first_ref, second_ref, state_ref, index_ref, shift_ref):
    index_ref[...] = triplet_index(column(start_row))
    shift_ref[...] = turned(0.5 * mid)
    lane = iota(1, (1, POINTS))

    def one(s, carry):
        value = lane_pick(read(s), index_ref[...])
        high, low = halves(value)
        wide = dot(jnp.concatenate([high, low], axis=1), first_ref[...])
        scale = 1.0 / (1.0 + diffusivity_ref[s] * eigen_ref[...])
        scale = jnp.where(lane == 0, 0.5, scale)
        high, low = halves((wide[:, :POINTS] + wide[:, POINTS:]) * scale)
        wide = dot(jnp.concatenate([high, low], axis=1), second_ref[...])
        shift = lane_pick(shift_ref[...], jnp.full((LINES, POINTS), s, jnp.int32))
        state_ref[s] = wide[:, :POINTS] + wide[:, POINTS:] + shift
        return carry

    lax.fori_loop(0, SPECIES, one, 0, unroll=2)


def chemistry(counts_row, high_ref, low_ref, state_ref, counts_ref):
    counts_ref[...] = column(counts_row)
    side = SPECIES * 8

    def substep(sub, carry):
        turn = sub.astype(F32)
        for unit in range(LINES // 16):
            parts = [slice(16 * unit, 16 * unit + 8), slice(16 * unit + 8, 16 * unit + 16)]
            old = [state_ref[:, part, :].reshape(side, POINTS) for part in parts]
            high, low = halves(jnp.tanh(jnp.concatenate(old, axis=1)))
            change = dot(high_ref[...], high) + (dot(low_ref[...], high) + dot(high_ref[...], low))
            for at, part in enumerate(parts):
                active = (counts_ref[part, :] > turn)[None]
                before = old[at].reshape(SPECIES, 8, POINTS)
                after = before + change[:, at * POINTS : (at + 1) * POINTS].reshape(SPECIES, 8, POINTS)
                state_ref[:, part, :] = jnp.where(active, after, before)
        return carry

    lax.fori_loop(0, KMAX, substep, 0)


def packing(owner_row, line_row, from_row, to_row, state_ref, out_ref, send_ref):
    lane = iota(1)
    pick = column(from_row).astype(jnp.int32) * SEG + lane % SEG
    group = lane // SEG
    for third in range(3):
        gathered = jnp.zeros((LINES, POINTS), F32)
        for s in range(8):
            gathered = jnp.where(group == s, lane_pick(state_ref[8 * third + s], pick), gathered)
        high, low = halves(gathered)
        out_ref[:LINES, third * POINTS : (third + 1) * POINTS] = high
        out_ref[LINES:, third * POINTS : (third + 1) * POINTS] = low
    owner = column(owner_row).astype(jnp.int32)
    earlier = (owner == owner_row) & (iota(0) < lane)
    rank = jnp.sum(earlier.astype(F32), axis=0, keepdims=True)
    aims = jnp.where(lane < 64, column(line_row) + 1.0, column(to_row)).astype(BF16)
    for slot in range(2):
        placing = ((iota(0) == owner_row) & (rank == slot)).astype(F32).astype(BF16)
        sending = dot(jnp.concatenate([placing, placing], axis=1), out_ref[...])
        for third in range(3):
            send_ref[pl.ds(3 * slot + third, OWNERS, stride=ROWS), :] = sending[
                :, third * POINTS : (third + 1) * POINTS
            ]
        send_ref[pl.ds(6 + slot, OWNERS, stride=ROWS), :] = dot(placing, aims)


def splicing(received_ref, state_ref, write, parts_ref, place_ref, land_ref):
    lane = iota(1)
    for slot in range(2):
        aim = received_ref[pl.ds(6 + slot, OWNERS, stride=ROWS), :]
        line = jnp.broadcast_to(aim[:, :1], (OWNERS, LINES)).astype(jnp.int32) - 1
        segment = jnp.broadcast_to(aim[:, 64:65], (OWNERS, POINTS)).astype(jnp.int32)
        hit = jnp.transpose((line == lane).astype(F32)).astype(BF16)
        place_ref[:, slot * OWNERS : (slot + 1) * OWNERS] = hit
        place_ref[:, (2 + slot) * OWNERS : (3 + slot) * OWNERS] = hit
        land_ref[slot * OWNERS : (slot + 1) * OWNERS, :] = (segment == lane // SEG).astype(F32)
        for third in range(3):
            parts_ref[third, slot * OWNERS : (slot + 1) * OWNERS, :] = received_ref[
                pl.ds(3 * slot + third, OWNERS, stride=ROWS), :
            ]
    arrivals = dot(place_ref[:, : 2 * OWNERS], land_ref[...].astype(BF16))
    both = iota(1, (2 * OWNERS, POINTS)) % SEG

    def one(s, means):
        piece = lane_pick(parts_ref[s // 8], both + (s % 8) * SEG)
        high, low = halves(jnp.where(land_ref[...] > 0.5, piece, 0.0))
        gained = dot(place_ref[...], jnp.concatenate([high, low], axis=0))
        old = state_ref[s]
        new = old + 0.5 * (gained - arrivals * old)
        write(s, new)
        mean = jnp.sum(new, axis=1, keepdims=True) * (1.0 / POINTS)
        return jnp.where(lane == s, mean, means)

    means = lax.fori_loop(0, SPECIES, one, jnp.zeros((LINES, POINTS), F32), unroll=2)
    return jnp.transpose(means)[:SPECIES]


def step_kernel(
    step, first, lines_ref, les_ref, north_ref, south_ref, west_ref, east_ref, start_ref, owner_ref, line_ref, from_ref,
    to_ref, counts_ref, diffusivity_ref, eigen_ref, first_ref, second_ref, a_ref, b_ref, *rest,
):
    if first:
        state_ref, send_ref, mid_ref, high_ref, low_ref, index_ref, shift_ref, turns_ref, out_ref = rest
        mix_tables(a_ref[...], b_ref[...], high_ref, low_ref)

        def read(s):
            return lines_ref[pl.ds(s, LINES, stride=SPECIES), :]
    else:
        state_ref, send_ref, mid_ref, index_ref, shift_ref, turns_ref, out_ref = rest
        high_ref, low_ref = a_ref, b_ref

        def read(s):
            return lines_ref[s]

    mid = middle(les_ref[:, 0], north_ref[:, 0], south_ref[:, 0], west_ref[:, 0], east_ref[:, 0])
    mid_ref[...] = mid
    mixing(
        read, start_ref[step, 0], mid, diffusivity_ref, eigen_ref, first_ref, second_ref, state_ref, index_ref, shift_ref
    )
    chemistry(counts_ref[0], high_ref, low_ref, state_ref, turns_ref)
    packing(owner_ref[step, 0], line_ref[step, 0], from_ref[step, 0], to_ref[step, 0], state_ref, out_ref, send_ref)


def splice_kernel(last, received_ref, state_ref, mid_ref, les_ref, lines_ref, parts_ref, place_ref, land_ref):
    def write(s, value):
        if last:
            lines_ref[pl.ds(s, LINES, stride=SPECIES), :] = value
        else:
            lines_ref[s] = value

    means = splicing(received_ref, state_ref, write, parts_ref, place_ref, land_ref)
    les_ref[:, 0] = 0.5 * mid_ref[...] + 0.5 * means


VMEM = pl.BlockSpec(memory_space=pltpu.VMEM)
SMEM = pl.BlockSpec(memory_space=pltpu.SMEM)
STATE = jax.ShapeDtypeStruct((SPECIES, LINES, POINTS), F32)


def call(kernel, inputs, outputs, scratch, flops):
    shapes = [x for x in outputs]
    specs = [SMEM if smem else VMEM for _, smem in inputs]
    size = sum(x.size * x.dtype.itemsize for x, _ in inputs) + sum(x.size * x.dtype.itemsize for x in shapes)
    return pl.pallas_call(
        kernel,
        out_shape=shapes,
        in_specs=specs,
        out_specs=[VMEM] * len(shapes),
        scratch_shapes=scratch,
        cost_estimate=pl.CostEstimate(flops=flops, bytes_accessed=size, transcendentals=0),
        compiler_params=pltpu.CompilerParams(vmem_limit_bytes=40 << 20),
    )(*[x for x, _ in inputs])


def beside(field):
    around = []
    for axis in ("grid", "line"):
        peers = lax.axis_size(axis)
        up = [(i, i + 1) for i in range(peers - 1)]
        around.append(lax.ppermute(field, axis, up))
        around.append(lax.ppermute(field, axis, [(b, a) for a, b in up]))
    return around


def body(
    les,
    lines,
    triplet_start,
    splice_owner,
    splice_line,
    splice_from,
    splice_to,
    chem_counts,
    diffusivity,
    rates,
    frozen_inverse,
):
    first_table, second_table, eigen = (jnp.asarray(x) for x in cosine_tables())
    side = SPECIES * 8
    tables = [jax.ShapeDtypeStruct((side, side), BF16)] * 2
    send = jax.ShapeDtypeStruct((OWNERS * ROWS, POINTS), F32)
    mid_shape = jax.ShapeDtypeStruct((SPECIES, LINES), F32)
    owner = splice_owner.reshape(STEPS, 1, 1, LINES)
    field = les
    state = lines.reshape(LINES * SPECIES, POINTS)
    mix = (rates, frozen_inverse)
    for step in range(STEPS):
        last = step == STEPS - 1
        rim = beside(field)
        inputs = [(x, False) for x in (state, field, *rim, triplet_start, owner, splice_line, splice_from, splice_to, chem_counts)]
        inputs += [(diffusivity, True)] + [(x, False) for x in (eigen, first_table, second_table, *mix)]
        scratch = [
            pltpu.VMEM((LINES, POINTS), jnp.int32),
            pltpu.VMEM((LINES, POINTS), F32),
            pltpu.VMEM((LINES, POINTS), F32),
            pltpu.VMEM((2 * LINES, 3 * POINTS), BF16),
        ]
        first = step == 0

        def advance(*refs, step=step, first=first):
            step_kernel(step, first, *refs)

        outs = call(advance, inputs, [STATE, send, mid_shape] + (tables if first else []), scratch, 4 * 10**9)
        state, sending, mid = outs[:3]
        if first:
            mix = outs[3:]
        received = lax.all_to_all(
            sending.reshape(OWNERS, ROWS, POINTS), ("grid", "line"), split_axis=0, concat_axis=0, tiled=True
        ).reshape(OWNERS * ROWS, POINTS)
        scratch = [
            pltpu.VMEM((3, 2 * OWNERS, POINTS), F32),
            pltpu.VMEM((LINES, 4 * OWNERS), BF16),
            pltpu.VMEM((2 * OWNERS, POINTS), F32),
        ]
        after = jax.ShapeDtypeStruct((LINES * SPECIES, POINTS), F32) if last else STATE

        def land(*refs, last=last):
            splice_kernel(last, *refs)

        field, state = call(
            land, [(x, False) for x in (received, state, mid)], [jax.ShapeDtypeStruct(les.shape, F32), after], scratch, 10**9
        )
    return (field, state.reshape(lines.shape))


def solution(mesh):
    in_specs = (
        P(None, "grid", "line"),
        P("grid", "line", None, None, None),
        P(None, "grid", "line", None),
        P(None, "grid", "line", None, None),
        P(None, "grid", "line", None),
        P(None, "grid", "line", None),
        P(None, "grid", "line", None),
        P("grid", "line", None),
        P(),
        P(),
        P(),
    )
    out_specs = (P(None, "grid", "line"), P("grid", "line", None, None, None))
    return jax.shard_map(body, mesh=mesh, in_specs=in_specs, out_specs=out_specs, check_vma=False)
```

profile of v0, /device:TPU:1, one launch (start us, length us, event | category | flops | bytes accessed | tf_op | source)
XLA Modules:
  0.0 120.8 jit_solution(3321748067771000023)
XLA Ops:
  0.6 4.0 %collective-permute-start.2 = (f32[24,1,128]{2,1,0:T(1,128)}, f32[24,1,128]{2,1,0:T(1,128)S(1)}, u32[]{:S(2)}, u32[]{:S(2)}) collective-permute-start(f32[24,1,128]{2,1,0:T(1,128)} %refs_1_.1), channel_id=1, source_target_pairs={{0,1},{1,2},{2,3},{3,4},{4,5},{5,6},{6,7},{7,8},{8,9},{9,10},{10,1... | collective-permute-start | bytes 36872 | tf_op jit(solution)/shard_map/ppermute | solution.py:256
  4.7 2.9 %collective-permute-start.1 = (f32[24,1,128]{2,1,0:T(1,128)}, f32[24,1,128]{2,1,0:T(1,128)S(1)}, u32[]{:S(2)}, u32[]{:S(2)}) collective-permute-start(f32[24,1,128]{2,1,0:T(1,128)} %refs_1_.1), channel_id=1, source_target_pairs={{16,0},{32,16},{48,32},{64,48},{80,64},{96,80},{112,96},{17,1},{33... | collective-permute-start | bytes 36872 | tf_op jit(solution)/shard_map/ppermute | solution.py:257
  7.5 3.4 %collective-permute-start = (f32[24,1,128]{2,1,0:T(1,128)}, f32[24,1,128]{2,1,0:T(1,128)S(1)}, u32[]{:S(2)}, u32[]{:S(2)}) collective-permute-start(f32[24,1,128]{2,1,0:T(1,128)} %refs_1_.1), channel_id=1, source_target_pairs={{0,16},{16,32},{32,48},{48,64},{64,80},{80,96},{96,112},{1,17},{17... | collective-permute-start | bytes 36872 | tf_op jit(solution)/shard_map/ppermute | solution.py:256
  11.0 1.3 %collective-permute-start.3 = (f32[24,1,128]{2,1,0:T(1,128)}, f32[24,1,128]{2,1,0:T(1,128)S(1)}, u32[]{:S(2)}, u32[]{:S(2)}) collective-permute-start(f32[24,1,128]{2,1,0:T(1,128)} %refs_1_.1), channel_id=1, source_target_pairs={{1,0},{2,1},{3,2},{4,3},{5,4},{6,5},{7,6},{8,7},{9,8},{10,9},{11,1... | collective-permute-start | bytes 36872 | tf_op jit(solution)/shard_map/ppermute | solution.py:257
  12.3 3.3 %collective-permute-done.3.refs_5_ = f32[24,1,128]{2,1,0:T(1,128)S(1)} collective-permute-done((f32[24,1,128]{2,1,0:T(1,128)}, f32[24,1,128]{2,1,0:T(1,128)S(1)}, u32[]{:S(2)}, u32[]{:S(2)}) %collective-permute-start.3) | collective-permute-done | bytes 12320 | tf_op jit(solution)/shard_map/ppermute | solution.py:257
  15.6 1.4 %copy-done = f32[1,1,128,24,128]{4,3,2,1,0:T(8,128)S(1)} copy-done((f32[1,1,128,24,128]{4,3,2,1,0:T(8,128)S(1)}, f32[1,1,128,24,128]{4,3,2,1,0:T(8,128)}, u32[]{:S(2)}) %copy-start) | copy-done | bytes 1572888
  17.1 0.7 copy-done.1
  17.8 0.7 copy-done.2
  18.5 0.7 copy-done.3
  19.2 0.7 copy-done.4
  19.9 0.7 copy-done.6
  20.5 0.7 copy-done.8
  21.2 0.7 copy-done.10
  21.9 0.7 copy-done.12
  22.6 0.7 copy-done.14
  23.2 0.7 copy-done.16
  23.9 0.9 copy-done.18
  24.8 0.9 copy-done.20
  25.7 0.7 copy-done.22
  26.3 12.9 %shard_map.149 = (f32[24,128,128]{2,1,0:T(8,128)S(1)}, f32[1024,128]{1,0:T(8,128)S(1)}, f32[24,128]{1,0:T(8,128)S(1)}, bf16[192,192]{1,0:T(8,128)(2,1)S(1)}, bf16[192,192]{1,0:T(8,128)(2,1)S(1)}) custom-call(f32[3072,128]{1,0:T(8,128)S(1)} %bitcast.11, f32[24,1,128]{2,1,0:T(1,128)S(1)} %copy-done.1, f32[24,1,128]{2,1,0:T(1,128)S(1)} %collective-permute-done.refs_2_, ...), custom_call_target="tpu_custom_call" | custom-call | flops 4000000000 | bytes 4164192 | tf_op jit(solution)/shard_map/pallas_call | solution.py:240
  39.2 24.5 %all_to_all.10 = f32[128,8,128]{2,1,0:T(8,128)S(1)} all-to-all(f32[128,8,128]{2,1,0:T(8,128)S(1)} %bitcast.8), channel_id=1, replica_groups=mesh['grid'=8,'line'=16] {'grid','line'}, dimensions={0} | all-to-all | bytes 1048576 | tf_op jit(solution)/shard_map/all_to_all | solution.py:303
  63.8 0.0 copy-start.19
  63.8 0.0 copy-start.21
  63.8 5.2 %shard_map.150 = (f32[24,1,128]{2,1,0:T(1,128)S(1)}, f32[24,128,128]{2,1,0:T(8,128)S(1)}) custom-call(f32[1024,128]{1,0:T(8,128)S(1)} %bitcast.10, f32[24,128,128]{2,1,0:T(8,128)S(1)} %get-tuple-element.15.refs_1_, f32[24,128]{1,0:T(8,128)S(1)} %get-tuple-element.16.refs_2_), custom_call_target="tpu_custom_call" | custom-call | flops 1000000000 | bytes 3694592 | tf_op jit(solution)/shard_map/pallas_call | solution.py:240
  69.0 1.3 %collective-permute-start.7 = (f32[24,1,128]{2,1,0:T(1,128)S(1)}, f32[24,1,128]{2,1,0:T(1,128)S(1)}, u32[]{:S(2)}, u32[]{:S(2)}) collective-permute-start(f32[24,1,128]{2,1,0:T(1,128)S(1)} %get-tuple-element.18.refs_1_), channel_id=1, source_target_pairs={{1,0},{2,1},{3,2},{4,3},{5,4},{6,5},{7,6},{8,7},{9,8},{10,9},{11,1... | collective-permute-start | bytes 36872 | tf_op jit(solution)/shard_map/ppermute | solution.py:257
  70.3 4.0 %collective-permute-start.6 = (f32[24,1,128]{2,1,0:T(1,128)S(1)}, f32[24,1,128]{2,1,0:T(1,128)S(1)}, u32[]{:S(2)}, u32[]{:S(2)}) collective-permute-start(f32[24,1,128]{2,1,0:T(1,128)S(1)} %get-tuple-element.18.refs_1_), channel_id=1, source_target_pairs={{0,1},{1,2},{2,3},{3,4},{4,5},{5,6},{6,7},{7,8},{8,9},{9,10},{10,1... | collective-permute-start | bytes 36872 | tf_op jit(solution)/shard_map/ppermute | solution.py:256
  74.3 3.8 %collective-permute-start.5 = (f32[24,1,128]{2,1,0:T(1,128)S(1)}, f32[24,1,128]{2,1,0:T(1,128)S(1)}, u32[]{:S(2)}, u32[]{:S(2)}) collective-permute-start(f32[24,1,128]{2,1,0:T(1,128)S(1)} %get-tuple-element.18.refs_1_), channel_id=1, source_target_pairs={{16,0},{32,16},{48,32},{64,48},{80,64},{96,80},{112,96},{17,1},{33... | collective-permute-start | bytes 36872 | tf_op jit(solution)/shard_map/ppermute | solution.py:257
  78.1 2.4 %collective-permute-start.4 = (f32[24,1,128]{2,1,0:T(1,128)S(1)}, f32[24,1,128]{2,1,0:T(1,128)S(1)}, u32[]{:S(2)}, u32[]{:S(2)}) collective-permute-start(f32[24,1,128]{2,1,0:T(1,128)S(1)} %get-tuple-element.18.refs_1_), channel_id=1, source_target_pairs={{0,16},{16,32},{32,48},{48,64},{64,80},{80,96},{96,112},{1,17},{17... | collective-permute-start | bytes 36872 | tf_op jit(solution)/shard_map/ppermute | solution.py:256
  80.5 0.8 collective-permute-done.4.refs_2_
  81.4 12.5 %shard_map.151 = (f32[24,128,128]{2,1,0:T(8,128)S(1)}, f32[1024,128]{1,0:T(8,128)S(1)}, f32[24,128]{1,0:T(8,128)S(1)}) custom-call(f32[24,128,128]{2,1,0:T(8,128)S(1)} %get-tuple-element.17.refs_0_, f32[24,1,128]{2,1,0:T(1,128)S(1)} %get-tuple-element.18.refs_1_, f32[24,1,128]{2,1,0:T(1,128)S(1)} %collective-permute-done.4.refs_2_, ...), custom_call_target="tpu_custom_call" | custom-call | flops 4000000000 | bytes 4159584 | tf_op jit(solution)/shard_map/pallas_call | solution.py:240
  93.9 20.7 %all_to_all.11 = f32[128,8,128]{2,1,0:T(8,128)S(1)} all-to-all(f32[128,8,128]{2,1,0:T(8,128)S(1)} %bitcast.7), channel_id=1, replica_groups=mesh['grid'=8,'line'=16] {'grid','line'}, dimensions={0} | all-to-all | bytes 1048576 | tf_op jit(solution)/shard_map/all_to_all | solution.py:303
  114.6 6.2 %shard_map.152 = (f32[24,1,128]{2,1,0:T(1,128)}, f32[3072,128]{1,0:T(8,128)}) custom-call(f32[1024,128]{1,0:T(8,128)S(1)} %bitcast.9, f32[24,128,128]{2,1,0:T(8,128)S(1)} %get-tuple-element.22.refs_1_, f32[24,128]{1,0:T(8,128)S(1)} %get-tuple-element.23.refs_2_), custom_call_target="tpu_custom_call" | custom-call | flops 1000000000 | bytes 3694592 | tf_op jit(solution)/shard_map/pallas_call | solution.py:240
  (38 shorter events, 0.1 us)
Async XLA Ops:
  0.6 11.7 %collective-permute-start.2 = (f32[24,1,128]{2,1,0:T(1,128)}, f32[24,1,128]{2,1,0:T(1,128)S(1)}, u32[]{:S(2)}, u32[]{:S(2)}) collective-permute-start(f32[24,1,128]{2,1,0:T(1,128)} %refs_1_.1), channel_id=1, source_target_pairs={{0,1},{1,2},{2,3},{3,4},{4,5},{5,6},{6,7},{7,8},{8,9},{9,10},{10,1... | collective-permute-start | bytes 36872 | tf_op jit(solution)/shard_map/ppermute | solution.py:256
  4.7 7.6 %collective-permute-start.1 = (f32[24,1,128]{2,1,0:T(1,128)}, f32[24,1,128]{2,1,0:T(1,128)S(1)}, u32[]{:S(2)}, u32[]{:S(2)}) collective-permute-start(f32[24,1,128]{2,1,0:T(1,128)} %refs_1_.1), channel_id=1, source_target_pairs={{16,0},{32,16},{48,32},{64,48},{80,64},{96,80},{112,96},{17,1},{33... | collective-permute-start | bytes 36872 | tf_op jit(solution)/shard_map/ppermute | solution.py:257
  7.5 4.8 %collective-permute-start = (f32[24,1,128]{2,1,0:T(1,128)}, f32[24,1,128]{2,1,0:T(1,128)S(1)}, u32[]{:S(2)}, u32[]{:S(2)}) collective-permute-start(f32[24,1,128]{2,1,0:T(1,128)} %refs_1_.1), channel_id=1, source_target_pairs={{0,16},{16,32},{32,48},{48,64},{64,80},{80,96},{96,112},{1,17},{17... | collective-permute-start | bytes 36872 | tf_op jit(solution)/shard_map/ppermute | solution.py:256
  11.0 4.6 %collective-permute-start.3 = (f32[24,1,128]{2,1,0:T(1,128)}, f32[24,1,128]{2,1,0:T(1,128)S(1)}, u32[]{:S(2)}, u32[]{:S(2)}) collective-permute-start(f32[24,1,128]{2,1,0:T(1,128)} %refs_1_.1), channel_id=1, source_target_pairs={{1,0},{2,1},{3,2},{4,3},{5,4},{6,5},{7,6},{8,7},{9,8},{10,9},{11,1... | collective-permute-start | bytes 36872 | tf_op jit(solution)/shard_map/ppermute | solution.py:257
  15.6 1.4 %copy-start = (f32[1,1,128,24,128]{4,3,2,1,0:T(8,128)S(1)}, f32[1,1,128,24,128]{4,3,2,1,0:T(8,128)}, u32[]{:S(2)}) copy-start(f32[1,1,128,24,128]{4,3,2,1,0:T(8,128)} %param.15) | copy-start | bytes 4718596
  17.0 0.7 copy-start.1
  17.8 0.7 copy-start.2
  18.5 0.7 copy-start.3
  19.2 0.7 copy-start.4
  19.9 0.7 copy-start.6
  20.5 0.7 copy-start.8
  21.2 0.7 copy-start.10
  21.9 0.7 copy-start.12
  22.6 0.7 copy-start.14
  23.2 0.7 copy-start.16
  23.9 0.9 copy-start.18
  24.8 0.9 copy-start.20
  25.7 0.7 copy-start.22
  63.7 17.6 %copy-start.5 = (s32[2,1,1,128]{3,2,1,0:T(1,128)S(1)}, s32[2,1,1,128]{3,2,1,0:T(1,128)}, u32[]{:S(2)}) copy-start(s32[2,1,1,128]{3,2,1,0:T(1,128)} %refs_6_.3) | copy-start | bytes 3076
  63.7 17.6 %copy-start.7 = (s32[2,1,1,128,1]{3,4,2,1,0:T(1,128)S(1)}, s32[2,1,1,128,1]{3,4,2,1,0:T(1,128)}, u32[]{:S(2)}) copy-start(s32[2,1,1,128,1]{3,4,2,1,0:T(1,128)} %param.17) | copy-start | bytes 3076
  63.7 17.6 %copy-start.9 = (s32[2,1,1,128]{3,2,1,0:T(1,128)S(1)}, s32[2,1,1,128]{3,2,1,0:T(1,128)}, u32[]{:S(2)}) copy-start(s32[2,1,1,128]{3,2,1,0:T(1,128)} %refs_8_.3) | copy-start | bytes 3076
  63.7 17.6 %copy-start.11 = (s32[2,1,1,128]{3,2,1,0:T(1,128)S(1)}, s32[2,1,1,128]{3,2,1,0:T(1,128)}, u32[]{:S(2)}) copy-start(s32[2,1,1,128]{3,2,1,0:T(1,128)} %refs_9_.3) | copy-start | bytes 3076
  63.7 17.6 %copy-start.13 = (s32[2,1,1,128]{3,2,1,0:T(1,128)S(1)}, s32[2,1,1,128]{3,2,1,0:T(1,128)}, u32[]{:S(2)}) copy-start(s32[2,1,1,128]{3,2,1,0:T(1,128)} %refs_10_.3) | copy-start | bytes 3076
  63.7 17.6 %copy-start.15 = (s32[1,1,128]{2,1,0:T(1,128)S(1)}, s32[1,1,128]{2,1,0:T(1,128)}, u32[]{:S(2)}) copy-start(s32[1,1,128]{2,1,0:T(1,128)} %refs_11_.3) | copy-start | bytes 1540
  63.7 17.6 %copy-start.17 = (f32[24]{0:T(128)S(1)}, f32[24]{0:T(128)}, u32[]{:S(2)}) copy-start(f32[24]{0:T(128)} %refs_12_.3) | copy-start | bytes 292
  63.8 17.6 %copy-start.19 = (bf16[256,256]{1,0:T(8,128)(2,1)S(1)}, bf16[256,256]{1,0:T(8,128)(2,1)}, u32[]{:S(2)}) copy-start(bf16[256,256]{1,0:T(8,128)(2,1)} %constant.7.clone.refs_15_) | copy-start | bytes 393220
  63.8 17.6 %copy-start.21 = (bf16[256,256]{1,0:T(8,128)(2,1)S(1)}, bf16[256,256]{1,0:T(8,128)(2,1)}, u32[]{:S(2)}) copy-start(bf16[256,256]{1,0:T(8,128)(2,1)} %constant.6.clone.refs_14_) | copy-start | bytes 393220
  63.8 17.6 %copy-start.23 = (f32[1,128]{1,0:T(1,128)S(1)}, f32[1,128]{1,0:T(1,128)}, u32[]{:S(2)}) copy-start(f32[1,128]{1,0:T(1,128)} %constant.8.clone.refs_13_) | copy-start | bytes 1540
  69.0 11.5 %collective-permute-start.7 = (f32[24,1,128]{2,1,0:T(1,128)S(1)}, f32[24,1,128]{2,1,0:T(1,128)S(1)}, u32[]{:S(2)}, u32[]{:S(2)}) collective-permute-start(f32[24,1,128]{2,1,0:T(1,128)S(1)} %get-tuple-element.18.refs_1_), channel_id=1, source_target_pairs={{1,0},{2,1},{3,2},{4,3},{5,4},{6,5},{7,6},{8,7},{9,8},{10,9},{11,1... | collective-permute-start | bytes 36872 | tf_op jit(solution)/shard_map/ppermute | solution.py:257
  70.3 10.2 %collective-permute-start.6 = (f32[24,1,128]{2,1,0:T(1,128)S(1)}, f32[24,1,128]{2,1,0:T(1,128)S(1)}, u32[]{:S(2)}, u32[]{:S(2)}) collective-permute-start(f32[24,1,128]{2,1,0:T(1,128)S(1)} %get-tuple-element.18.refs_1_), channel_id=1, source_target_pairs={{0,1},{1,2},{2,3},{3,4},{4,5},{5,6},{6,7},{7,8},{8,9},{9,10},{10,1... | collective-permute-start | bytes 36872 | tf_op jit(solution)/shard_map/ppermute | solution.py:256
  74.3 6.2 %collective-permute-start.5 = (f32[24,1,128]{2,1,0:T(1,128)S(1)}, f32[24,1,128]{2,1,0:T(1,128)S(1)}, u32[]{:S(2)}, u32[]{:S(2)}) collective-permute-start(f32[24,1,128]{2,1,0:T(1,128)S(1)} %get-tuple-element.18.refs_1_), channel_id=1, source_target_pairs={{16,0},{32,16},{48,32},{64,48},{80,64},{96,80},{112,96},{17,1},{33... | collective-permute-start | bytes 36872 | tf_op jit(solution)/shard_map/ppermute | solution.py:257
  78.1 3.2 %collective-permute-start.4 = (f32[24,1,128]{2,1,0:T(1,128)S(1)}, f32[24,1,128]{2,1,0:T(1,128)S(1)}, u32[]{:S(2)}, u32[]{:S(2)}) collective-permute-start(f32[24,1,128]{2,1,0:T(1,128)S(1)} %get-tuple-element.18.refs_1_), channel_id=1, source_target_pairs={{0,16},{16,32},{32,48},{48,64},{64,80},{80,96},{96,112},{1,17},{17... | collective-permute-start | bytes 36872 | tf_op jit(solution)/shard_map/ppermute | solution.py:256
where the time goes:
time: 121 us
  blocking collectives  45.1 us (37%)
  Pallas kernels  36.9 us (30%)
  starting transfers between devices  23.1 us (19%)
  local copies, waits for them, and re-layouts  10.7 us (9%)
  waiting for transfers between devices  4.11 us (3%)
    all_to_all x2, blocking collectives, body(): lax.all_to_all(sending.reshape(OWNERS, ROWS, POINTS), ('grid', 'line'), s...  45.1 us
    pallas_call x4, Pallas kernels, call(): pl.pallas_call(kernel, out_shape=shapes, in_specs=specs, out_specs=[VMEM]...  36.9 us
    ppermute x4, starting transfers between devices, beside(): around.append(lax.ppermute(field, axis, up))  13.8 us
    unnamed x48, local copies, waits for them, and re-layouts  10.7 us
    ppermute x4, starting transfers between devices, beside(): around.append(lax.ppermute(field, axis, [(b, a) for a, b in up]))  9.25 us
    ppermute x4, waiting for transfers between devices, beside(): around.append(lax.ppermute(field, axis, [(b, a) for a, b in up]))  3.33 us
  transfers between devices with their start and end apart: 8, of which 2 were waited for; matrix products, arithmetic and copies ran while one was open for 0% of the time, Pallas kernels for 0%

commit v1 on v0

v1 whole, which is shorter than its diff:
```python
import jax
import jax.numpy as jnp
import numpy as np
from jax import lax
from jax.experimental import pallas as pl
from jax.experimental.pallas import tpu as pltpu
from jax.sharding import PartitionSpec as P

SEG = 16
TRIP = 48
KMAX = 6
STEPS = 2
LES_RATE = 0.2
SPECIES = 24
POINTS = 128
LINES = 128
OWNERS = 128
ROWS = 8
F32 = jnp.float32
BF16 = jnp.bfloat16


def cosine_tables():
    k = np.arange(POINTS)[:, None]
    p = np.arange(POINTS)[None, :]
    basis = np.sqrt(2.0 / POINTS) * np.cos(np.pi * k * (2 * p + 1) / (2 * POINTS))
    basis[0] = 1.0 / np.sqrt(POINTS)
    tables = []
    for table in (basis.T, basis):
        high = table.astype(BF16)
        low = (table - high.astype(np.float64)).astype(BF16)
        half = np.concatenate([high, low], axis=1)
        tables.append(np.concatenate([half, half], axis=0))
    eigen = 4.0 * np.sin(np.pi * np.arange(POINTS) / (2 * POINTS)) ** 2
    return tables[0], tables[1], eigen.astype(np.float32)[None, :]


def halves(value):
    high = value.astype(BF16)
    return high, (value - high.astype(F32)).astype(BF16)


def dot(a, b):
    return jnp.dot(a, b, preferred_element_type=F32)


def iota(axis, shape=(LINES, POINTS)):
    return lax.broadcasted_iota(jnp.int32, shape, axis)


def column(row):
    return jnp.transpose(jnp.broadcast_to(row.astype(F32), (LINES, POINTS)))


def lane_pick(value, index):
    return jnp.take_along_axis(value, index, axis=1, mode="promise_in_bounds")


def mix_tables(rates, frozen, high_ref, low_ref):
    exact = dict(precision=lax.Precision.HIGHEST, preferred_element_type=F32)
    matrix = jnp.dot(frozen, rates, **exact)
    side = SPECIES * 8
    spread = (iota(0, (side, SPECIES)) // 8 == iota(1, (side, SPECIES))).astype(F32)
    gather = (iota(0, (SPECIES, side)) == iota(1, (SPECIES, side)) // 8).astype(F32)
    wide = jnp.dot(jnp.dot(spread, matrix, **exact), gather, **exact)
    same = iota(0, (side, side)) % 8 == iota(1, (side, side)) % 8
    high, low = halves(jnp.where(same, wide, 0.0))
    high_ref[...] = high
    low_ref[...] = low


def middle(les, grid_even, grid_odd, line_even, line_odd):
    row, place = lax.axis_index("grid"), lax.axis_index("line")
    inner = jnp.logical_and(row > 0, row < lax.axis_size("grid") - 1)
    even = place % 2 == 0
    west = jnp.where(even, line_odd, line_even)
    east = jnp.where(even, line_even, line_odd)
    west = jnp.where(place > 0, west, 0.0)
    east = jnp.where(place < lax.axis_size("line") - 1, east, 0.0)
    lane = iota(1, (SPECIES, LINES))
    left = jnp.where(lane == 0, pltpu.roll(west, 1, 1), pltpu.roll(les, 1, 1))
    right = jnp.where(lane == LINES - 1, pltpu.roll(east, LINES - 1, 1), pltpu.roll(les, LINES - 1, 1))
    return les + LES_RATE * (grid_even + jnp.where(inner, grid_odd, 0.0) + left + right - 4.0 * les)


def turned(value):
    pad = jnp.zeros((POINTS - SPECIES, LINES), F32)
    return jnp.transpose(jnp.concatenate([value, pad], axis=0))


def triplet_index(start):
    place = iota(1)
    start = start.astype(jnp.int32)
    rel = place - start
    third = TRIP // 3
    source = jnp.where(
        rel < third,
        3 * rel,
        jnp.where(rel < 2 * third, 3 * (2 * third - 1 - rel) + 1, 3 * (rel - 2 * third) + 2),
    )
    return jnp.where((rel >= 0) & (rel < TRIP), source + start, place)


def mixing(read, start_row, scale_ref, first_ref, second_ref, state_ref, index_ref):
    index_ref[...] = triplet_index(column(start_row))
    group = 8

    def one(at, carry):
        species = [at * group + i for i in range(group)]
        value = jnp.concatenate([lane_pick(read(s), index_ref[...]) for s in species], axis=0)
        wide = dot(jnp.concatenate(halves(value), axis=1), first_ref[...])
        value = wide[:, :POINTS] + wide[:, POINTS:]
        value = value.reshape(group, LINES, POINTS)
        value = jnp.concatenate([value[i] * scale_ref[pl.ds(s, 1), :] for i, s in enumerate(species)], axis=0)
        wide = dot(jnp.concatenate(halves(value), axis=1), second_ref[...])
        value = (wide[:, :POINTS] + wide[:, POINTS:]).reshape(group, LINES, POINTS)
        for i, s in enumerate(species):
            state_ref[s] = value[i]
        return carry

    lax.fori_loop(0, SPECIES // group, one, 0)


def chemistry(counts_row, shift, high_ref, low_ref, mixed_ref, state_ref, counts_ref):
    counts_ref[...] = column(counts_row)
    side = SPECIES * 8

    def substep(turn, read):
        for unit in range(LINES // 16):
            parts = [slice(16 * unit, 16 * unit + 8), slice(16 * unit + 8, 16 * unit + 16)]
            old = [read(part).reshape(side, POINTS) for part in parts]
            high, low = halves(jnp.tanh(jnp.concatenate(old, axis=1)))
            change = dot(high_ref[...], high) + (dot(low_ref[...], high) + dot(high_ref[...], low))
            for at, part in enumerate(parts):
                active = (counts_ref[part, :] > turn)[None]
                before = old[at].reshape(SPECIES, 8, POINTS)
                after = before + change[:, at * POINTS : (at + 1) * POINTS].reshape(SPECIES, 8, POINTS)
                state_ref[:, part, :] = jnp.where(active, after, before)

    def shifted(part):
        rows = [jnp.broadcast_to(shift[part, s : s + 1], (8, POINTS))[None] for s in range(SPECIES)]
        return mixed_ref[:, part, :] + jnp.concatenate(rows, axis=0)

    substep(0.0, shifted)

    def later(sub, carry):
        substep(sub.astype(F32), lambda part: state_ref[:, part, :])
        return carry

    lax.fori_loop(1, KMAX, later, 0)


def packing(owner_row, line_row, from_row, to_row, state_ref, out_ref, send_ref):
    lane = iota(1)
    pick = column(from_row).astype(jnp.int32) * SEG + lane % SEG
    landing = column(to_row)
    group = (lane // SEG - landing.astype(jnp.int32)) & 7
    for third in range(3):
        gathered = jnp.zeros((LINES, POINTS), F32)
        for s in range(8):
            gathered = jnp.where(group == s, lane_pick(state_ref[8 * third + s], pick), gathered)
        high, low = halves(gathered)
        out_ref[:LINES, third * POINTS : (third + 1) * POINTS] = high
        out_ref[LINES:, third * POINTS : (third + 1) * POINTS] = low
    owner = column(owner_row).astype(jnp.int32)
    earlier = (owner == owner_row) & (iota(0) < lane)
    rank = jnp.sum(earlier.astype(F32), axis=0, keepdims=True)
    aims = jnp.where(lane < 64, column(line_row) + 1.0, landing).astype(BF16)
    for slot in range(2):
        placing = ((iota(0) == owner_row) & (rank == slot)).astype(F32).astype(BF16)
        sending = dot(jnp.concatenate([placing, placing], axis=1), out_ref[...])
        for third in range(3):
            send_ref[pl.ds(3 * slot + third, OWNERS, stride=ROWS), :] = sending[
                :, third * POINTS : (third + 1) * POINTS
            ]
        send_ref[pl.ds(6 + slot, OWNERS, stride=ROWS), :] = dot(placing, aims)


def splicing(received_ref, state_ref, write, parts_ref, hits_ref, gain_ref):
    place = iota(0).astype(F32)
    for slot in range(2):
        aim = jnp.transpose(received_ref[pl.ds(6 + slot, OWNERS, stride=ROWS), :])
        code = aim[64:65] * LINES + aim[:1] - 1.0
        rows = slice(slot * OWNERS, (slot + 1) * OWNERS)
        lows = slice((2 + slot) * OWNERS, (3 + slot) * OWNERS)
        for third in range(3):
            high, low = halves(received_ref[pl.ds(3 * slot + third, OWNERS, stride=ROWS), :])
            parts_ref[rows, third * POINTS : (third + 1) * POINTS] = high
            parts_ref[lows, third * POINTS : (third + 1) * POINTS] = low
        parts_ref[rows, 3 * POINTS :] = jnp.ones((OWNERS, POINTS), BF16)
        parts_ref[lows, 3 * POINTS :] = jnp.zeros((OWNERS, POINTS), BF16)
        for segment in range(8):
            hit = jnp.where(place + float(segment * LINES) == code, 0.5, 0.0).astype(BF16)
            hits_ref[segment * LINES : (segment + 1) * LINES, rows] = hit
            hits_ref[segment * LINES : (segment + 1) * LINES, lows] = hit
    gain_ref[...] = dot(hits_ref[...], parts_ref[...]).reshape(8, LINES, 4 * POINTS)
    group = iota(1, (8, POINTS)) // SEG
    bits = [(group & bit) != 0 for bit in (1, 2, 4)]

    def block(at, carry):
        first = pl.multiple_of(8 * at, 8)
        lines = pl.ds(first, 8)
        share = gain_ref[0, lines, 3 * POINTS :]
        for segment in range(1, 8):
            share = jnp.where(group == segment, gain_ref[segment, lines, 3 * POINTS :], share)
        keep = 1.0 - share
        for third in range(3):
            shifted = [gain_ref[segment, lines, third * POINTS : (third + 1) * POINTS] for segment in range(8)]
            for bit, mask in zip((1, 2, 4), bits):
                shifted = [jnp.where(mask, shifted[(i + bit) % 8], shifted[i]) for i in range(8)]
            for s in range(8):
                gained = shifted[-s % 8]
                if s:
                    gained = pltpu.roll(gained, POINTS - SEG * s, 1)
                write(8 * third + s, at, state_ref[8 * third + s, lines, :] * keep + gained)
        return carry

    lax.fori_loop(0, LINES // 8, block, 0, unroll=2)


def means_of(read):
    lane = iota(1)

    def one(s, means):
        return jnp.where(lane == s, jnp.sum(read(s), axis=1, keepdims=True) * (1.0 / POINTS), means)

    return jnp.transpose(lax.fori_loop(0, SPECIES, one, jnp.zeros((LINES, POINTS), F32), unroll=4))[:SPECIES]


def scales(diffusivity_row, eigen_row):
    row = jnp.concatenate([diffusivity_row, jnp.zeros((1, POINTS - SPECIES), F32)], axis=1)
    lane = iota(1, (SPECIES, POINTS))
    return jnp.where(lane == 0, 0.5, 1.0 / (1.0 + column(row)[:SPECIES] * eigen_row))


def first_mix_kernel(
    lines_hbm, start_hbm, diffusivity_hbm, eigen_hbm, first_hbm, second_hbm, rates_hbm, frozen_hbm,
    mixed_ref, high_ref, low_ref, scale_ref,
    lines_ref, start_ref, diffusivity_ref, eigen_ref, first_ref, second_ref, rates_ref, frozen_ref, index_ref, sems,
):
    here = (rates_ref, frozen_ref, diffusivity_ref, eigen_ref, start_ref, first_ref, second_ref, lines_ref)
    there = (rates_hbm, frozen_hbm, diffusivity_hbm, eigen_hbm, start_hbm, first_hbm, second_hbm, lines_hbm)
    copies = [pltpu.make_async_copy(a, b, sems.at[i]) for i, (a, b) in enumerate(zip(there, here))]
    for copy in reversed(copies):
        copy.start()
    for copy in copies[:5]:
        copy.wait()
    mix_tables(rates_ref[...], frozen_ref[...], high_ref, low_ref)
    scale_ref[...] = scales(diffusivity_ref[...], eigen_ref[...])
    for copy in copies[5:]:
        copy.wait()

    def read(s):
        return lines_ref[pl.ds(s, LINES, stride=SPECIES), :]

    mixing(read, start_ref[0, 0], scale_ref, first_ref, second_ref, mixed_ref, index_ref)


def next_mix_kernel(state_ref, start_ref, scale_ref, first_ref, second_ref, mixed_ref, index_ref):
    mixing(lambda s: state_ref[s], start_ref[1, 0], scale_ref, first_ref, second_ref, mixed_ref, index_ref)


def react_kernel(
    step, mixed_ref, les_ref, grid_even_ref, grid_odd_ref, line_even_ref, line_odd_ref, owner_ref, line_ref, from_ref,
    to_ref, counts_ref, high_ref, low_ref, state_ref, send_ref, mid_ref, turns_ref, out_ref,
):
    mid = middle(les_ref[:, 0], grid_even_ref[:, 0], grid_odd_ref[:, 0], line_even_ref[:, 0], line_odd_ref[:, 0])
    mid_ref[...] = mid
    chemistry(counts_ref[0], turned(0.5 * mid), high_ref, low_ref, mixed_ref, state_ref, turns_ref)
    packing(owner_ref[step, 0], line_ref[step, 0], from_ref[step, 0], to_ref[step, 0], state_ref, out_ref, send_ref)


def next_splice_kernel(received_ref, state_ref, mid_ref, les_ref, lines_ref, parts_ref, hits_ref, gain_ref):
    def write(species, at, value):
        lines_ref[species, pl.ds(pl.multiple_of(8 * at, 8), 8), :] = value

    splicing(received_ref, state_ref, write, parts_ref, hits_ref, gain_ref)
    les_ref[:, 0] = 0.5 * mid_ref[...] + 0.5 * means_of(lambda s: lines_ref[s])


def last_splice_kernel(
    received_ref, state_ref, mid_ref, les_ref, lines_hbm, parts_ref, hits_ref, gain_ref, lines_ref, sems
):
    rows = 8 * SPECIES

    def out(at):
        part = pl.ds(pl.multiple_of(at * rows, rows), rows)
        return pltpu.make_async_copy(lines_ref.at[part], lines_hbm.at[part], sems.at[at])

    def write(species, at, value):
        lines_ref[pl.ds(at * rows + species, 8, stride=SPECIES), :] = value
        if species == SPECIES - 1:
            out(at).start()

    splicing(received_ref, state_ref, write, parts_ref, hits_ref, gain_ref)
    means = means_of(lambda s: lines_ref[pl.ds(s, LINES, stride=SPECIES), :])
    les_ref[:, 0] = 0.5 * mid_ref[...] + 0.5 * means
    for at in range(LINES // 8):
        out(at).wait()


VMEM = pl.BlockSpec(memory_space=pltpu.VMEM)
HBM = pl.BlockSpec(memory_space=pltpu.HBM)
STATE = jax.ShapeDtypeStruct((SPECIES, LINES, POINTS), F32)
FLAT = jax.ShapeDtypeStruct((LINES * SPECIES, POINTS), F32)
SPLICE_SCRATCH = [
    pltpu.VMEM((4 * OWNERS, 4 * POINTS), BF16),
    pltpu.VMEM((8 * LINES, 4 * OWNERS), BF16),
    pltpu.VMEM((8, LINES, 4 * POINTS), F32),
]


def call(kernel, inputs, outputs, scratch, micros, in_space=VMEM, out_specs=None):
    size = sum(x.size * x.dtype.itemsize for x in [*inputs, *outputs])
    if in_space is HBM:
        inputs = [pltpu.with_memory_space_constraint(x, pltpu.HBM) for x in inputs]
    return pl.pallas_call(
        kernel,
        out_shape=outputs,
        in_specs=[in_space] * len(inputs),
        out_specs=out_specs or [VMEM] * len(outputs),
        scratch_shapes=scratch,
        cost_estimate=pl.CostEstimate(flops=micros * 10**9, bytes_accessed=size, transcendentals=0),
        compiler_params=pltpu.CompilerParams(vmem_limit_bytes=32 << 20),
    )(*inputs)


def beside(field):
    around = []
    for axis in ("grid", "line"):
        peers = lax.axis_size(axis)
        for start in (0, 1):
            pairs = [(i, (i + 1) % peers) for i in range(start, peers, 2)]
            around.append(lax.ppermute(field, axis, pairs + [(b, a) for a, b in pairs]))
    return around


def body(
    les,
    lines,
    triplet_start,
    splice_owner,
    splice_line,
    splice_from,
    splice_to,
    chem_counts,
    diffusivity,
    rates,
    frozen_inverse,
):
    first_table, second_table, eigen = (jnp.asarray(x) for x in cosine_tables())
    side = SPECIES * 8
    send = jax.ShapeDtypeStruct((OWNERS * ROWS, POINTS), F32)
    plane = jax.ShapeDtypeStruct((SPECIES, LINES), F32)
    table = jax.ShapeDtypeStruct((side, side), BF16)
    owner = splice_owner.reshape(STEPS, 1, 1, LINES)
    field = les
    index = pltpu.VMEM((LINES, POINTS), jnp.int32)
    for step in range(STEPS):
        last = step == STEPS - 1
        rim = beside(field)
        if step == 0:
            inputs = [lines.reshape(FLAT.shape), triplet_start, diffusivity.reshape(1, SPECIES), eigen]
            inputs += [first_table, second_table, rates, frozen_inverse]
            scratch = [pltpu.VMEM(x.shape, x.dtype) for x in inputs] + [index, pltpu.SemaphoreType.DMA((len(inputs),))]
            mixed, high, low, scale = call(
                first_mix_kernel, inputs, [STATE, table, table, plane], scratch, 4, in_space=HBM
            )
        else:
            inputs = [state, triplet_start, scale, first_table, second_table]
            (mixed,) = call(next_mix_kernel, inputs, [STATE], [index], 3)

        def react(*refs, step=step):
            react_kernel(step, *refs)

        inputs = [mixed, field, *rim, owner, splice_line, splice_from, splice_to, chem_counts, high, low]
        scratch = [pltpu.VMEM((LINES, POINTS), F32), pltpu.VMEM((2 * LINES, 3 * POINTS), BF16)]
        state, sending, mid = call(react, inputs, [STATE, send, plane], scratch, 8)
        received = lax.all_to_all(
            sending.reshape(OWNERS, ROWS, POINTS), ("grid", "line"), split_axis=0, concat_axis=0, tiled=True
        ).reshape(OWNERS * ROWS, POINTS)
        inputs = [received, state, mid]
        outputs = [jax.ShapeDtypeStruct(les.shape, F32), FLAT if last else STATE]
        if last:
            scratch = SPLICE_SCRATCH + [pltpu.VMEM(FLAT.shape, F32), pltpu.SemaphoreType.DMA((LINES // 8,))]
            field, state = call(last_splice_kernel, inputs, outputs, scratch, 3, out_specs=[VMEM, HBM])
        else:
            field, state = call(next_splice_kernel, inputs, outputs, SPLICE_SCRATCH, 3)
    return (field, state.reshape(lines.shape))


def solution(mesh):
    in_specs = (
        P(None, "grid", "line"),
        P("grid", "line", None, None, None),
        P(None, "grid", "line", None),
        P(None, "grid", "line", None, None),
        P(None, "grid", "line", None),
        P(None, "grid", "line", None),
        P(None, "grid", "line", None),
        P("grid", "line", None),
        P(),
        P(),
        P(),
    )
    out_specs = (P(None, "grid", "line"), P("grid", "line", None, None, None))
    return jax.shard_map(body, mesh=mesh, in_specs=in_specs, out_specs=out_specs, check_vma=False)
```

time: 121 us -> 82.3 us (0.68)
  local copies, waits for them, and re-layouts: 10.7 us -> 0.03 us
  Pallas kernels: 36.9 us -> 26.8 us
  starting transfers between devices: 23.1 us -> 13.7 us
  blocking collectives: 45.1 us -> 40.2 us
  waiting for transfers between devices: 4.11 us -> 0.53 us
    unnamed x48 -> x18, local copies, waits for them, and re-layouts: 10.7 us -> 0.03 us
    pallas_call x4 -> x6, Pallas kernels: 36.9 us -> 26.8 us  [call(): pl.pallas_call(kernel, out_shape=outputs, in_specs=[in_space] * len(input...]
    ppermute x8, starting transfers between devices: 23.1 us -> 13.7 us  [beside(): around.append(lax.ppermute(field, axis, pairs + [(b, a) for a, b in pairs]))]
    all_to_all x2, blocking collectives: 45.1 us -> 40.2 us  [body(): lax.all_to_all(sending.reshape(OWNERS, ROWS, POINTS), ('grid', 'line'), s...]
    ppermute x8, waiting for transfers between devices: 4.11 us -> 0.53 us  [beside(): around.append(lax.ppermute(field, axis, pairs + [(b, a) for a, b in pairs]))]
  transfers between devices with their start and end apart: 8 -> 8, of which waited for: 2 -> 1; matrix products, arithmetic and copies ran while one was open for 0% -> 0% of each run, Pallas kernels for 0% -> 8%
where the time goes in v1:
time: 82.3 us; the launch traced here: 82.1 us
  blocking collectives  40.2 us (49%)
  Pallas kernels  26.8 us (33%)
  starting transfers between devices  13.7 us (17%)
    all_to_all x2, blocking collectives, body(): lax.all_to_all(sending.reshape(OWNERS, ROWS, POINTS), ('grid', 'line'), s...  40.2 us
    pallas_call x6, Pallas kernels, call(): pl.pallas_call(kernel, out_shape=outputs, in_specs=[in_space] * len(input...  26.8 us
    ppermute x8, starting transfers between devices, beside(): around.append(lax.ppermute(field, axis, pairs + [(b, a) for a, b in pairs]))  13.7 us
  transfers between devices with their start and end apart: 8, of which 1 were waited for; matrix products, arithmetic and copies ran while one was open for 0% of the time, Pallas kernels for 8%

profile of v1, /device:TPU:1, one launch (start us, length us, event | category | flops | bytes accessed | tf_op | source)
XLA Modules:
  0.0 82.1 jit_solution(11527173357605980987)
XLA Ops:
  0.6 2.2 %collective-permute-start.2 = (f32[24,1,128]{2,1,0:T(1,128)}, f32[24,1,128]{2,1,0:T(1,128)S(1)}, u32[]{:S(2)}, u32[]{:S(2)}) collective-permute-start(f32[24,1,128]{2,1,0:T(1,128)} %refs_1_.1), channel_id=1, source_target_pairs={{0,1},{2,3},{4,5},{6,7},{8,9},{10,11},{12,13},{14,15},{1,0},{3,2},... | collective-permute-start | bytes 36872 | tf_op jit(solution)/shard_map/ppermute | solution.py:334
  2.8 2.5 %collective-permute-start.1 = (f32[24,1,128]{2,1,0:T(1,128)}, f32[24,1,128]{2,1,0:T(1,128)S(1)}, u32[]{:S(2)}, u32[]{:S(2)}) collective-permute-start(f32[24,1,128]{2,1,0:T(1,128)} %refs_1_.1), channel_id=1, source_target_pairs={{16,32},{48,64},{80,96},{112,0},{32,16},{64,48},{96,80},{0,112},{1... | collective-permute-start | bytes 36872 | tf_op jit(solution)/shard_map/ppermute | solution.py:334
  5.3 1.7 %collective-permute-start = (f32[24,1,128]{2,1,0:T(1,128)}, f32[24,1,128]{2,1,0:T(1,128)S(1)}, u32[]{:S(2)}, u32[]{:S(2)}) collective-permute-start(f32[24,1,128]{2,1,0:T(1,128)} %refs_1_.1), channel_id=1, source_target_pairs={{0,16},{32,48},{64,80},{96,112},{16,0},{48,32},{80,64},{112,96},{1... | collective-permute-start | bytes 36872 | tf_op jit(solution)/shard_map/ppermute | solution.py:334
  7.0 4.1 %collective-permute-start.3 = (f32[24,1,128]{2,1,0:T(1,128)}, f32[24,1,128]{2,1,0:T(1,128)S(1)}, u32[]{:S(2)}, u32[]{:S(2)}) collective-permute-start(f32[24,1,128]{2,1,0:T(1,128)} %refs_1_.1), channel_id=1, source_target_pairs={{1,2},{3,4},{5,6},{7,8},{9,10},{11,12},{13,14},{15,0},{2,1},{4,3},... | collective-permute-start | bytes 36872 | tf_op jit(solution)/shard_map/ppermute | solution.py:334
  11.1 0.0 copy-start.5
  11.1 0.0 copy-start.6
  11.1 4.3 %shard_map.149 = (f32[24,128,128]{2,1,0:T(8,128)S(1)}, bf16[192,192]{1,0:T(8,128)(2,1)S(1)}, bf16[192,192]{1,0:T(8,128)(2,1)S(1)}, f32[24,128]{1,0:T(8,128)S(1)}) custom-call(f32[3072,128]{1,0:T(8,128)} %bitcast.14, s32[2,1,1,128]{3,2,1,0:T(1,128)} %start_ref.1, f32[1,24]{1,0:T(1,128)} %bitcast.15, f32[1,128]{1,0:T(1,128)} %constant.8.clone.eigen_hbm, ...), custom_call_target="tpu_custom_call" | custom-call | flops 4000000000 | bytes 3573856 | tf_op jit(solution)/shard_map/pallas_call | solution.py:317
  15.5 0.0 collective-permute-done.2.refs_4_
  15.5 0.0 collective-permute-done.1.refs_3_
  15.5 0.0 collective-permute-done.refs_2_
  15.5 0.0 collective-permute-done.3.refs_5_
  15.5 0.0 copy-done
  15.5 0.0 copy-done.2
  15.5 0.0 copy-done.3
  15.5 0.0 copy-done.4
  15.6 0.0 copy-done.5
  15.6 7.0 %shard_map.150 = (f32[24,128,128]{2,1,0:T(8,128)S(1)}, f32[1024,128]{1,0:T(8,128)S(1)}, f32[24,128]{1,0:T(8,128)S(1)}) custom-call(f32[24,128,128]{2,1,0:T(8,128)S(1)} %get-tuple-element.16.refs_0_, f32[24,1,128]{2,1,0:T(1,128)S(1)} %copy-done, f32[24,1,128]{2,1,0:T(1,128)S(1)} %collective-permute-done.refs_2_, ...), custom_call_target="tpu_custom_call" | custom-call | flops 8000000000 | bytes 3895808 | tf_op jit(solution)/shard_map/pallas_call | solution.py:317
  22.6 18.9 %all_to_all.10 = f32[128,8,128]{2,1,0:T(8,128)S(1)} all-to-all(f32[128,8,128]{2,1,0:T(8,128)S(1)} %bitcast.9), channel_id=1, replica_groups=mesh['grid'=8,'line'=16] {'grid','line'}, dimensions={0} | all-to-all | bytes 1048576 | tf_op jit(solution)/shard_map/all_to_all | solution.py:379
  41.5 2.7 %shard_map.151 = (f32[24,1,128]{2,1,0:T(1,128)S(1)}, f32[24,128,128]{2,1,0:T(8,128)S(1)}) custom-call(f32[1024,128]{1,0:T(8,128)S(1)} %bitcast.10, f32[24,128,128]{2,1,0:T(8,128)S(1)} %get-tuple-element.20.state_ref, f32[24,128]{1,0:T(8,128)S(1)} %get-tuple-element.21.mid_ref), custom_call_target="tpu_custom_call" | custom-call | flops 3000000000 | bytes 3694592 | tf_op jit(solution)/shard_map/pallas_call | solution.py:317
  44.3 1.8 %collective-permute-start.7 = (f32[24,1,128]{2,1,0:T(1,128)S(1)}, f32[24,1,128]{2,1,0:T(1,128)S(1)}, u32[]{:S(2)}, u32[]{:S(2)}) collective-permute-start(f32[24,1,128]{2,1,0:T(1,128)S(1)} %get-tuple-element.24.refs_1_), channel_id=1, source_target_pairs={{1,2},{3,4},{5,6},{7,8},{9,10},{11,12},{13,14},{15,0},{2,1},{4,3},... | collective-permute-start | bytes 36872 | tf_op jit(solution)/shard_map/ppermute | solution.py:334
  46.1 0.0 collective-permute-start.6
  46.1 0.8 collective-permute-start.5
  46.9 0.6 collective-permute-start.4
  47.5 0.0 copy-done.1
  47.5 2.1 %shard_map.152.refs_0_ = f32[24,128,128]{2,1,0:T(8,128)S(1)} custom-call(f32[24,128,128]{2,1,0:T(8,128)S(1)} %get-tuple-element.22.state_ref, s32[2,1,1,128]{3,2,1,0:T(1,128)S(1)} %copy-done.1, f32[24,128]{1,0:T(8,128)S(1)} %get-tuple-element.23.scale_ref, bf16[256,256]{1,0:T(8,128)(2,1)S(1)} %copy-done.8, bf16[256,256]{1,0:T(8,128)(2,1)S(1)} %copy-done.7), custom_call_target="tpu_custom_call" | custom-call | flops 3000000000 | bytes 3421184 | tf_op jit(solution)/shard_map/pallas_call | solution.py:317
  49.7 0.5 collective-permute-done.7.refs_5_
  50.2 0.0 collective-permute-done.6.refs_4_
  50.2 0.0 collective-permute-done.5.refs_3_
  50.2 0.0 collective-permute-done.4.refs_2_
  50.2 7.0 %shard_map.153 = (f32[24,128,128]{2,1,0:T(8,128)S(1)}, f32[1024,128]{1,0:T(8,128)S(1)}, f32[24,128]{1,0:T(8,128)S(1)}) custom-call(f32[24,128,128]{2,1,0:T(8,128)S(1)} %shard_map.152.refs_0_, f32[24,1,128]{2,1,0:T(1,128)S(1)} %get-tuple-element.24.refs_1_, f32[24,1,128]{2,1,0:T(1,128)S(1)} %collective-permute-done.4.refs_2_, ...), custom_call_target="tpu_custom_call" | custom-call | flops 8000000000 | bytes 3895808 | tf_op jit(solution)/shard_map/pallas_call | solution.py:317
  57.3 21.3 %all_to_all.11 = f32[128,8,128]{2,1,0:T(8,128)S(1)} all-to-all(f32[128,8,128]{2,1,0:T(8,128)S(1)} %bitcast.8), channel_id=1, replica_groups=mesh['grid'=8,'line'=16] {'grid','line'}, dimensions={0} | all-to-all | bytes 1048576 | tf_op jit(solution)/shard_map/all_to_all | solution.py:379
  78.5 3.5 %shard_map.154 = (f32[24,1,128]{2,1,0:T(1,128)}, f32[3072,128]{1,0:T(8,128)}) custom-call(f32[1024,128]{1,0:T(8,128)S(1)} %bitcast.11, f32[24,128,128]{2,1,0:T(8,128)S(1)} %get-tuple-element.26.state_ref, f32[24,128]{1,0:T(8,128)S(1)} %get-tuple-element.27.mid_ref), custom_call_target="tpu_custom_call" | custom-call | flops 3000000000 | bytes 3694592 | tf_op jit(solution)/shard_map/pallas_call | solution.py:317
  (10 shorter events, 0.0 us)
Async XLA Ops:
  0.6 14.8 %collective-permute-start.2 = (f32[24,1,128]{2,1,0:T(1,128)}, f32[24,1,128]{2,1,0:T(1,128)S(1)}, u32[]{:S(2)}, u32[]{:S(2)}) collective-permute-start(f32[24,1,128]{2,1,0:T(1,128)} %refs_1_.1), channel_id=1, source_target_pairs={{0,1},{2,3},{4,5},{6,7},{8,9},{10,11},{12,13},{14,15},{1,0},{3,2},... | collective-permute-start | bytes 36872 | tf_op jit(solution)/shard_map/ppermute | solution.py:334
  2.8 12.6 %collective-permute-start.1 = (f32[24,1,128]{2,1,0:T(1,128)}, f32[24,1,128]{2,1,0:T(1,128)S(1)}, u32[]{:S(2)}, u32[]{:S(2)}) collective-permute-start(f32[24,1,128]{2,1,0:T(1,128)} %refs_1_.1), channel_id=1, source_target_pairs={{16,32},{48,64},{80,96},{112,0},{32,16},{64,48},{96,80},{0,112},{1... | collective-permute-start | bytes 36872 | tf_op jit(solution)/shard_map/ppermute | solution.py:334
  5.3 10.2 %collective-permute-start = (f32[24,1,128]{2,1,0:T(1,128)}, f32[24,1,128]{2,1,0:T(1,128)S(1)}, u32[]{:S(2)}, u32[]{:S(2)}) collective-permute-start(f32[24,1,128]{2,1,0:T(1,128)} %refs_1_.1), channel_id=1, source_target_pairs={{0,16},{32,48},{64,80},{96,112},{16,0},{48,32},{80,64},{112,96},{1... | collective-permute-start | bytes 36872 | tf_op jit(solution)/shard_map/ppermute | solution.py:334
  7.0 8.5 %collective-permute-start.3 = (f32[24,1,128]{2,1,0:T(1,128)}, f32[24,1,128]{2,1,0:T(1,128)S(1)}, u32[]{:S(2)}, u32[]{:S(2)}) collective-permute-start(f32[24,1,128]{2,1,0:T(1,128)} %refs_1_.1), channel_id=1, source_target_pairs={{1,2},{3,4},{5,6},{7,8},{9,10},{11,12},{13,14},{15,0},{2,1},{4,3},... | collective-permute-start | bytes 36872 | tf_op jit(solution)/shard_map/ppermute | solution.py:334
  11.1 4.4 %copy-start = (f32[24,1,128]{2,1,0:T(1,128)S(1)}, f32[24,1,128]{2,1,0:T(1,128)}, u32[]{:S(2)}) copy-start(f32[24,1,128]{2,1,0:T(1,128)} %refs_1_.1) | copy-start | bytes 36868
  11.1 4.4 %copy-start.2 = (s32[2,1,1,128,1]{3,4,2,1,0:T(1,128)S(1)}, s32[2,1,1,128,1]{3,4,2,1,0:T(1,128)}, u32[]{:S(2)}) copy-start(s32[2,1,1,128,1]{3,4,2,1,0:T(1,128)} %param.17) | copy-start | bytes 3076
  11.1 4.4 %copy-start.3 = (s32[2,1,1,128]{3,2,1,0:T(1,128)S(1)}, s32[2,1,1,128]{3,2,1,0:T(1,128)}, u32[]{:S(2)}) copy-start(s32[2,1,1,128]{3,2,1,0:T(1,128)} %refs_7_.3) | copy-start | bytes 3076
  11.1 4.4 %copy-start.4 = (s32[2,1,1,128]{3,2,1,0:T(1,128)S(1)}, s32[2,1,1,128]{3,2,1,0:T(1,128)}, u32[]{:S(2)}) copy-start(s32[2,1,1,128]{3,2,1,0:T(1,128)} %refs_8_.3) | copy-start | bytes 3076
  11.1 4.5 %copy-start.5 = (s32[2,1,1,128]{3,2,1,0:T(1,128)S(1)}, s32[2,1,1,128]{3,2,1,0:T(1,128)}, u32[]{:S(2)}) copy-start(s32[2,1,1,128]{3,2,1,0:T(1,128)} %refs_9_.3) | copy-start | bytes 3076
  11.1 4.5 %copy-start.6 = (s32[1,1,128]{2,1,0:T(1,128)S(1)}, s32[1,1,128]{2,1,0:T(1,128)}, u32[]{:S(2)}) copy-start(s32[1,1,128]{2,1,0:T(1,128)} %refs_10_.3) | copy-start | bytes 1540
  41.5 6.0 %copy-start.1 = (s32[2,1,1,128]{3,2,1,0:T(1,128)S(1)}, s32[2,1,1,128]{3,2,1,0:T(1,128)}, u32[]{:S(2)}) copy-start(s32[2,1,1,128]{3,2,1,0:T(1,128)} %start_ref.1) | copy-start | bytes 3076
  41.5 6.0 %copy-start.7 = (bf16[256,256]{1,0:T(8,128)(2,1)S(1)}, bf16[256,256]{1,0:T(8,128)(2,1)}, u32[]{:S(2)}) copy-start(bf16[256,256]{1,0:T(8,128)(2,1)} %constant.7.clone.second_hbm.second_ref) | copy-start | bytes 393220
  41.5 6.0 %copy-start.8 = (bf16[256,256]{1,0:T(8,128)(2,1)S(1)}, bf16[256,256]{1,0:T(8,128)(2,1)}, u32[]{:S(2)}) copy-start(bf16[256,256]{1,0:T(8,128)(2,1)} %constant.6.clone.first_hbm.first_ref) | copy-start | bytes 393220
  44.3 5.9 %collective-permute-start.7 = (f32[24,1,128]{2,1,0:T(1,128)S(1)}, f32[24,1,128]{2,1,0:T(1,128)S(1)}, u32[]{:S(2)}, u32[]{:S(2)}) collective-permute-start(f32[24,1,128]{2,1,0:T(1,128)S(1)} %get-tuple-element.24.refs_1_), channel_id=1, source_target_pairs={{1,2},{3,4},{5,6},{7,8},{9,10},{11,12},{13,14},{15,0},{2,1},{4,3},... | collective-permute-start | bytes 36872 | tf_op jit(solution)/shard_map/ppermute | solution.py:334
  46.1 4.1 %collective-permute-start.6 = (f32[24,1,128]{2,1,0:T(1,128)S(1)}, f32[24,1,128]{2,1,0:T(1,128)S(1)}, u32[]{:S(2)}, u32[]{:S(2)}) collective-permute-start(f32[24,1,128]{2,1,0:T(1,128)S(1)} %get-tuple-element.24.refs_1_), channel_id=1, source_target_pairs={{0,1},{2,3},{4,5},{6,7},{8,9},{10,11},{12,13},{14,15},{1,0},{3,2},... | collective-permute-start | bytes 36872 | tf_op jit(solution)/shard_map/ppermute | solution.py:334
  46.1 4.1 %collective-permute-start.5 = (f32[24,1,128]{2,1,0:T(1,128)S(1)}, f32[24,1,128]{2,1,0:T(1,128)S(1)}, u32[]{:S(2)}, u32[]{:S(2)}) collective-permute-start(f32[24,1,128]{2,1,0:T(1,128)S(1)} %get-tuple-element.24.refs_1_), channel_id=1, source_target_pairs={{16,32},{48,64},{80,96},{112,0},{32,16},{64,48},{96,80},{0,112},{1... | collective-permute-start | bytes 36872 | tf_op jit(solution)/shard_map/ppermute | solution.py:334
  46.9 3.3 %collective-permute-start.4 = (f32[24,1,128]{2,1,0:T(1,128)S(1)}, f32[24,1,128]{2,1,0:T(1,128)S(1)}, u32[]{:S(2)}, u32[]{:S(2)}) collective-permute-start(f32[24,1,128]{2,1,0:T(1,128)S(1)} %get-tuple-element.24.refs_1_), channel_id=1, source_target_pairs={{0,16},{32,48},{64,80},{96,112},{16,0},{48,32},{80,64},{112,96},{1... | collective-permute-start | bytes 36872 | tf_op jit(solution)/shard_map/ppermute | solution.py:334

commit v2 on v1

--- a/solution.py
+++ b/solution.py
@@ -101,79 +101,89 @@
     return jnp.where((rel >= 0) & (rel < TRIP), source + start, place)
 
 
-def mixing(read, start_row, scale_ref, first_ref, second_ref, state_ref, index_ref):
+def mixing(read, start_row, scale_ref, first_ref, second_ref, state_ref, index_ref, ready=None):
     index_ref[...] = triplet_index(column(start_row))
     group = 8
 
-    def one(at, carry):
+    for at in range(SPECIES // group):
         species = [at * group + i for i in range(group)]
+        if ready is not None:
+            ready(at)
         value = jnp.concatenate([lane_pick(read(s), index_ref[...]) for s in species], axis=0)
         wide = dot(jnp.concatenate(halves(value), axis=1), first_ref[...])
         value = wide[:, :POINTS] + wide[:, POINTS:]
         value = value.reshape(group, LINES, POINTS)
-        value = jnp.concatenate([value[i] * scale_ref[pl.ds(s, 1), :] for i, s in enumerate(species)], axis=0)
+        value = jnp.concatenate([value[i] * scale_ref[s : s + 1, :] for i, s in enumerate(species)], axis=0)
         wide = dot(jnp.concatenate(halves(value), axis=1), second_ref[...])
         value = (wide[:, :POINTS] + wide[:, POINTS:]).reshape(group, LINES, POINTS)
         for i, s in enumerate(species):
             state_ref[s] = value[i]
-        return carry
-
-    lax.fori_loop(0, SPECIES // group, one, 0)
-
-
-def chemistry(counts_row, shift, high_ref, low_ref, mixed_ref, state_ref, counts_ref):
+
+
+def chemistry(counts_row, shift, high_ref, low_ref, mixed_ref, state_ref, counts_ref, finish):
     counts_ref[...] = column(counts_row)
     side = SPECIES * 8
-
-    def substep(turn, read):
-        for unit in range(LINES // 16):
-            parts = [slice(16 * unit, 16 * unit + 8), slice(16 * unit + 8, 16 * unit + 16)]
-            old = [read(part).reshape(side, POINTS) for part in parts]
-            high, low = halves(jnp.tanh(jnp.concatenate(old, axis=1)))
-            change = dot(high_ref[...], high) + (dot(low_ref[...], high) + dot(high_ref[...], low))
-            for at, part in enumerate(parts):
-                active = (counts_ref[part, :] > turn)[None]
-                before = old[at].reshape(SPECIES, 8, POINTS)
-                after = before + change[:, at * POINTS : (at + 1) * POINTS].reshape(SPECIES, 8, POINTS)
-                state_ref[:, part, :] = jnp.where(active, after, before)
 
     def shifted(part):
         rows = [jnp.broadcast_to(shift[part, s : s + 1], (8, POINTS))[None] for s in range(SPECIES)]
         return mixed_ref[:, part, :] + jnp.concatenate(rows, axis=0)
 
-    substep(0.0, shifted)
-
-    def later(sub, carry):
-        substep(sub.astype(F32), lambda part: state_ref[:, part, :])
-        return carry
-
-    lax.fori_loop(1, KMAX, later, 0)
-
-
-def packing(owner_row, line_row, from_row, to_row, state_ref, out_ref, send_ref):
+    for turn in range(KMAX):
+        for unit in range(LINES // 16):
+            parts = [slice(16 * unit, 16 * unit + 8), slice(16 * unit + 8, 16 * unit + 16)]
+            old = [(state_ref[:, part, :] if turn else shifted(part)).reshape(side, POINTS) for part in parts]
+            high, low = halves(jnp.tanh(jnp.concatenate(old, axis=1)))
+            change = dot(high_ref[...], high) + (dot(low_ref[...], high) + dot(high_ref[...], low))
+            done = []
+            for at, part in enumerate(parts):
+                active = (counts_ref[part, :] > float(turn))[None]
+                before = old[at].reshape(SPECIES, 8, POINTS)
+                after = before + change[:, at * POINTS : (at + 1) * POINTS].reshape(SPECIES, 8, POINTS)
+                done.append(jnp.where(active, after, before))
+                state_ref[:, part, :] = done[at]
+            if turn == KMAX - 1:
+                finish(unit, done)
+
+
+def pack_tables(owner_row, line_row, from_row, to_row, pick_ref, group_ref, placing_ref, aims_ref):
     lane = iota(1)
-    pick = column(from_row).astype(jnp.int32) * SEG + lane % SEG
+    pick_ref[...] = column(from_row).astype(jnp.int32) * SEG + lane % SEG
     landing = column(to_row)
-    group = (lane // SEG - landing.astype(jnp.int32)) & 7
-    for third in range(3):
-        gathered = jnp.zeros((LINES, POINTS), F32)
-        for s in range(8):
-            gathered = jnp.where(group == s, lane_pick(state_ref[8 * third + s], pick), gathered)
-        high, low = halves(gathered)
-        out_ref[:LINES, third * POINTS : (third + 1) * POINTS] = high
-        out_ref[LINES:, third * POINTS : (third + 1) * POINTS] = low
+    group_ref[...] = (lane // SEG - landing.astype(jnp.int32)) & 7
     owner = column(owner_row).astype(jnp.int32)
     earlier = (owner == owner_row) & (iota(0) < lane)
     rank = jnp.sum(earlier.astype(F32), axis=0, keepdims=True)
-    aims = jnp.where(lane < 64, column(line_row) + 1.0, landing).astype(BF16)
+    aims_ref[...] = jnp.where(lane < 64, column(line_row) + 1.0, landing).astype(BF16)
     for slot in range(2):
         placing = ((iota(0) == owner_row) & (rank == slot)).astype(F32).astype(BF16)
-        sending = dot(jnp.concatenate([placing, placing], axis=1), out_ref[...])
+        placing_ref[slot, :, :LINES] = placing
+        placing_ref[slot, :, LINES:] = placing
+
+
+def pack_segments(unit, values, pick_ref, group_ref, out_ref):
+    parts = [slice(16 * unit, 16 * unit + 8), slice(16 * unit + 8, 16 * unit + 16)]
+    for third in range(3):
+        halves_of = []
+        for part, value in zip(parts, values):
+            pick, group = pick_ref[part, :], group_ref[part, :]
+            gathered = lane_pick(value[8 * third], pick)
+            for s in range(1, 8):
+                gathered = jnp.where(group == s, lane_pick(value[8 * third + s], pick), gathered)
+            halves_of.append(gathered)
+        high, low = halves(jnp.concatenate(halves_of, axis=0))
+        columns = slice(third * POINTS, (third + 1) * POINTS)
+        out_ref[16 * unit : 16 * unit + 16, columns] = high
+        out_ref[LINES + 16 * unit : LINES + 16 * unit + 16, columns] = low
+
+
+def sending_rows(placing_ref, aims_ref, out_ref, send_ref):
+    for slot in range(2):
+        sending = dot(placing_ref[slot], out_ref[...])
         for third in range(3):
             send_ref[pl.ds(3 * slot + third, OWNERS, stride=ROWS), :] = sending[
                 :, third * POINTS : (third + 1) * POINTS
             ]
-        send_ref[pl.ds(6 + slot, OWNERS, stride=ROWS), :] = dot(placing, aims)
+        send_ref[pl.ds(6 + slot, OWNERS, stride=ROWS), :] = dot(placing_ref[slot, :, :LINES], aims_ref[...])
 
 
 def splicing(received_ref, state_ref, write, parts_ref, hits_ref, gain_ref):
@@ -219,12 +229,13 @@
 
 
 def means_of(read):
-    lane = iota(1)
-
-    def one(s, means):
-        return jnp.where(lane == s, jnp.sum(read(s), axis=1, keepdims=True) * (1.0 / POINTS), means)
-
-    return jnp.transpose(lax.fori_loop(0, SPECIES, one, jnp.zeros((LINES, POINTS), F32), unroll=4))[:SPECIES]
+    ones = jnp.full((8, 2 * POINTS), 1.0 / POINTS, BF16)
+    rows = []
+    for s in range(SPECIES):
+        both = jnp.concatenate(halves(read(s)), axis=1)
+        sums = lax.dot_general(ones, both, (((1,), (1,)), ((), ())), preferred_element_type=F32)
+        rows.append(sums[:1])
+    return jnp.concatenate(rows, axis=0)
 
 
 def scales(diffusivity_row, eigen_row):
@@ -238,22 +249,25 @@
     mixed_ref, high_ref, low_ref, scale_ref,
     lines_ref, start_ref, diffusivity_ref, eigen_ref, first_ref, second_ref, rates_ref, frozen_ref, index_ref, sems,
 ):
-    here = (rates_ref, frozen_ref, diffusivity_ref, eigen_ref, start_ref, first_ref, second_ref, lines_ref)
-    there = (rates_hbm, frozen_hbm, diffusivity_hbm, eigen_hbm, start_hbm, first_hbm, second_hbm, lines_hbm)
+    here = [lines_ref.at[third].reshape(LINES, 8, POINTS) for third in range(3)]
+    there = [lines_hbm.at[:, pl.ds(8 * third, 8), :] for third in range(3)]
+    here = [rates_ref, frozen_ref, diffusivity_ref, eigen_ref, start_ref, first_ref, second_ref] + here
+    there = [rates_hbm, frozen_hbm, diffusivity_hbm, eigen_hbm, start_hbm, first_hbm, second_hbm] + there
     copies = [pltpu.make_async_copy(a, b, sems.at[i]) for i, (a, b) in enumerate(zip(there, here))]
-    for copy in reversed(copies):
+    for copy in copies:
         copy.start()
-    for copy in copies[:5]:
+    for copy in copies[:7]:
         copy.wait()
     mix_tables(rates_ref[...], frozen_ref[...], high_ref, low_ref)
     scale_ref[...] = scales(diffusivity_ref[...], eigen_ref[...])
-    for copy in copies[5:]:
-        copy.wait()
+
+    def ready(third):
+        copies[7 + third].wait()
 
     def read(s):
-        return lines_ref[pl.ds(s, LINES, stride=SPECIES), :]
-
-    mixing(read, start_ref[0, 0], scale_ref, first_ref, second_ref, mixed_ref, index_ref)
+        return lines_ref[s // 8, pl.ds(s % 8, LINES, stride=8), :]
+
+    mixing(read, start_ref[0, 0], scale_ref, first_ref, second_ref, mixed_ref, index_ref, ready)
 
 
 def next_mix_kernel(state_ref, start_ref, scale_ref, first_ref, second_ref, mixed_ref, index_ref):
@@ -262,12 +276,19 @@
 
 def react_kernel(
     step, mixed_ref, les_ref, grid_even_ref, grid_odd_ref, line_even_ref, line_odd_ref, owner_ref, line_ref, from_ref,
-    to_ref, counts_ref, high_ref, low_ref, state_ref, send_ref, mid_ref, turns_ref, out_ref,
+    to_ref, counts_ref, high_ref, low_ref, state_ref, send_ref, mid_ref, turns_ref, out_ref, pick_ref, group_ref,
+    placing_ref, aims_ref,
 ):
     mid = middle(les_ref[:, 0], grid_even_ref[:, 0], grid_odd_ref[:, 0], line_even_ref[:, 0], line_odd_ref[:, 0])
     mid_ref[...] = mid
-    chemistry(counts_ref[0], turned(0.5 * mid), high_ref, low_ref, mixed_ref, state_ref, turns_ref)
-    packing(owner_ref[step, 0], line_ref[step, 0], from_ref[step, 0], to_ref[step, 0], state_ref, out_ref, send_ref)
+    rows = (ref[step, 0] for ref in (owner_ref, line_ref, from_ref, to_ref))
+    pack_tables(*rows, pick_ref, group_ref, placing_ref, aims_ref)
+
+    def finish(unit, values):
+        pack_segments(unit, values, pick_ref, group_ref, out_ref)
+
+    chemistry(counts_ref[0], turned(0.5 * mid), high_ref, low_ref, mixed_ref, state_ref, turns_ref, finish)
+    sending_rows(placing_ref, aims_ref, out_ref, send_ref)
 
 
 def next_splice_kernel(received_ref, state_ref, mid_ref, les_ref, lines_ref, parts_ref, hits_ref, gain_ref):
@@ -360,9 +381,10 @@
         last = step == STEPS - 1
         rim = beside(field)
         if step == 0:
-            inputs = [lines.reshape(FLAT.shape), triplet_start, diffusivity.reshape(1, SPECIES), eigen]
+            inputs = [lines.reshape(LINES, SPECIES, POINTS), triplet_start, diffusivity.reshape(1, SPECIES), eigen]
             inputs += [first_table, second_table, rates, frozen_inverse]
-            scratch = [pltpu.VMEM(x.shape, x.dtype) for x in inputs] + [index, pltpu.SemaphoreType.DMA((len(inputs),))]
+            scratch = [pltpu.VMEM((3, LINES * 8, POINTS), F32)] + [pltpu.VMEM(x.shape, x.dtype) for x in inputs[1:]]
+            scratch += [index, pltpu.SemaphoreType.DMA((len(inputs) + 2,))]
             mixed, high, low, scale = call(
                 first_mix_kernel, inputs, [STATE, table, table, plane], scratch, 4, in_space=HBM
             )
@@ -374,7 +396,14 @@
             react_kernel(step, *refs)
 
         inputs = [mixed, field, *rim, owner, splice_line, splice_from, splice_to, chem_counts, high, low]
-        scratch = [pltpu.VMEM((LINES, POINTS), F32), pltpu.VMEM((2 * LINES, 3 * POINTS), BF16)]
+        scratch = [
+            pltpu.VMEM((LINES, POINTS), F32),
+            pltpu.VMEM((2 * LINES, 3 * POINTS), BF16),
+            index,
+            index,
+            pltpu.VMEM((2, OWNERS, 2 * LINES), BF16),
+            pltpu.VMEM((LINES, POINTS), BF16),
+        ]
         state, sending, mid = call(react, inputs, [STATE, send, plane], scratch, 8)
         received = lax.all_to_all(
             sending.reshape(OWNERS, ROWS, POINTS), ("grid", "line"), split_axis=0, concat_axis=0, tiled=True

time: 82.3 us -> 78.1 us (0.949)
  Pallas kernels: 26.8 us -> 22.2 us
    pallas_call x6, Pallas kernels: 26.8 us -> 22.2 us  [call(): pl.pallas_call(kernel, out_shape=outputs, in_specs=[in_space] * len(input...]
  transfers between devices with their start and end apart: 8 -> 8, of which waited for: 1 -> 1; matrix products, arithmetic and copies ran while one was open for 0% -> 0% of each run, Pallas kernels for 8% -> 7%
where the time goes in v2:
time: 78.1 us; the launch traced here: 77.9 us
  blocking collectives  39.9 us (51%)
  Pallas kernels  22.2 us (28%)
  starting transfers between devices  13.7 us (18%)
  waiting for transfers between devices  1.18 us (2%)
  between operations  0.94 us (1%)
    all_to_all x2, blocking collectives, body(): lax.all_to_all(sending.reshape(OWNERS, ROWS, POINTS), ('grid', 'line'), s...  39.9 us
    pallas_call x6, Pallas kernels, call(): pl.pallas_call(kernel, out_shape=outputs, in_specs=[in_space] * len(input...  22.2 us
    ppermute x8, starting transfers between devices, beside(): around.append(lax.ppermute(field, axis, pairs + [(b, a) for a, b in pairs]))  13.7 us
  transfers between devices with their start and end apart: 8, of which 1 were waited for; matrix products, arithmetic and copies ran while one was open for 0% of the time, Pallas kernels for 7%

profile of v2, /device:TPU:1, one launch (start us, length us, event | category | flops | bytes accessed | tf_op | source)
XLA Modules:
  0.0 77.9 jit_solution(17627688865781931811)
XLA Ops:
  0.6 2.2 %collective-permute-start.2 = (f32[24,1,128]{2,1,0:T(1,128)}, f32[24,1,128]{2,1,0:T(1,128)S(1)}, u32[]{:S(2)}, u32[]{:S(2)}) collective-permute-start(f32[24,1,128]{2,1,0:T(1,128)} %refs_1_.1), channel_id=1, source_target_pairs={{0,1},{2,3},{4,5},{6,7},{8,9},{10,11},{12,13},{14,15},{1,0},{3,2},... | collective-permute-start | bytes 36872 | tf_op jit(solution)/shard_map/ppermute | solution.py:355
  2.8 2.5 %collective-permute-start.1 = (f32[24,1,128]{2,1,0:T(1,128)}, f32[24,1,128]{2,1,0:T(1,128)S(1)}, u32[]{:S(2)}, u32[]{:S(2)}) collective-permute-start(f32[24,1,128]{2,1,0:T(1,128)} %refs_1_.1), channel_id=1, source_target_pairs={{16,32},{48,64},{80,96},{112,0},{32,16},{64,48},{96,80},{0,112},{1... | collective-permute-start | bytes 36872 | tf_op jit(solution)/shard_map/ppermute | solution.py:355
  5.3 1.7 %collective-permute-start = (f32[24,1,128]{2,1,0:T(1,128)}, f32[24,1,128]{2,1,0:T(1,128)S(1)}, u32[]{:S(2)}, u32[]{:S(2)}) collective-permute-start(f32[24,1,128]{2,1,0:T(1,128)} %refs_1_.1), channel_id=1, source_target_pairs={{0,16},{32,48},{64,80},{96,112},{16,0},{48,32},{80,64},{112,96},{1... | collective-permute-start | bytes 36872 | tf_op jit(solution)/shard_map/ppermute | solution.py:355
  7.0 4.1 %collective-permute-start.3 = (f32[24,1,128]{2,1,0:T(1,128)}, f32[24,1,128]{2,1,0:T(1,128)S(1)}, u32[]{:S(2)}, u32[]{:S(2)}) collective-permute-start(f32[24,1,128]{2,1,0:T(1,128)} %refs_1_.1), channel_id=1, source_target_pairs={{1,2},{3,4},{5,6},{7,8},{9,10},{11,12},{13,14},{15,0},{2,1},{4,3},... | collective-permute-start | bytes 36872 | tf_op jit(solution)/shard_map/ppermute | solution.py:355
  11.1 0.0 copy-start.5
  11.1 0.0 copy-start.6
  11.1 4.0 %shard_map.149 = (f32[24,128,128]{2,1,0:T(8,128)S(1)}, bf16[192,192]{1,0:T(8,128)(2,1)S(1)}, bf16[192,192]{1,0:T(8,128)(2,1)S(1)}, f32[24,128]{1,0:T(8,128)S(1)}) custom-call(f32[128,24,128]{2,1,0:T(8,128)} %bitcast.14, s32[2,1,1,128]{3,2,1,0:T(1,128)} %start_ref.1, f32[1,24]{1,0:T(1,128)} %bitcast.15, f32[1,128]{1,0:T(1,128)} %constant.8.clone.eigen_hbm, ...), custom_call_target="tpu_custom_call" | custom-call | flops 4000000000 | bytes 3573856 | tf_op jit(solution)/shard_map/pallas_call | solution.py:338
  15.2 0.0 collective-permute-done.2.refs_4_
  15.2 0.0 collective-permute-done.1.refs_3_
  15.2 0.0 collective-permute-done.refs_2_
  15.2 0.0 collective-permute-done.3.refs_5_
  15.2 0.0 copy-done
  15.2 0.0 copy-done.2
  15.2 0.0 copy-done.3
  15.2 0.0 copy-done.4
  15.3 0.0 copy-done.5
  15.3 0.0 copy-done.6
  15.3 5.5 %shard_map.150 = (f32[24,128,128]{2,1,0:T(8,128)S(1)}, f32[1024,128]{1,0:T(8,128)S(1)}, f32[24,128]{1,0:T(8,128)S(1)}) custom-call(f32[24,128,128]{2,1,0:T(8,128)S(1)} %get-tuple-element.16.refs_0_, f32[24,1,128]{2,1,0:T(1,128)S(1)} %copy-done, f32[24,1,128]{2,1,0:T(1,128)S(1)} %collective-permute-done.refs_2_, ...), custom_call_target="tpu_custom_call" | custom-call | flops 8000000000 | bytes 3895808 | tf_op jit(solution)/shard_map/pallas_call | solution.py:338
  20.8 19.2 %all_to_all.10 = f32[128,8,128]{2,1,0:T(8,128)S(1)} all-to-all(f32[128,8,128]{2,1,0:T(8,128)S(1)} %bitcast.9), channel_id=1, replica_groups=mesh['grid'=8,'line'=16] {'grid','line'}, dimensions={0} | all-to-all | bytes 1048576 | tf_op jit(solution)/shard_map/all_to_all | solution.py:408
  40.1 2.3 %shard_map.151 = (f32[24,1,128]{2,1,0:T(1,128)S(1)}, f32[24,128,128]{2,1,0:T(8,128)S(1)}) custom-call(f32[1024,128]{1,0:T(8,128)S(1)} %bitcast.10, f32[24,128,128]{2,1,0:T(8,128)S(1)} %get-tuple-element.20.state_ref, f32[24,128]{1,0:T(8,128)S(1)} %get-tuple-element.21.mid_ref), custom_call_target="tpu_custom_call" | custom-call | flops 3000000000 | bytes 3694592 | tf_op jit(solution)/shard_map/pallas_call | solution.py:338
  42.4 1.8 %collective-permute-start.7 = (f32[24,1,128]{2,1,0:T(1,128)S(1)}, f32[24,1,128]{2,1,0:T(1,128)S(1)}, u32[]{:S(2)}, u32[]{:S(2)}) collective-permute-start(f32[24,1,128]{2,1,0:T(1,128)S(1)} %get-tuple-element.24.refs_1_), channel_id=1, source_target_pairs={{1,2},{3,4},{5,6},{7,8},{9,10},{11,12},{13,14},{15,0},{2,1},{4,3},... | collective-permute-start | bytes 36872 | tf_op jit(solution)/shard_map/ppermute | solution.py:355
  44.2 0.0 collective-permute-start.6
  44.2 0.8 %collective-permute-start.5 = (f32[24,1,128]{2,1,0:T(1,128)S(1)}, f32[24,1,128]{2,1,0:T(1,128)S(1)}, u32[]{:S(2)}, u32[]{:S(2)}) collective-permute-start(f32[24,1,128]{2,1,0:T(1,128)S(1)} %get-tuple-element.24.refs_1_), channel_id=1, source_target_pairs={{16,32},{48,64},{80,96},{112,0},{32,16},{64,48},{96,80},{0,112},{1... | collective-permute-start | bytes 36872 | tf_op jit(solution)/shard_map/ppermute | solution.py:355
  45.0 0.6 collective-permute-start.4
  45.7 1.5 %shard_map.152.refs_0_ = f32[24,128,128]{2,1,0:T(8,128)S(1)} custom-call(f32[24,128,128]{2,1,0:T(8,128)S(1)} %get-tuple-element.22.state_ref, s32[2,1,1,128]{3,2,1,0:T(1,128)S(1)} %copy-done.1, f32[24,128]{1,0:T(8,128)S(1)} %get-tuple-element.23.scale_ref, bf16[256,256]{1,0:T(8,128)(2,1)S(1)} %copy-done.8, bf16[256,256]{1,0:T(8,128)(2,1)S(1)} %copy-done.7), custom_call_target="tpu_custom_call" | custom-call | flops 3000000000 | bytes 3421184 | tf_op jit(solution)/shard_map/pallas_call | solution.py:338
  47.2 1.2 %collective-permute-done.7.refs_5_ = f32[24,1,128]{2,1,0:T(1,128)S(1)} collective-permute-done((f32[24,1,128]{2,1,0:T(1,128)S(1)}, f32[24,1,128]{2,1,0:T(1,128)S(1)}, u32[]{:S(2)}, u32[]{:S(2)}) %collective-permute-start.7) | collective-permute-done | bytes 12320 | tf_op jit(solution)/shard_map/ppermute | solution.py:355
  48.3 0.0 collective-permute-done.6.refs_4_
  48.3 0.0 collective-permute-done.5.refs_3_
  48.4 0.0 collective-permute-done.4.refs_2_
  48.4 5.6 %shard_map.153 = (f32[24,128,128]{2,1,0:T(8,128)S(1)}, f32[1024,128]{1,0:T(8,128)S(1)}, f32[24,128]{1,0:T(8,128)S(1)}) custom-call(f32[24,128,128]{2,1,0:T(8,128)S(1)} %shard_map.152.refs_0_, f32[24,1,128]{2,1,0:T(1,128)S(1)} %get-tuple-element.24.refs_1_, f32[24,1,128]{2,1,0:T(1,128)S(1)} %collective-permute-done.4.refs_2_, ...), custom_call_target="tpu_custom_call" | custom-call | flops 8000000000 | bytes 3895808 | tf_op jit(solution)/shard_map/pallas_call | solution.py:338
  53.9 20.6 %all_to_all.11 = f32[128,8,128]{2,1,0:T(8,128)S(1)} all-to-all(f32[128,8,128]{2,1,0:T(8,128)S(1)} %bitcast.8), channel_id=1, replica_groups=mesh['grid'=8,'line'=16] {'grid','line'}, dimensions={0} | all-to-all | bytes 1048576 | tf_op jit(solution)/shard_map/all_to_all | solution.py:408
  74.5 3.2 %shard_map.154 = (f32[24,1,128]{2,1,0:T(1,128)}, f32[3072,128]{1,0:T(8,128)}) custom-call(f32[1024,128]{1,0:T(8,128)S(1)} %bitcast.11, f32[24,128,128]{2,1,0:T(8,128)S(1)} %get-tuple-element.26.state_ref, f32[24,128]{1,0:T(8,128)S(1)} %get-tuple-element.27.mid_ref), custom_call_target="tpu_custom_call" | custom-call | flops 3000000000 | bytes 3694592 | tf_op jit(solution)/shard_map/pallas_call | solution.py:338
  (10 shorter events, 0.0 us)
Async XLA Ops:
  0.6 14.5 %collective-permute-start.2 = (f32[24,1,128]{2,1,0:T(1,128)}, f32[24,1,128]{2,1,0:T(1,128)S(1)}, u32[]{:S(2)}, u32[]{:S(2)}) collective-permute-start(f32[24,1,128]{2,1,0:T(1,128)} %refs_1_.1), channel_id=1, source_target_pairs={{0,1},{2,3},{4,5},{6,7},{8,9},{10,11},{12,13},{14,15},{1,0},{3,2},... | collective-permute-start | bytes 36872 | tf_op jit(solution)/shard_map/ppermute | solution.py:355
  2.8 12.3 %collective-permute-start.1 = (f32[24,1,128]{2,1,0:T(1,128)}, f32[24,1,128]{2,1,0:T(1,128)S(1)}, u32[]{:S(2)}, u32[]{:S(2)}) collective-permute-start(f32[24,1,128]{2,1,0:T(1,128)} %refs_1_.1), channel_id=1, source_target_pairs={{16,32},{48,64},{80,96},{112,0},{32,16},{64,48},{96,80},{0,112},{1... | collective-permute-start | bytes 36872 | tf_op jit(solution)/shard_map/ppermute | solution.py:355
  5.3 9.9 %collective-permute-start = (f32[24,1,128]{2,1,0:T(1,128)}, f32[24,1,128]{2,1,0:T(1,128)S(1)}, u32[]{:S(2)}, u32[]{:S(2)}) collective-permute-start(f32[24,1,128]{2,1,0:T(1,128)} %refs_1_.1), channel_id=1, source_target_pairs={{0,16},{32,48},{64,80},{96,112},{16,0},{48,32},{80,64},{112,96},{1... | collective-permute-start | bytes 36872 | tf_op jit(solution)/shard_map/ppermute | solution.py:355
  7.0 8.2 %collective-permute-start.3 = (f32[24,1,128]{2,1,0:T(1,128)}, f32[24,1,128]{2,1,0:T(1,128)S(1)}, u32[]{:S(2)}, u32[]{:S(2)}) collective-permute-start(f32[24,1,128]{2,1,0:T(1,128)} %refs_1_.1), channel_id=1, source_target_pairs={{1,2},{3,4},{5,6},{7,8},{9,10},{11,12},{13,14},{15,0},{2,1},{4,3},... | collective-permute-start | bytes 36872 | tf_op jit(solution)/shard_map/ppermute | solution.py:355
  11.1 4.1 %copy-start = (f32[24,1,128]{2,1,0:T(1,128)S(1)}, f32[24,1,128]{2,1,0:T(1,128)}, u32[]{:S(2)}) copy-start(f32[24,1,128]{2,1,0:T(1,128)} %refs_1_.1) | copy-start | bytes 36868
  11.1 4.1 %copy-start.2 = (s32[2,1,1,128,1]{3,4,2,1,0:T(1,128)S(1)}, s32[2,1,1,128,1]{3,4,2,1,0:T(1,128)}, u32[]{:S(2)}) copy-start(s32[2,1,1,128,1]{3,4,2,1,0:T(1,128)} %param.17) | copy-start | bytes 3076
  11.1 4.1 %copy-start.3 = (s32[2,1,1,128]{3,2,1,0:T(1,128)S(1)}, s32[2,1,1,128]{3,2,1,0:T(1,128)}, u32[]{:S(2)}) copy-start(s32[2,1,1,128]{3,2,1,0:T(1,128)} %refs_7_.3) | copy-start | bytes 3076
  11.1 4.2 %copy-start.4 = (s32[2,1,1,128]{3,2,1,0:T(1,128)S(1)}, s32[2,1,1,128]{3,2,1,0:T(1,128)}, u32[]{:S(2)}) copy-start(s32[2,1,1,128]{3,2,1,0:T(1,128)} %refs_8_.3) | copy-start | bytes 3076
  11.1 4.2 %copy-start.5 = (s32[2,1,1,128]{3,2,1,0:T(1,128)S(1)}, s32[2,1,1,128]{3,2,1,0:T(1,128)}, u32[]{:S(2)}) copy-start(s32[2,1,1,128]{3,2,1,0:T(1,128)} %refs_9_.3) | copy-start | bytes 3076
  11.1 4.2 %copy-start.6 = (s32[1,1,128]{2,1,0:T(1,128)S(1)}, s32[1,1,128]{2,1,0:T(1,128)}, u32[]{:S(2)}) copy-start(s32[1,1,128]{2,1,0:T(1,128)} %refs_10_.3) | copy-start | bytes 1540
  40.1 5.6 %copy-start.1 = (s32[2,1,1,128]{3,2,1,0:T(1,128)S(1)}, s32[2,1,1,128]{3,2,1,0:T(1,128)}, u32[]{:S(2)}) copy-start(s32[2,1,1,128]{3,2,1,0:T(1,128)} %start_ref.1) | copy-start | bytes 3076
  40.1 5.6 %copy-start.7 = (bf16[256,256]{1,0:T(8,128)(2,1)S(1)}, bf16[256,256]{1,0:T(8,128)(2,1)}, u32[]{:S(2)}) copy-start(bf16[256,256]{1,0:T(8,128)(2,1)} %constant.7.clone.second_hbm.second_ref) | copy-start | bytes 393220
  40.1 5.6 %copy-start.8 = (bf16[256,256]{1,0:T(8,128)(2,1)S(1)}, bf16[256,256]{1,0:T(8,128)(2,1)}, u32[]{:S(2)}) copy-start(bf16[256,256]{1,0:T(8,128)(2,1)} %constant.6.clone.first_hbm.first_ref) | copy-start | bytes 393220
  42.4 5.9 %collective-permute-start.7 = (f32[24,1,128]{2,1,0:T(1,128)S(1)}, f32[24,1,128]{2,1,0:T(1,128)S(1)}, u32[]{:S(2)}, u32[]{:S(2)}) collective-permute-start(f32[24,1,128]{2,1,0:T(1,128)S(1)} %get-tuple-element.24.refs_1_), channel_id=1, source_target_pairs={{1,2},{3,4},{5,6},{7,8},{9,10},{11,12},{13,14},{15,0},{2,1},{4,3},... | collective-permute-start | bytes 36872 | tf_op jit(solution)/shard_map/ppermute | solution.py:355
  44.2 4.1 %collective-permute-start.6 = (f32[24,1,128]{2,1,0:T(1,128)S(1)}, f32[24,1,128]{2,1,0:T(1,128)S(1)}, u32[]{:S(2)}, u32[]{:S(2)}) collective-permute-start(f32[24,1,128]{2,1,0:T(1,128)S(1)} %get-tuple-element.24.refs_1_), channel_id=1, source_target_pairs={{0,1},{2,3},{4,5},{6,7},{8,9},{10,11},{12,13},{14,15},{1,0},{3,2},... | collective-permute-start | bytes 36872 | tf_op jit(solution)/shard_map/ppermute | solution.py:355
  44.2 4.1 %collective-permute-start.5 = (f32[24,1,128]{2,1,0:T(1,128)S(1)}, f32[24,1,128]{2,1,0:T(1,128)S(1)}, u32[]{:S(2)}, u32[]{:S(2)}) collective-permute-start(f32[24,1,128]{2,1,0:T(1,128)S(1)} %get-tuple-element.24.refs_1_), channel_id=1, source_target_pairs={{16,32},{48,64},{80,96},{112,0},{32,16},{64,48},{96,80},{0,112},{1... | collective-permute-start | bytes 36872 | tf_op jit(solution)/shard_map/ppermute | solution.py:355
  45.0 3.3 %collective-permute-start.4 = (f32[24,1,128]{2,1,0:T(1,128)S(1)}, f32[24,1,128]{2,1,0:T(1,128)S(1)}, u32[]{:S(2)}, u32[]{:S(2)}) collective-permute-start(f32[24,1,128]{2,1,0:T(1,128)S(1)} %get-tuple-element.24.refs_1_), channel_id=1, source_target_pairs={{0,16},{32,48},{64,80},{96,112},{16,0},{48,32},{80,64},{112,96},{1... | collective-permute-start | bytes 36872 | tf_op jit(solution)/shard_map/ppermute | solution.py:355

commit v3 on v2

--- a/solution.py
+++ b/solution.py
@@ -15,7 +15,8 @@
 POINTS = 128
 LINES = 128
 OWNERS = 128
-ROWS = 8
+ROWS = 6
+AIMS = 1
 F32 = jnp.float32
 BF16 = jnp.bfloat16
 
@@ -101,14 +102,12 @@
     return jnp.where((rel >= 0) & (rel < TRIP), source + start, place)
 
 
-def mixing(read, start_row, scale_ref, first_ref, second_ref, state_ref, index_ref, ready=None):
+def mixing(read, start_row, scale_ref, first_ref, second_ref, state_ref, index_ref):
     index_ref[...] = triplet_index(column(start_row))
     group = 8
 
     for at in range(SPECIES // group):
         species = [at * group + i for i in range(group)]
-        if ready is not None:
-            ready(at)
         value = jnp.concatenate([lane_pick(read(s), index_ref[...]) for s in species], axis=0)
         wide = dot(jnp.concatenate(halves(value), axis=1), first_ref[...])
         value = wide[:, :POINTS] + wide[:, POINTS:]
@@ -120,8 +119,7 @@
             state_ref[s] = value[i]
 
 
-def chemistry(counts_row, shift, high_ref, low_ref, mixed_ref, state_ref, counts_ref, finish):
-    counts_ref[...] = column(counts_row)
+def chemistry(turns_ref, shift, high_ref, low_ref, mixed_ref, state_ref, finish):
     side = SPECIES * 8
 
     def shifted(part):
@@ -136,7 +134,7 @@
             change = dot(high_ref[...], high) + (dot(low_ref[...], high) + dot(high_ref[...], low))
             done = []
             for at, part in enumerate(parts):
-                active = (counts_ref[part, :] > float(turn))[None]
+                active = (turns_ref[part, :] > float(turn))[None]
                 before = old[at].reshape(SPECIES, 8, POINTS)
                 after = before + change[:, at * POINTS : (at + 1) * POINTS].reshape(SPECIES, 8, POINTS)
                 done.append(jnp.where(active, after, before))
@@ -145,19 +143,50 @@
                 finish(unit, done)
 
 
-def pack_tables(owner_row, line_row, from_row, to_row, pick_ref, group_ref, placing_ref, aims_ref):
+def pick_tables(from_row, to_row, pick_ref, group_ref):
     lane = iota(1)
     pick_ref[...] = column(from_row).astype(jnp.int32) * SEG + lane % SEG
-    landing = column(to_row)
-    group_ref[...] = (lane // SEG - landing.astype(jnp.int32)) & 7
+    group_ref[...] = (lane // SEG - column(to_row).astype(jnp.int32)) & 7
+
+
+def place_tables(owner_row, placing_ref):
+    lane = iota(1)
     owner = column(owner_row).astype(jnp.int32)
     earlier = (owner == owner_row) & (iota(0) < lane)
     rank = jnp.sum(earlier.astype(F32), axis=0, keepdims=True)
-    aims_ref[...] = jnp.where(lane < 64, column(line_row) + 1.0, landing).astype(BF16)
     for slot in range(2):
         placing = ((iota(0) == owner_row) & (rank == slot)).astype(F32).astype(BF16)
         placing_ref[slot, :, :LINES] = placing
         placing_ref[slot, :, LINES:] = placing
+
+
+def aim_rows(step, line_row, to_row):
+    lane = iota(1)
+    line, segment = column(line_row) + 1.0, column(to_row)
+    rows = []
+    for slot in range(2):
+        at = 4 * step + 2 * slot
+        rows.append(jnp.where(lane // SEG == at, line, jnp.where(lane // SEG == at + 1, segment, 0.0)).astype(BF16))
+    return rows
+
+
+def aim_codes(aims):
+    turned_aims = jnp.transpose(aims)
+
+    def code(at):
+        line, segment = turned_aims[SEG * at : SEG * at + 1], turned_aims[SEG * at + SEG : SEG * at + SEG + 1]
+        return segment * LINES + line - 1.0
+
+    return [[code(4 * step + 2 * slot) for slot in range(2)] for step in range(STEPS)]
+
+
+def hit_table(codes, hits_ref):
+    place = iota(0).astype(F32)
+    for slot in range(2):
+        for segment in range(8):
+            hit = jnp.where(place + float(segment * LINES) == codes[slot], 0.5, 0.0).astype(BF16)
+            for at in (slot, 2 + slot):
+                hits_ref[segment * LINES : (segment + 1) * LINES, at * OWNERS : (at + 1) * OWNERS] = hit
 
 
 def pack_segments(unit, values, pick_ref, group_ref, out_ref):
@@ -176,33 +205,25 @@
         out_ref[LINES + 16 * unit : LINES + 16 * unit + 16, columns] = low
 
 
-def sending_rows(placing_ref, aims_ref, out_ref, send_ref):
+def sending_rows(placing_ref, out_ref, send_ref, rows):
     for slot in range(2):
         sending = dot(placing_ref[slot], out_ref[...])
         for third in range(3):
-            send_ref[pl.ds(3 * slot + third, OWNERS, stride=ROWS), :] = sending[
+            send_ref[pl.ds(3 * slot + third, OWNERS, stride=rows), :] = sending[
                 :, third * POINTS : (third + 1) * POINTS
             ]
-        send_ref[pl.ds(6 + slot, OWNERS, stride=ROWS), :] = dot(placing_ref[slot, :, :LINES], aims_ref[...])
-
-
-def splicing(received_ref, state_ref, write, parts_ref, hits_ref, gain_ref):
-    place = iota(0).astype(F32)
+
+
+def splicing(received_ref, rows, state_ref, write, parts_ref, hits_ref, gain_ref):
     for slot in range(2):
-        aim = jnp.transpose(received_ref[pl.ds(6 + slot, OWNERS, stride=ROWS), :])
-        code = aim[64:65] * LINES + aim[:1] - 1.0
-        rows = slice(slot * OWNERS, (slot + 1) * OWNERS)
+        highs = slice(slot * OWNERS, (slot + 1) * OWNERS)
         lows = slice((2 + slot) * OWNERS, (3 + slot) * OWNERS)
         for third in range(3):
-            high, low = halves(received_ref[pl.ds(3 * slot + third, OWNERS, stride=ROWS), :])
-            parts_ref[rows, third * POINTS : (third + 1) * POINTS] = high
+            high, low = halves(received_ref[pl.ds(3 * slot + third, OWNERS, stride=rows), :])
+            parts_ref[highs, third * POINTS : (third + 1) * POINTS] = high
             parts_ref[lows, third * POINTS : (third + 1) * POINTS] = low
-        parts_ref[rows, 3 * POINTS :] = jnp.ones((OWNERS, POINTS), BF16)
+        parts_ref[highs, 3 * POINTS :] = jnp.ones((OWNERS, POINTS), BF16)
         parts_ref[lows, 3 * POINTS :] = jnp.zeros((OWNERS, POINTS), BF16)
-        for segment in range(8):
-            hit = jnp.where(place + float(segment * LINES) == code, 0.5, 0.0).astype(BF16)
-            hits_ref[segment * LINES : (segment + 1) * LINES, rows] = hit
-            hits_ref[segment * LINES : (segment + 1) * LINES, lows] = hit
     gain_ref[...] = dot(hits_ref[...], parts_ref[...]).reshape(8, LINES, 4 * POINTS)
     group = iota(1, (8, POINTS)) // SEG
     bits = [(group & bit) != 0 for bit in (1, 2, 4)]
@@ -256,51 +277,79 @@
     copies = [pltpu.make_async_copy(a, b, sems.at[i]) for i, (a, b) in enumerate(zip(there, here))]
     for copy in copies:
         copy.start()
-    for copy in copies[:7]:
+    for copy in copies:
         copy.wait()
     mix_tables(rates_ref[...], frozen_ref[...], high_ref, low_ref)
     scale_ref[...] = scales(diffusivity_ref[...], eigen_ref[...])
 
-    def ready(third):
-        copies[7 + third].wait()
-
     def read(s):
         return lines_ref[s // 8, pl.ds(s % 8, LINES, stride=8), :]
 
-    mixing(read, start_ref[0, 0], scale_ref, first_ref, second_ref, mixed_ref, index_ref, ready)
-
-
-def next_mix_kernel(state_ref, start_ref, scale_ref, first_ref, second_ref, mixed_ref, index_ref):
+    mixing(read, start_ref[0, 0], scale_ref, first_ref, second_ref, mixed_ref, index_ref)
+
+
+def next_mix_kernel(
+    state_ref, start_ref, scale_ref, first_ref, second_ref, from_ref, to_ref, codes_ref,
+    mixed_ref, pick_ref, group_ref, hits_ref, index_ref,
+):
     mixing(lambda s: state_ref[s], start_ref[1, 0], scale_ref, first_ref, second_ref, mixed_ref, index_ref)
-
-
-def react_kernel(
-    step, mixed_ref, les_ref, grid_even_ref, grid_odd_ref, line_even_ref, line_odd_ref, owner_ref, line_ref, from_ref,
-    to_ref, counts_ref, high_ref, low_ref, state_ref, send_ref, mid_ref, turns_ref, out_ref, pick_ref, group_ref,
-    placing_ref, aims_ref,
-):
-    mid = middle(les_ref[:, 0], grid_even_ref[:, 0], grid_odd_ref[:, 0], line_even_ref[:, 0], line_odd_ref[:, 0])
+    pick_tables(from_ref[1, 0], to_ref[1, 0], pick_ref, group_ref)
+    hit_table([codes_ref[:1], codes_ref[1:2]], hits_ref)
+
+
+def react(mixed_ref, les_ref, rim_refs, turns_ref, high_ref, low_ref, pick_ref, group_ref, state_ref, mid_ref, out_ref):
+    mid = middle(les_ref[:, 0], *[ref[:, 0] for ref in rim_refs])
     mid_ref[...] = mid
-    rows = (ref[step, 0] for ref in (owner_ref, line_ref, from_ref, to_ref))
-    pack_tables(*rows, pick_ref, group_ref, placing_ref, aims_ref)
 
     def finish(unit, values):
         pack_segments(unit, values, pick_ref, group_ref, out_ref)
 
-    chemistry(counts_ref[0], turned(0.5 * mid), high_ref, low_ref, mixed_ref, state_ref, turns_ref, finish)
-    sending_rows(placing_ref, aims_ref, out_ref, send_ref)
-
-
-def next_splice_kernel(received_ref, state_ref, mid_ref, les_ref, lines_ref, parts_ref, hits_ref, gain_ref):
+    chemistry(turns_ref, turned(0.5 * mid), high_ref, low_ref, mixed_ref, state_ref, finish)
+
+
+def first_react_kernel(
+    mixed_ref, les_ref, grid_even_ref, grid_odd_ref, line_even_ref, line_odd_ref, high_ref, low_ref, owner_ref, line_ref,
+    from_ref, to_ref, counts_ref, state_ref, send_ref, mid_ref, turns_ref, later_ref, out_ref, pick_ref, group_ref,
+    placing_ref,
+):
+    turns_ref[...] = column(counts_ref[0])
+    pick_tables(from_ref[0, 0], to_ref[0, 0], pick_ref, group_ref)
+    place_tables(owner_ref[0, 0], placing_ref)
+    place_tables(owner_ref[1, 0], later_ref)
+    aims = [row for step in range(STEPS) for row in aim_rows(step, line_ref[step, 0], to_ref[step, 0])]
+    placings = [ref[slot, :, :LINES] for ref in (placing_ref, later_ref) for slot in range(2)]
+    rows = ROWS + AIMS
+    send_ref[pl.ds(ROWS, OWNERS, stride=rows), :] = dot(
+        jnp.concatenate(placings, axis=1), jnp.concatenate(aims, axis=0)
+    )
+    rim = (grid_even_ref, grid_odd_ref, line_even_ref, line_odd_ref)
+    react(mixed_ref, les_ref, rim, turns_ref, high_ref, low_ref, pick_ref, group_ref, state_ref, mid_ref, out_ref)
+    sending_rows(placing_ref, out_ref, send_ref, rows)
+
+
+def next_react_kernel(
+    mixed_ref, les_ref, grid_even_ref, grid_odd_ref, line_even_ref, line_odd_ref, high_ref, low_ref, pick_ref, group_ref,
+    turns_ref, placing_ref, state_ref, send_ref, mid_ref, out_ref,
+):
+    rim = (grid_even_ref, grid_odd_ref, line_even_ref, line_odd_ref)
+    react(mixed_ref, les_ref, rim, turns_ref, high_ref, low_ref, pick_ref, group_ref, state_ref, mid_ref, out_ref)
+    sending_rows(placing_ref, out_ref, send_ref, ROWS)
+
+
+def next_splice_kernel(received_ref, state_ref, mid_ref, les_ref, lines_ref, codes_ref, parts_ref, gain_ref, hits_ref):
     def write(species, at, value):
         lines_ref[species, pl.ds(pl.multiple_of(8 * at, 8), 8), :] = value
 
-    splicing(received_ref, state_ref, write, parts_ref, hits_ref, gain_ref)
+    rows = ROWS + AIMS
+    codes = aim_codes(received_ref[pl.ds(ROWS, OWNERS, stride=rows), :])
+    codes_ref[...] = jnp.concatenate(codes[1] + [jnp.zeros((6, OWNERS), F32)], axis=0)
+    hit_table(codes[0], hits_ref)
+    splicing(received_ref, rows, state_ref, write, parts_ref, hits_ref, gain_ref)
     les_ref[:, 0] = 0.5 * mid_ref[...] + 0.5 * means_of(lambda s: lines_ref[s])
 
 
 def last_splice_kernel(
-    received_ref, state_ref, mid_ref, les_ref, lines_hbm, parts_ref, hits_ref, gain_ref, lines_ref, sems
+    received_ref, state_ref, mid_ref, hits_ref, les_ref, lines_hbm, parts_ref, gain_ref, lines_ref, sems
 ):
     rows = 8 * SPECIES
 
@@ -313,7 +362,7 @@
         if species == SPECIES - 1:
             out(at).start()
 
-    splicing(received_ref, state_ref, write, parts_ref, hits_ref, gain_ref)
+    splicing(received_ref, ROWS, state_ref, write, parts_ref, hits_ref, gain_ref)
     means = means_of(lambda s: lines_ref[pl.ds(s, LINES, stride=SPECIES), :])
     les_ref[:, 0] = 0.5 * mid_ref[...] + 0.5 * means
     for at in range(LINES // 8):
@@ -324,11 +373,7 @@
 HBM = pl.BlockSpec(memory_space=pltpu.HBM)
 STATE = jax.ShapeDtypeStruct((SPECIES, LINES, POINTS), F32)
 FLAT = jax.ShapeDtypeStruct((LINES * SPECIES, POINTS), F32)
-SPLICE_SCRATCH = [
-    pltpu.VMEM((4 * OWNERS, 4 * POINTS), BF16),
-    pltpu.VMEM((8 * LINES, 4 * OWNERS), BF16),
-    pltpu.VMEM((8, LINES, 4 * POINTS), F32),
-]
+SPLICE_SCRATCH = [pltpu.VMEM((4 * OWNERS, 4 * POINTS), BF16), pltpu.VMEM((8, LINES, 4 * POINTS), F32)]
 
 
 def call(kernel, inputs, outputs, scratch, micros, in_space=VMEM, out_specs=None):
@@ -369,52 +414,56 @@
     rates,
     frozen_inverse,
 ):
+    def shaped(shape, dtype=F32):
+        return jax.ShapeDtypeStruct(shape, dtype)
+
     first_table, second_table, eigen = (jnp.asarray(x) for x in cosine_tables())
     side = SPECIES * 8
-    send = jax.ShapeDtypeStruct((OWNERS * ROWS, POINTS), F32)
-    plane = jax.ShapeDtypeStruct((SPECIES, LINES), F32)
-    table = jax.ShapeDtypeStruct((side, side), BF16)
+    plane = shaped((SPECIES, LINES))
     owner = splice_owner.reshape(STEPS, 1, 1, LINES)
-    field = les
-    index = pltpu.VMEM((LINES, POINTS), jnp.int32)
-    for step in range(STEPS):
-        last = step == STEPS - 1
-        rim = beside(field)
-        if step == 0:
-            inputs = [lines.reshape(LINES, SPECIES, POINTS), triplet_start, diffusivity.reshape(1, SPECIES), eigen]
-            inputs += [first_table, second_table, rates, frozen_inverse]
-            scratch = [pltpu.VMEM((3, LINES * 8, POINTS), F32)] + [pltpu.VMEM(x.shape, x.dtype) for x in inputs[1:]]
-            scratch += [index, pltpu.SemaphoreType.DMA((len(inputs) + 2,))]
-            mixed, high, low, scale = call(
-                first_mix_kernel, inputs, [STATE, table, table, plane], scratch, 4, in_space=HBM
-            )
-        else:
-            inputs = [state, triplet_start, scale, first_table, second_table]
-            (mixed,) = call(next_mix_kernel, inputs, [STATE], [index], 3)
-
-        def react(*refs, step=step):
-            react_kernel(step, *refs)
-
-        inputs = [mixed, field, *rim, owner, splice_line, splice_from, splice_to, chem_counts, high, low]
-        scratch = [
-            pltpu.VMEM((LINES, POINTS), F32),
-            pltpu.VMEM((2 * LINES, 3 * POINTS), BF16),
-            index,
-            index,
-            pltpu.VMEM((2, OWNERS, 2 * LINES), BF16),
-            pltpu.VMEM((LINES, POINTS), BF16),
-        ]
-        state, sending, mid = call(react, inputs, [STATE, send, plane], scratch, 8)
-        received = lax.all_to_all(
-            sending.reshape(OWNERS, ROWS, POINTS), ("grid", "line"), split_axis=0, concat_axis=0, tiled=True
-        ).reshape(OWNERS * ROWS, POINTS)
-        inputs = [received, state, mid]
-        outputs = [jax.ShapeDtypeStruct(les.shape, F32), FLAT if last else STATE]
-        if last:
-            scratch = SPLICE_SCRATCH + [pltpu.VMEM(FLAT.shape, F32), pltpu.SemaphoreType.DMA((LINES // 8,))]
-            field, state = call(last_splice_kernel, inputs, outputs, scratch, 3, out_specs=[VMEM, HBM])
-        else:
-            field, state = call(next_splice_kernel, inputs, outputs, SPLICE_SCRATCH, 3)
+    square = shaped((LINES, POINTS))
+    index = shaped((LINES, POINTS), jnp.int32)
+    placing = shaped((2, OWNERS, 2 * LINES), BF16)
+    hits = shaped((8 * LINES, 4 * OWNERS), BF16)
+    scratch_of = lambda x: pltpu.VMEM(x.shape, x.dtype)
+    outgoing = pltpu.VMEM((2 * LINES, 3 * POINTS), BF16)
+
+    def exchange(sending):
+        sending = sending.reshape(OWNERS, 1, -1)
+        received = lax.all_to_all(sending, ("grid", "line"), split_axis=0, concat_axis=0, tiled=True)
+        return received.reshape(-1, POINTS)
+
+    rim = beside(les)
+    inputs = [lines.reshape(LINES, SPECIES, POINTS), triplet_start, diffusivity.reshape(1, SPECIES), eigen]
+    inputs += [first_table, second_table, rates, frozen_inverse]
+    scratch = [pltpu.VMEM((3, LINES * 8, POINTS), F32)] + [scratch_of(x) for x in inputs[1:]]
+    scratch += [scratch_of(index), pltpu.SemaphoreType.DMA((len(inputs) + 2,))]
+    table = shaped((side, side), BF16)
+    mixed, high, low, scale = call(first_mix_kernel, inputs, [STATE, table, table, plane], scratch, 4, in_space=HBM)
+
+    inputs = [mixed, les, *rim, high, low, owner, splice_line, splice_from, splice_to, chem_counts]
+    outputs = [STATE, shaped((OWNERS * (ROWS + AIMS), POINTS)), plane, square, placing]
+    scratch = [outgoing, scratch_of(index), scratch_of(index), scratch_of(placing)]
+    state, sending, mid, turns, later = call(first_react_kernel, inputs, outputs, scratch, 6)
+
+    inputs = [exchange(sending), state, mid]
+    outputs = [shaped(les.shape), STATE, shaped((8, OWNERS))]
+    field, state, codes = call(next_splice_kernel, inputs, outputs, SPLICE_SCRATCH + [scratch_of(hits)], 3)
+
+    rim = beside(field)
+    inputs = [state, triplet_start, scale, first_table, second_table, splice_from, splice_to, codes]
+    mixed, pick, group, landing = call(
+        next_mix_kernel, inputs, [STATE, index, index, hits], [scratch_of(index)], 3
+    )
+
+    inputs = [mixed, field, *rim, high, low, pick, group, turns, later]
+    outputs = [STATE, shaped((OWNERS * ROWS, POINTS)), plane]
+    state, sending, mid = call(next_react_kernel, inputs, outputs, [outgoing], 6)
+
+    inputs = [exchange(sending), state, mid, landing]
+    outputs = [shaped(les.shape), FLAT]
+    scratch = SPLICE_SCRATCH + [scratch_of(FLAT), pltpu.SemaphoreType.DMA((LINES // 8,))]
+    field, state = call(last_splice_kernel, inputs, outputs, scratch, 3, out_specs=[VMEM, HBM])
     return (field, state.reshape(lines.shape))
 
 

time: 78.1 us -> 76.1 us (0.974)
  blocking collectives: 39.9 us -> 38.7 us
    all_to_all x2, blocking collectives: 39.9 us -> 38.7 us  [exchange(): lax.all_to_all(sending, ('grid', 'line'), split_axis=0, concat_axis=0, ti...]
  transfers between devices with their start and end apart: 8 -> 8, of which waited for: 1 -> 1; matrix products, arithmetic and copies ran while one was open for 0% -> 0% of each run, Pallas kernels for 7% -> 6%
where the time goes in v3:
time: 76.1 us; the launch traced here: 76 us
  blocking collectives  38.7 us (51%)
  Pallas kernels  21.5 us (28%)
  starting transfers between devices  13.7 us (18%)
  waiting for transfers between devices  1.12 us (1%)
  between operations  0.94 us (1%)
    all_to_all x2, blocking collectives, exchange(): lax.all_to_all(sending, ('grid', 'line'), split_axis=0, concat_axis=0, ti...  38.7 us
    pallas_call x6, Pallas kernels, call(): pl.pallas_call(kernel, out_shape=outputs, in_specs=[in_space] * len(input...  21.5 us
    ppermute x8, starting transfers between devices, beside(): around.append(lax.ppermute(field, axis, pairs + [(b, a) for a, b in pairs]))  13.7 us
  transfers between devices with their start and end apart: 8, of which 1 were waited for; matrix products, arithmetic and copies ran while one was open for 0% of the time, Pallas kernels for 6%

profile of v3, /device:TPU:1, one launch (start us, length us, event | category | flops | bytes accessed | tf_op | source)
XLA Modules:
  0.0 76.0 jit_solution(14342465942753089915)
XLA Ops:
  0.6 2.2 %collective-permute-start.2 = (f32[24,1,128]{2,1,0:T(1,128)}, f32[24,1,128]{2,1,0:T(1,128)S(1)}, u32[]{:S(2)}, u32[]{:S(2)}) collective-permute-start(f32[24,1,128]{2,1,0:T(1,128)} %les_ref.1), channel_id=1, source_target_pairs={{0,1},{2,3},{4,5},{6,7},{8,9},{10,11},{12,13},{14,15},{1,0},{3,2},... | collective-permute-start | bytes 36872 | tf_op jit(solution)/shard_map/ppermute | solution.py:400
  2.8 2.5 %collective-permute-start.1 = (f32[24,1,128]{2,1,0:T(1,128)}, f32[24,1,128]{2,1,0:T(1,128)S(1)}, u32[]{:S(2)}, u32[]{:S(2)}) collective-permute-start(f32[24,1,128]{2,1,0:T(1,128)} %les_ref.1), channel_id=1, source_target_pairs={{16,32},{48,64},{80,96},{112,0},{32,16},{64,48},{96,80},{0,112},{1... | collective-permute-start | bytes 36872 | tf_op jit(solution)/shard_map/ppermute | solution.py:400
  5.3 1.7 %collective-permute-start = (f32[24,1,128]{2,1,0:T(1,128)}, f32[24,1,128]{2,1,0:T(1,128)S(1)}, u32[]{:S(2)}, u32[]{:S(2)}) collective-permute-start(f32[24,1,128]{2,1,0:T(1,128)} %les_ref.1), channel_id=1, source_target_pairs={{0,16},{32,48},{64,80},{96,112},{16,0},{48,32},{80,64},{112,96},{1... | collective-permute-start | bytes 36872 | tf_op jit(solution)/shard_map/ppermute | solution.py:400
  7.0 4.1 %collective-permute-start.3 = (f32[24,1,128]{2,1,0:T(1,128)}, f32[24,1,128]{2,1,0:T(1,128)S(1)}, u32[]{:S(2)}, u32[]{:S(2)}) collective-permute-start(f32[24,1,128]{2,1,0:T(1,128)} %les_ref.1), channel_id=1, source_target_pairs={{1,2},{3,4},{5,6},{7,8},{9,10},{11,12},{13,14},{15,0},{2,1},{4,3},... | collective-permute-start | bytes 36872 | tf_op jit(solution)/shard_map/ppermute | solution.py:400
  11.1 0.0 copy-start.5
  11.1 0.0 copy-start.6
  11.1 3.3 %shard_map.149 = (f32[24,128,128]{2,1,0:T(8,128)S(1)}, bf16[192,192]{1,0:T(8,128)(2,1)S(1)}, bf16[192,192]{1,0:T(8,128)(2,1)S(1)}, f32[24,128]{1,0:T(8,128)S(1)}) custom-call(f32[128,24,128]{2,1,0:T(8,128)} %bitcast.13, s32[2,1,1,128]{3,2,1,0:T(1,128)} %start_ref.1, f32[1,24]{1,0:T(1,128)} %bitcast.14, f32[1,128]{1,0:T(1,128)} %constant.8.clone.eigen_hbm, ...), custom_call_target="tpu_custom_call" | custom-call | flops 4000000000 | bytes 3573856 | tf_op jit(solution)/shard_map/pallas_call | solution.py:383
  14.4 0.0 collective-permute-done.2.line_even_ref
  14.4 0.0 collective-permute-done.1.grid_odd_ref
  14.4 0.0 collective-permute-done.grid_even_ref
  14.5 0.0 collective-permute-done.3.line_odd_ref
  14.5 0.0 copy-done
  14.5 0.0 copy-done.1
  14.5 0.0 copy-done.2
  14.5 0.0 copy-done.4
  14.5 5.7 %shard_map.150 = (f32[24,128,128]{2,1,0:T(8,128)S(1)}, f32[896,128]{1,0:T(8,128)S(1)}, f32[24,128]{1,0:T(8,128)S(1)}, f32[128,128]{1,0:T(8,128)S(1)}, bf16[2,128,256]{2,1,0:T(8,128)(2,1)S(1)}) custom-call(f32[24,128,128]{2,1,0:T(8,128)S(1)} %get-tuple-element.23.mixed_ref, f32[24,1,128]{2,1,0:T(1,128)S(1)} %copy-done, ...), custom_call_target="tpu_custom_call" | custom-call | flops 6000000000 | bytes 4026880 | tf_op jit(solution)/shard_map/pallas_call | solution.py:383
  20.2 19.3 %all_to_all.10 = f32[128,1,896]{2,1,0:T(1,128)S(1)} all-to-all(f32[128,1,896]{2,1,0:T(1,128)S(1)} %bitcast.8), channel_id=1, replica_groups=mesh['grid'=8,'line'=16] {'grid','line'}, dimensions={0} | all-to-all | bytes 917504 | tf_op jit(solution)/shard_map/all_to_all | solution.py:433
  39.5 2.3 %shard_map.151 = (f32[24,1,128]{2,1,0:T(1,128)S(1)}, f32[24,128,128]{2,1,0:T(8,128)S(1)}, f32[8,128]{1,0:T(8,128)S(1)}) custom-call(f32[896,128]{1,0:T(8,128)S(1)} %bitcast.9, f32[24,128,128]{2,1,0:T(8,128)S(1)} %get-tuple-element.27.state_ref, f32[24,128]{1,0:T(8,128)S(1)} %get-tuple-element.28.mid_ref), custom_call_target="tpu_custom_call" | custom-call | flops 3000000000 | bytes 3633152 | tf_op jit(solution)/shard_map/pallas_call | solution.py:383
  41.8 1.8 %collective-permute-start.7 = (f32[24,1,128]{2,1,0:T(1,128)S(1)}, f32[24,1,128]{2,1,0:T(1,128)S(1)}, u32[]{:S(2)}, u32[]{:S(2)}) collective-permute-start(f32[24,1,128]{2,1,0:T(1,128)S(1)} %get-tuple-element.33.les_ref), channel_id=1, source_target_pairs={{1,2},{3,4},{5,6},{7,8},{9,10},{11,12},{13,14},{15,0},{2,1},{4,3},... | collective-permute-start | bytes 36872 | tf_op jit(solution)/shard_map/ppermute | solution.py:400
  43.6 0.0 collective-permute-start.6
  43.6 0.8 %collective-permute-start.5 = (f32[24,1,128]{2,1,0:T(1,128)S(1)}, f32[24,1,128]{2,1,0:T(1,128)S(1)}, u32[]{:S(2)}, u32[]{:S(2)}) collective-permute-start(f32[24,1,128]{2,1,0:T(1,128)S(1)} %get-tuple-element.33.les_ref), channel_id=1, source_target_pairs={{16,32},{48,64},{80,96},{112,0},{32,16},{64,48},{96,80},{0,112},{1... | collective-permute-start | bytes 36872 | tf_op jit(solution)/shard_map/ppermute | solution.py:400
  44.4 0.6 collective-permute-start.4
  45.1 0.0 copy-done.3
  45.1 0.0 copy-done.8
  45.1 1.6 %shard_map.152 = (f32[24,128,128]{2,1,0:T(8,128)S(1)}, s32[128,128]{1,0:T(8,128)S(1)}, s32[128,128]{1,0:T(8,128)S(1)}, bf16[1024,512]{1,0:T(8,128)(2,1)S(1)}) custom-call(f32[24,128,128]{2,1,0:T(8,128)S(1)} %get-tuple-element.29.state_ref, s32[2,1,1,128]{3,2,1,0:T(1,128)S(1)} %copy-done.3, f32[24,128]{1,0:T(8,128)S(1)} %get-tuple-element.30.scale_ref, ...), custom_call_target="tpu_custom_call" | custom-call | flops 3000000000 | bytes 4606976 | tf_op jit(solution)/shard_map/pallas_call | solution.py:383
  46.7 1.1 %collective-permute-done.7.line_odd_ref = f32[24,1,128]{2,1,0:T(1,128)S(1)} collective-permute-done((f32[24,1,128]{2,1,0:T(1,128)S(1)}, f32[24,1,128]{2,1,0:T(1,128)S(1)}, u32[]{:S(2)}, u32[]{:S(2)}) %collective-permute-start.7) | collective-permute-done | bytes 12320 | tf_op jit(solution)/shard_map/ppermute | solution.py:400
  47.8 0.0 collective-permute-done.6.line_even_ref
  47.8 0.0 collective-permute-done.5.grid_odd_ref
  47.8 0.0 collective-permute-done.4.grid_even_ref
  47.8 5.5 %shard_map.153 = (f32[24,128,128]{2,1,0:T(8,128)S(1)}, f32[768,128]{1,0:T(8,128)S(1)}, f32[24,128]{1,0:T(8,128)S(1)}) custom-call(f32[24,128,128]{2,1,0:T(8,128)S(1)} %get-tuple-element.32.mixed_ref, f32[24,1,128]{2,1,0:T(1,128)S(1)} %get-tuple-element.33.les_ref, f32[24,1,128]{2,1,0:T(1,128)S(1)} %collective-permute-done.4.grid_even_ref, ...), custom_call_target="tpu_custom_call" | custom-call | flops 6000000000 | bytes 4087808 | tf_op jit(solution)/shard_map/pallas_call | solution.py:383
  53.3 19.4 %all_to_all.11 = f32[128,1,768]{2,1,0:T(1,128)S(1)} all-to-all(f32[128,1,768]{2,1,0:T(1,128)S(1)} %bitcast.10), channel_id=1, replica_groups=mesh['grid'=8,'line'=16] {'grid','line'}, dimensions={0} | all-to-all | bytes 786432 | tf_op jit(solution)/shard_map/all_to_all | solution.py:433
  72.7 3.1 %shard_map.154 = (f32[24,1,128]{2,1,0:T(1,128)}, f32[3072,128]{1,0:T(8,128)}) custom-call(f32[768,128]{1,0:T(8,128)S(1)} %bitcast.11, f32[24,128,128]{2,1,0:T(8,128)S(1)} %get-tuple-element.39.state_ref, f32[24,128]{1,0:T(8,128)S(1)} %get-tuple-element.40.mid_ref, bf16[1024,512]{1,0:T(8,128)(2,1)S(1)} %get-tuple-element.41.hits_ref), custom_call_target="tpu_custom_call" | custom-call | flops 3000000000 | bytes 4612096 | tf_op jit(solution)/shard_map/pallas_call | solution.py:383
  (10 shorter events, 0.0 us)
Async XLA Ops:
  0.6 13.8 %collective-permute-start.2 = (f32[24,1,128]{2,1,0:T(1,128)}, f32[24,1,128]{2,1,0:T(1,128)S(1)}, u32[]{:S(2)}, u32[]{:S(2)}) collective-permute-start(f32[24,1,128]{2,1,0:T(1,128)} %les_ref.1), channel_id=1, source_target_pairs={{0,1},{2,3},{4,5},{6,7},{8,9},{10,11},{12,13},{14,15},{1,0},{3,2},... | collective-permute-start | bytes 36872 | tf_op jit(solution)/shard_map/ppermute | solution.py:400
  2.8 11.6 %collective-permute-start.1 = (f32[24,1,128]{2,1,0:T(1,128)}, f32[24,1,128]{2,1,0:T(1,128)S(1)}, u32[]{:S(2)}, u32[]{:S(2)}) collective-permute-start(f32[24,1,128]{2,1,0:T(1,128)} %les_ref.1), channel_id=1, source_target_pairs={{16,32},{48,64},{80,96},{112,0},{32,16},{64,48},{96,80},{0,112},{1... | collective-permute-start | bytes 36872 | tf_op jit(solution)/shard_map/ppermute | solution.py:400
  5.3 9.1 %collective-permute-start = (f32[24,1,128]{2,1,0:T(1,128)}, f32[24,1,128]{2,1,0:T(1,128)S(1)}, u32[]{:S(2)}, u32[]{:S(2)}) collective-permute-start(f32[24,1,128]{2,1,0:T(1,128)} %les_ref.1), channel_id=1, source_target_pairs={{0,16},{32,48},{64,80},{96,112},{16,0},{48,32},{80,64},{112,96},{1... | collective-permute-start | bytes 36872 | tf_op jit(solution)/shard_map/ppermute | solution.py:400
  7.0 7.5 %collective-permute-start.3 = (f32[24,1,128]{2,1,0:T(1,128)}, f32[24,1,128]{2,1,0:T(1,128)S(1)}, u32[]{:S(2)}, u32[]{:S(2)}) collective-permute-start(f32[24,1,128]{2,1,0:T(1,128)} %les_ref.1), channel_id=1, source_target_pairs={{1,2},{3,4},{5,6},{7,8},{9,10},{11,12},{13,14},{15,0},{2,1},{4,3},... | collective-permute-start | bytes 36872 | tf_op jit(solution)/shard_map/ppermute | solution.py:400
  11.1 3.4 %copy-start = (f32[24,1,128]{2,1,0:T(1,128)S(1)}, f32[24,1,128]{2,1,0:T(1,128)}, u32[]{:S(2)}) copy-start(f32[24,1,128]{2,1,0:T(1,128)} %les_ref.1) | copy-start | bytes 36868
  11.1 3.4 %copy-start.1 = (s32[2,1,1,128,1]{3,4,2,1,0:T(1,128)S(1)}, s32[2,1,1,128,1]{3,4,2,1,0:T(1,128)}, u32[]{:S(2)}) copy-start(s32[2,1,1,128,1]{3,4,2,1,0:T(1,128)} %param.17) | copy-start | bytes 3076
  11.1 3.4 %copy-start.2 = (s32[2,1,1,128]{3,2,1,0:T(1,128)S(1)}, s32[2,1,1,128]{3,2,1,0:T(1,128)}, u32[]{:S(2)}) copy-start(s32[2,1,1,128]{3,2,1,0:T(1,128)} %line_ref.1) | copy-start | bytes 3076
  11.1 3.4 %copy-start.4 = (s32[2,1,1,128]{3,2,1,0:T(1,128)S(1)}, s32[2,1,1,128]{3,2,1,0:T(1,128)}, u32[]{:S(2)}) copy-start(s32[2,1,1,128]{3,2,1,0:T(1,128)} %from_ref.3) | copy-start | bytes 3076
  11.1 3.4 %copy-start.5 = (s32[2,1,1,128]{3,2,1,0:T(1,128)S(1)}, s32[2,1,1,128]{3,2,1,0:T(1,128)}, u32[]{:S(2)}) copy-start(s32[2,1,1,128]{3,2,1,0:T(1,128)} %to_ref.3) | copy-start | bytes 3076
  11.1 3.4 %copy-start.6 = (s32[1,1,128]{2,1,0:T(1,128)S(1)}, s32[1,1,128]{2,1,0:T(1,128)}, u32[]{:S(2)}) copy-start(s32[1,1,128]{2,1,0:T(1,128)} %counts_ref.1) | copy-start | bytes 1540
  39.5 5.5 %copy-start.3 = (s32[2,1,1,128]{3,2,1,0:T(1,128)S(1)}, s32[2,1,1,128]{3,2,1,0:T(1,128)}, u32[]{:S(2)}) copy-start(s32[2,1,1,128]{3,2,1,0:T(1,128)} %start_ref.1) | copy-start | bytes 3076
  39.5 5.5 %copy-start.7 = (bf16[256,256]{1,0:T(8,128)(2,1)S(1)}, bf16[256,256]{1,0:T(8,128)(2,1)}, u32[]{:S(2)}) copy-start(bf16[256,256]{1,0:T(8,128)(2,1)} %constant.7.clone.second_hbm.second_ref) | copy-start | bytes 393220
  39.5 5.5 %copy-start.8 = (bf16[256,256]{1,0:T(8,128)(2,1)S(1)}, bf16[256,256]{1,0:T(8,128)(2,1)}, u32[]{:S(2)}) copy-start(bf16[256,256]{1,0:T(8,128)(2,1)} %constant.6.clone.first_hbm.first_ref) | copy-start | bytes 393220
  41.8 5.9 %collective-permute-start.7 = (f32[24,1,128]{2,1,0:T(1,128)S(1)}, f32[24,1,128]{2,1,0:T(1,128)S(1)}, u32[]{:S(2)}, u32[]{:S(2)}) collective-permute-start(f32[24,1,128]{2,1,0:T(1,128)S(1)} %get-tuple-element.33.les_ref), channel_id=1, source_target_pairs={{1,2},{3,4},{5,6},{7,8},{9,10},{11,12},{13,14},{15,0},{2,1},{4,3},... | collective-permute-start | bytes 36872 | tf_op jit(solution)/shard_map/ppermute | solution.py:400
  43.6 4.2 %collective-permute-start.6 = (f32[24,1,128]{2,1,0:T(1,128)S(1)}, f32[24,1,128]{2,1,0:T(1,128)S(1)}, u32[]{:S(2)}, u32[]{:S(2)}) collective-permute-start(f32[24,1,128]{2,1,0:T(1,128)S(1)} %get-tuple-element.33.les_ref), channel_id=1, source_target_pairs={{0,1},{2,3},{4,5},{6,7},{8,9},{10,11},{12,13},{14,15},{1,0},{3,2},... | collective-permute-start | bytes 36872 | tf_op jit(solution)/shard_map/ppermute | solution.py:400
  43.6 4.2 %collective-permute-start.5 = (f32[24,1,128]{2,1,0:T(1,128)S(1)}, f32[24,1,128]{2,1,0:T(1,128)S(1)}, u32[]{:S(2)}, u32[]{:S(2)}) collective-permute-start(f32[24,1,128]{2,1,0:T(1,128)S(1)} %get-tuple-element.33.les_ref), channel_id=1, source_target_pairs={{16,32},{48,64},{80,96},{112,0},{32,16},{64,48},{96,80},{0,112},{1... | collective-permute-start | bytes 36872 | tf_op jit(solution)/shard_map/ppermute | solution.py:400
  44.4 3.4 %collective-permute-start.4 = (f32[24,1,128]{2,1,0:T(1,128)S(1)}, f32[24,1,128]{2,1,0:T(1,128)S(1)}, u32[]{:S(2)}, u32[]{:S(2)}) collective-permute-start(f32[24,1,128]{2,1,0:T(1,128)S(1)} %get-tuple-element.33.les_ref), channel_id=1, source_target_pairs={{0,16},{32,48},{64,80},{96,112},{16,0},{48,32},{80,64},{112,96},{1... | collective-permute-start | bytes 36872 | tf_op jit(solution)/shard_map/ppermute | solution.py:400

commit v4 on v3

--- a/solution.py
+++ b/solution.py
@@ -272,8 +272,8 @@
 ):
     here = [lines_ref.at[third].reshape(LINES, 8, POINTS) for third in range(3)]
     there = [lines_hbm.at[:, pl.ds(8 * third, 8), :] for third in range(3)]
-    here = [rates_ref, frozen_ref, diffusivity_ref, eigen_ref, start_ref, first_ref, second_ref] + here
-    there = [rates_hbm, frozen_hbm, diffusivity_hbm, eigen_hbm, start_hbm, first_hbm, second_hbm] + there
+    here += [rates_ref, frozen_ref, diffusivity_ref, eigen_ref, start_ref, first_ref, second_ref]
+    there += [rates_hbm, frozen_hbm, diffusivity_hbm, eigen_hbm, start_hbm, first_hbm, second_hbm]
     copies = [pltpu.make_async_copy(a, b, sems.at[i]) for i, (a, b) in enumerate(zip(there, here))]
     for copy in copies:
         copy.start()
@@ -308,7 +308,7 @@
 
 
 def first_react_kernel(
-    mixed_ref, les_ref, grid_even_ref, grid_odd_ref, line_even_ref, line_odd_ref, high_ref, low_ref, owner_ref, line_ref,
+    mixed_ref, les_ref, line_even_ref, grid_odd_ref, line_odd_ref, grid_even_ref, high_ref, low_ref, owner_ref, line_ref,
     from_ref, to_ref, counts_ref, state_ref, send_ref, mid_ref, turns_ref, later_ref, out_ref, pick_ref, group_ref,
     placing_ref,
 ):
@@ -328,7 +328,7 @@
 
 
 def next_react_kernel(
-    mixed_ref, les_ref, grid_even_ref, grid_odd_ref, line_even_ref, line_odd_ref, high_ref, low_ref, pick_ref, group_ref,
+    mixed_ref, les_ref, grid_even_ref, line_even_ref, grid_odd_ref, line_odd_ref, high_ref, low_ref, pick_ref, group_ref,
     turns_ref, placing_ref, state_ref, send_ref, mid_ref, out_ref,
 ):
     rim = (grid_even_ref, grid_odd_ref, line_even_ref, line_odd_ref)
@@ -433,7 +433,7 @@
         received = lax.all_to_all(sending, ("grid", "line"), split_axis=0, concat_axis=0, tiled=True)
         return received.reshape(-1, POINTS)
 
-    rim = beside(les)
+    grid_even, grid_odd, line_even, line_odd = beside(les)
     inputs = [lines.reshape(LINES, SPECIES, POINTS), triplet_start, diffusivity.reshape(1, SPECIES), eigen]
     inputs += [first_table, second_table, rates, frozen_inverse]
     scratch = [pltpu.VMEM((3, LINES * 8, POINTS), F32)] + [scratch_of(x) for x in inputs[1:]]
@@ -441,7 +441,7 @@
     table = shaped((side, side), BF16)
     mixed, high, low, scale = call(first_mix_kernel, inputs, [STATE, table, table, plane], scratch, 4, in_space=HBM)
 
-    inputs = [mixed, les, *rim, high, low, owner, splice_line, splice_from, splice_to, chem_counts]
+    inputs = [mixed, les, line_even, grid_odd, line_odd, grid_even, high, low, owner, splice_line, splice_from, splice_to, chem_counts]
     outputs = [STATE, shaped((OWNERS * (ROWS + AIMS), POINTS)), plane, square, placing]
     scratch = [outgoing, scratch_of(index), scratch_of(index), scratch_of(placing)]
     state, sending, mid, turns, later = call(first_react_kernel, inputs, outputs, scratch, 6)
@@ -450,13 +450,13 @@
     outputs = [shaped(les.shape), STATE, shaped((8, OWNERS))]
     field, state, codes = call(next_splice_kernel, inputs, outputs, SPLICE_SCRATCH + [scratch_of(hits)], 3)
 
-    rim = beside(field)
+    grid_even, grid_odd, line_even, line_odd = beside(field)
     inputs = [state, triplet_start, scale, first_table, second_table, splice_from, splice_to, codes]
     mixed, pick, group, landing = call(
         next_mix_kernel, inputs, [STATE, index, index, hits], [scratch_of(index)], 3
     )
 
-    inputs = [mixed, field, *rim, high, low, pick, group, turns, later]
+    inputs = [mixed, field, grid_even, line_even, grid_odd, line_odd, high, low, pick, group, turns, later]
     outputs = [STATE, shaped((OWNERS * ROWS, POINTS)), plane]
     state, sending, mid = call(next_react_kernel, inputs, outputs, [outgoing], 6)
 

time: 76.1 us -> 73.6 us (0.967)
  blocking collectives: 38.7 us -> 36.7 us
    all_to_all x2, blocking collectives: 38.7 us -> 36.7 us  [exchange(): lax.all_to_all(sending, ('grid', 'line'), split_axis=0, concat_axis=0, ti...]
  transfers between devices with their start and end apart: 8 -> 8, of which waited for: 1 -> 1; matrix products, arithmetic and copies ran while one was open for 0% -> 0% of each run, Pallas kernels for 6% -> 7%
where the time goes in v4:
time: 73.6 us; the launch traced here: 73.4 us
  blocking collectives  36.7 us (50%)
  Pallas kernels  21.4 us (29%)
  starting transfers between devices  13.2 us (18%)
  waiting for transfers between devices  1.12 us (2%)
  between operations  0.94 us (1%)
    all_to_all x2, blocking collectives, exchange(): lax.all_to_all(sending, ('grid', 'line'), split_axis=0, concat_axis=0, ti...  36.7 us
    pallas_call x6, Pallas kernels, call(): pl.pallas_call(kernel, out_shape=outputs, in_specs=[in_space] * len(input...  21.4 us
    ppermute x8, starting transfers between devices, beside(): around.append(lax.ppermute(field, axis, pairs + [(b, a) for a, b in pairs]))  13.2 us
  transfers between devices with their start and end apart: 8, of which 1 were waited for; matrix products, arithmetic and copies ran while one was open for 0% of the time, Pallas kernels for 7%

profile of v4, /device:TPU:1, one launch (start us, length us, event | category | flops | bytes accessed | tf_op | source)
XLA Modules:
  0.0 73.4 jit_solution(7034117349525790723)
XLA Ops:
  0.6 5.8 %collective-permute-start.2 = (f32[24,1,128]{2,1,0:T(1,128)}, f32[24,1,128]{2,1,0:T(1,128)S(1)}, u32[]{:S(2)}, u32[]{:S(2)}) collective-permute-start(f32[24,1,128]{2,1,0:T(1,128)} %les_ref.1), channel_id=1, source_target_pairs={{1,2},{3,4},{5,6},{7,8},{9,10},{11,12},{13,14},{15,0},{2,1},{4,3},... | collective-permute-start | bytes 36872 | tf_op jit(solution)/shard_map/ppermute | solution.py:400
  6.5 2.5 %collective-permute-start.1 = (f32[24,1,128]{2,1,0:T(1,128)}, f32[24,1,128]{2,1,0:T(1,128)S(1)}, u32[]{:S(2)}, u32[]{:S(2)}) collective-permute-start(f32[24,1,128]{2,1,0:T(1,128)} %les_ref.1), channel_id=1, source_target_pairs={{16,32},{48,64},{80,96},{112,0},{32,16},{64,48},{96,80},{0,112},{1... | collective-permute-start | bytes 36872 | tf_op jit(solution)/shard_map/ppermute | solution.py:400
  8.9 0.0 collective-permute-start
  9.0 1.7 %collective-permute-start.3 = (f32[24,1,128]{2,1,0:T(1,128)}, f32[24,1,128]{2,1,0:T(1,128)S(1)}, u32[]{:S(2)}, u32[]{:S(2)}) collective-permute-start(f32[24,1,128]{2,1,0:T(1,128)} %les_ref.1), channel_id=1, source_target_pairs={{0,16},{32,48},{64,80},{96,112},{16,0},{48,32},{80,64},{112,96},{1... | collective-permute-start | bytes 36872 | tf_op jit(solution)/shard_map/ppermute | solution.py:400
  10.6 0.0 copy-start.5
  10.6 0.0 copy-start.6
  10.7 3.2 %shard_map.149 = (f32[24,128,128]{2,1,0:T(8,128)S(1)}, bf16[192,192]{1,0:T(8,128)(2,1)S(1)}, bf16[192,192]{1,0:T(8,128)(2,1)S(1)}, f32[24,128]{1,0:T(8,128)S(1)}) custom-call(f32[128,24,128]{2,1,0:T(8,128)} %bitcast.13, s32[2,1,1,128]{3,2,1,0:T(1,128)} %start_ref.1, f32[1,24]{1,0:T(1,128)} %bitcast.14, f32[1,128]{1,0:T(1,128)} %constant.8.clone.eigen_hbm, ...), custom_call_target="tpu_custom_call" | custom-call | flops 4000000000 | bytes 3573856 | tf_op jit(solution)/shard_map/pallas_call | solution.py:383
  13.9 0.0 collective-permute-done.2.line_odd_ref
  13.9 0.0 collective-permute-done.1.grid_odd_ref
  13.9 0.0 collective-permute-done.line_even_ref
  13.9 0.0 collective-permute-done.3.grid_even_ref
  13.9 0.0 copy-done
  13.9 0.0 copy-done.1
  13.9 0.0 copy-done.2
  13.9 0.0 copy-done.4
  13.9 0.0 copy-done.5
  14.0 5.7 %shard_map.150 = (f32[24,128,128]{2,1,0:T(8,128)S(1)}, f32[896,128]{1,0:T(8,128)S(1)}, f32[24,128]{1,0:T(8,128)S(1)}, f32[128,128]{1,0:T(8,128)S(1)}, bf16[2,128,256]{2,1,0:T(8,128)(2,1)S(1)}) custom-call(f32[24,128,128]{2,1,0:T(8,128)S(1)} %get-tuple-element.23.mixed_ref, f32[24,1,128]{2,1,0:T(1,128)S(1)} %copy-done, ...), custom_call_target="tpu_custom_call" | custom-call | flops 6000000000 | bytes 4026880 | tf_op jit(solution)/shard_map/pallas_call | solution.py:383
  19.6 17.6 %all_to_all.10 = f32[128,1,896]{2,1,0:T(1,128)S(1)} all-to-all(f32[128,1,896]{2,1,0:T(1,128)S(1)} %bitcast.8), channel_id=1, replica_groups=mesh['grid'=8,'line'=16] {'grid','line'}, dimensions={0} | all-to-all | bytes 917504 | tf_op jit(solution)/shard_map/all_to_all | solution.py:433
  37.2 2.3 %shard_map.151 = (f32[24,1,128]{2,1,0:T(1,128)S(1)}, f32[24,128,128]{2,1,0:T(8,128)S(1)}, f32[8,128]{1,0:T(8,128)S(1)}) custom-call(f32[896,128]{1,0:T(8,128)S(1)} %bitcast.9, f32[24,128,128]{2,1,0:T(8,128)S(1)} %get-tuple-element.27.state_ref, f32[24,128]{1,0:T(8,128)S(1)} %get-tuple-element.28.mid_ref), custom_call_target="tpu_custom_call" | custom-call | flops 3000000000 | bytes 3633152 | tf_op jit(solution)/shard_map/pallas_call | solution.py:383
  39.5 1.8 %collective-permute-start.7 = (f32[24,1,128]{2,1,0:T(1,128)S(1)}, f32[24,1,128]{2,1,0:T(1,128)S(1)}, u32[]{:S(2)}, u32[]{:S(2)}) collective-permute-start(f32[24,1,128]{2,1,0:T(1,128)S(1)} %get-tuple-element.33.les_ref), channel_id=1, source_target_pairs={{1,2},{3,4},{5,6},{7,8},{9,10},{11,12},{13,14},{15,0},{2,1},{4,3},... | collective-permute-start | bytes 36872 | tf_op jit(solution)/shard_map/ppermute | solution.py:400
  41.3 0.5 collective-permute-start.6
  41.8 0.1 collective-permute-start.5
  41.9 0.9 %collective-permute-start.4 = (f32[24,1,128]{2,1,0:T(1,128)S(1)}, f32[24,1,128]{2,1,0:T(1,128)S(1)}, u32[]{:S(2)}, u32[]{:S(2)}) collective-permute-start(f32[24,1,128]{2,1,0:T(1,128)S(1)} %get-tuple-element.33.les_ref), channel_id=1, source_target_pairs={{0,16},{32,48},{64,80},{96,112},{16,0},{48,32},{80,64},{112,96},{1... | collective-permute-start | bytes 36872 | tf_op jit(solution)/shard_map/ppermute | solution.py:400
  42.8 0.0 copy-done.7
  42.8 1.6 %shard_map.152 = (f32[24,128,128]{2,1,0:T(8,128)S(1)}, s32[128,128]{1,0:T(8,128)S(1)}, s32[128,128]{1,0:T(8,128)S(1)}, bf16[1024,512]{1,0:T(8,128)(2,1)S(1)}) custom-call(f32[24,128,128]{2,1,0:T(8,128)S(1)} %get-tuple-element.29.state_ref, s32[2,1,1,128]{3,2,1,0:T(1,128)S(1)} %copy-done.3, f32[24,128]{1,0:T(8,128)S(1)} %get-tuple-element.30.scale_ref, ...), custom_call_target="tpu_custom_call" | custom-call | flops 3000000000 | bytes 4606976 | tf_op jit(solution)/shard_map/pallas_call | solution.py:383
  44.4 1.1 %collective-permute-done.7.line_odd_ref = f32[24,1,128]{2,1,0:T(1,128)S(1)} collective-permute-done((f32[24,1,128]{2,1,0:T(1,128)S(1)}, f32[24,1,128]{2,1,0:T(1,128)S(1)}, u32[]{:S(2)}, u32[]{:S(2)}) %collective-permute-start.7) | collective-permute-done | bytes 12320 | tf_op jit(solution)/shard_map/ppermute | solution.py:400
  45.5 0.0 collective-permute-done.6.grid_odd_ref
  45.5 0.0 collective-permute-done.5.line_even_ref
  45.5 0.0 collective-permute-done.4.grid_even_ref
  45.5 5.5 %shard_map.153 = (f32[24,128,128]{2,1,0:T(8,128)S(1)}, f32[768,128]{1,0:T(8,128)S(1)}, f32[24,128]{1,0:T(8,128)S(1)}) custom-call(f32[24,128,128]{2,1,0:T(8,128)S(1)} %get-tuple-element.32.mixed_ref, f32[24,1,128]{2,1,0:T(1,128)S(1)} %get-tuple-element.33.les_ref, f32[24,1,128]{2,1,0:T(1,128)S(1)} %collective-permute-done.4.grid_even_ref, ...), custom_call_target="tpu_custom_call" | custom-call | flops 6000000000 | bytes 4087808 | tf_op jit(solution)/shard_map/pallas_call | solution.py:383
  51.0 19.1 %all_to_all.11 = f32[128,1,768]{2,1,0:T(1,128)S(1)} all-to-all(f32[128,1,768]{2,1,0:T(1,128)S(1)} %bitcast.10), channel_id=1, replica_groups=mesh['grid'=8,'line'=16] {'grid','line'}, dimensions={0} | all-to-all | bytes 786432 | tf_op jit(solution)/shard_map/all_to_all | solution.py:433
  70.1 3.1 %shard_map.154 = (f32[24,1,128]{2,1,0:T(1,128)}, f32[3072,128]{1,0:T(8,128)}) custom-call(f32[768,128]{1,0:T(8,128)S(1)} %bitcast.11, f32[24,128,128]{2,1,0:T(8,128)S(1)} %get-tuple-element.39.state_ref, f32[24,128]{1,0:T(8,128)S(1)} %get-tuple-element.40.mid_ref, bf16[1024,512]{1,0:T(8,128)(2,1)S(1)} %get-tuple-element.41.hits_ref), custom_call_target="tpu_custom_call" | custom-call | flops 3000000000 | bytes 4612096 | tf_op jit(solution)/shard_map/pallas_call | solution.py:383
  (10 shorter events, 0.0 us)
Async XLA Ops:
  0.6 13.2 %collective-permute-start.2 = (f32[24,1,128]{2,1,0:T(1,128)}, f32[24,1,128]{2,1,0:T(1,128)S(1)}, u32[]{:S(2)}, u32[]{:S(2)}) collective-permute-start(f32[24,1,128]{2,1,0:T(1,128)} %les_ref.1), channel_id=1, source_target_pairs={{1,2},{3,4},{5,6},{7,8},{9,10},{11,12},{13,14},{15,0},{2,1},{4,3},... | collective-permute-start | bytes 36872 | tf_op jit(solution)/shard_map/ppermute | solution.py:400
  6.5 7.4 %collective-permute-start.1 = (f32[24,1,128]{2,1,0:T(1,128)}, f32[24,1,128]{2,1,0:T(1,128)S(1)}, u32[]{:S(2)}, u32[]{:S(2)}) collective-permute-start(f32[24,1,128]{2,1,0:T(1,128)} %les_ref.1), channel_id=1, source_target_pairs={{16,32},{48,64},{80,96},{112,0},{32,16},{64,48},{96,80},{0,112},{1... | collective-permute-start | bytes 36872 | tf_op jit(solution)/shard_map/ppermute | solution.py:400
  8.9 4.9 %collective-permute-start = (f32[24,1,128]{2,1,0:T(1,128)}, f32[24,1,128]{2,1,0:T(1,128)S(1)}, u32[]{:S(2)}, u32[]{:S(2)}) collective-permute-start(f32[24,1,128]{2,1,0:T(1,128)} %les_ref.1), channel_id=1, source_target_pairs={{0,1},{2,3},{4,5},{6,7},{8,9},{10,11},{12,13},{14,15},{1,0},{3,2},... | collective-permute-start | bytes 36872 | tf_op jit(solution)/shard_map/ppermute | solution.py:400
  9.0 4.9 %collective-permute-start.3 = (f32[24,1,128]{2,1,0:T(1,128)}, f32[24,1,128]{2,1,0:T(1,128)S(1)}, u32[]{:S(2)}, u32[]{:S(2)}) collective-permute-start(f32[24,1,128]{2,1,0:T(1,128)} %les_ref.1), channel_id=1, source_target_pairs={{0,16},{32,48},{64,80},{96,112},{16,0},{48,32},{80,64},{112,96},{1... | collective-permute-start | bytes 36872 | tf_op jit(solution)/shard_map/ppermute | solution.py:400
  10.6 3.3 %copy-start = (f32[24,1,128]{2,1,0:T(1,128)S(1)}, f32[24,1,128]{2,1,0:T(1,128)}, u32[]{:S(2)}) copy-start(f32[24,1,128]{2,1,0:T(1,128)} %les_ref.1) | copy-start | bytes 36868
  10.6 3.3 %copy-start.1 = (s32[2,1,1,128,1]{3,4,2,1,0:T(1,128)S(1)}, s32[2,1,1,128,1]{3,4,2,1,0:T(1,128)}, u32[]{:S(2)}) copy-start(s32[2,1,1,128,1]{3,4,2,1,0:T(1,128)} %param.17) | copy-start | bytes 3076
  10.6 3.3 %copy-start.2 = (s32[2,1,1,128]{3,2,1,0:T(1,128)S(1)}, s32[2,1,1,128]{3,2,1,0:T(1,128)}, u32[]{:S(2)}) copy-start(s32[2,1,1,128]{3,2,1,0:T(1,128)} %line_ref.1) | copy-start | bytes 3076
  10.6 3.3 %copy-start.4 = (s32[2,1,1,128]{3,2,1,0:T(1,128)S(1)}, s32[2,1,1,128]{3,2,1,0:T(1,128)}, u32[]{:S(2)}) copy-start(s32[2,1,1,128]{3,2,1,0:T(1,128)} %from_ref.3) | copy-start | bytes 3076
  10.6 3.3 %copy-start.5 = (s32[2,1,1,128]{3,2,1,0:T(1,128)S(1)}, s32[2,1,1,128]{3,2,1,0:T(1,128)}, u32[]{:S(2)}) copy-start(s32[2,1,1,128]{3,2,1,0:T(1,128)} %to_ref.3) | copy-start | bytes 3076
  10.6 3.3 %copy-start.6 = (s32[1,1,128]{2,1,0:T(1,128)S(1)}, s32[1,1,128]{2,1,0:T(1,128)}, u32[]{:S(2)}) copy-start(s32[1,1,128]{2,1,0:T(1,128)} %counts_ref.1) | copy-start | bytes 1540
  37.2 5.5 %copy-start.3 = (s32[2,1,1,128]{3,2,1,0:T(1,128)S(1)}, s32[2,1,1,128]{3,2,1,0:T(1,128)}, u32[]{:S(2)}) copy-start(s32[2,1,1,128]{3,2,1,0:T(1,128)} %start_ref.1) | copy-start | bytes 3076
  37.2 5.5 %copy-start.7 = (bf16[256,256]{1,0:T(8,128)(2,1)S(1)}, bf16[256,256]{1,0:T(8,128)(2,1)}, u32[]{:S(2)}) copy-start(bf16[256,256]{1,0:T(8,128)(2,1)} %constant.7.clone.second_hbm.second_ref) | copy-start | bytes 393220
  37.2 5.5 %copy-start.8 = (bf16[256,256]{1,0:T(8,128)(2,1)S(1)}, bf16[256,256]{1,0:T(8,128)(2,1)}, u32[]{:S(2)}) copy-start(bf16[256,256]{1,0:T(8,128)(2,1)} %constant.6.clone.first_hbm.first_ref) | copy-start | bytes 393220
  39.5 5.9 %collective-permute-start.7 = (f32[24,1,128]{2,1,0:T(1,128)S(1)}, f32[24,1,128]{2,1,0:T(1,128)S(1)}, u32[]{:S(2)}, u32[]{:S(2)}) collective-permute-start(f32[24,1,128]{2,1,0:T(1,128)S(1)} %get-tuple-element.33.les_ref), channel_id=1, source_target_pairs={{1,2},{3,4},{5,6},{7,8},{9,10},{11,12},{13,14},{15,0},{2,1},{4,3},... | collective-permute-start | bytes 36872 | tf_op jit(solution)/shard_map/ppermute | solution.py:400
  41.3 4.2 %collective-permute-start.6 = (f32[24,1,128]{2,1,0:T(1,128)S(1)}, f32[24,1,128]{2,1,0:T(1,128)S(1)}, u32[]{:S(2)}, u32[]{:S(2)}) collective-permute-start(f32[24,1,128]{2,1,0:T(1,128)S(1)} %get-tuple-element.33.les_ref), channel_id=1, source_target_pairs={{16,32},{48,64},{80,96},{112,0},{32,16},{64,48},{96,80},{0,112},{1... | collective-permute-start | bytes 36872 | tf_op jit(solution)/shard_map/ppermute | solution.py:400
  41.8 3.7 %collective-permute-start.5 = (f32[24,1,128]{2,1,0:T(1,128)S(1)}, f32[24,1,128]{2,1,0:T(1,128)S(1)}, u32[]{:S(2)}, u32[]{:S(2)}) collective-permute-start(f32[24,1,128]{2,1,0:T(1,128)S(1)} %get-tuple-element.33.les_ref), channel_id=1, source_target_pairs={{0,1},{2,3},{4,5},{6,7},{8,9},{10,11},{12,13},{14,15},{1,0},{3,2},... | collective-permute-start | bytes 36872 | tf_op jit(solution)/shard_map/ppermute | solution.py:400
  41.9 3.6 %collective-permute-start.4 = (f32[24,1,128]{2,1,0:T(1,128)S(1)}, f32[24,1,128]{2,1,0:T(1,128)S(1)}, u32[]{:S(2)}, u32[]{:S(2)}) collective-permute-start(f32[24,1,128]{2,1,0:T(1,128)S(1)} %get-tuple-element.33.les_ref), channel_id=1, source_target_pairs={{0,16},{32,48},{64,80},{96,112},{16,0},{48,32},{80,64},{112,96},{1... | collective-permute-start | bytes 36872 | tf_op jit(solution)/shard_map/ppermute | solution.py:400

commit v5 on v4

--- a/solution.py
+++ b/solution.py
@@ -246,7 +246,7 @@
                 write(8 * third + s, at, state_ref[8 * third + s, lines, :] * keep + gained)
         return carry
 
-    lax.fori_loop(0, LINES // 8, block, 0, unroll=2)
+    lax.fori_loop(0, LINES // 8, block, 0, unroll=8)
 
 
 def means_of(read):

time: 73.6 us -> 72.8 us (0.989)
  Pallas kernels: 21.4 us -> 20.6 us
    pallas_call x6, Pallas kernels: 21.4 us -> 20.6 us  [call(): pl.pallas_call(kernel, out_shape=outputs, in_specs=[in_space] * len(input...]
where the time goes in v5:
time: 72.8 us; the launch traced here: 72.6 us
  blocking collectives  36.7 us (50%)
  Pallas kernels  20.6 us (28%)
  starting transfers between devices  13.2 us (18%)
  waiting for transfers between devices  1.12 us (2%)
  between operations  0.94 us (1%)
    all_to_all x2, blocking collectives, exchange(): lax.all_to_all(sending, ('grid', 'line'), split_axis=0, concat_axis=0, ti...  36.7 us
    pallas_call x6, Pallas kernels, call(): pl.pallas_call(kernel, out_shape=outputs, in_specs=[in_space] * len(input...  20.6 us
    ppermute x8, starting transfers between devices, beside(): around.append(lax.ppermute(field, axis, pairs + [(b, a) for a, b in pairs]))  13.2 us
  transfers between devices with their start and end apart: 8, of which 1 were waited for; matrix products, arithmetic and copies ran while one was open for 0% of the time, Pallas kernels for 7%

profile of v5, /device:TPU:1, one launch (start us, length us, event | category | flops | bytes accessed | tf_op | source)
XLA Modules:
  0.0 72.6 jit_solution(8442777289051083376)
XLA Ops:
  0.6 5.8 %collective-permute-start.2 = (f32[24,1,128]{2,1,0:T(1,128)}, f32[24,1,128]{2,1,0:T(1,128)S(1)}, u32[]{:S(2)}, u32[]{:S(2)}) collective-permute-start(f32[24,1,128]{2,1,0:T(1,128)} %les_ref.1), channel_id=1, source_target_pairs={{1,2},{3,4},{5,6},{7,8},{9,10},{11,12},{13,14},{15,0},{2,1},{4,3},... | collective-permute-start | bytes 36872 | tf_op jit(solution)/shard_map/ppermute | solution.py:400
  6.5 2.5 %collective-permute-start.1 = (f32[24,1,128]{2,1,0:T(1,128)}, f32[24,1,128]{2,1,0:T(1,128)S(1)}, u32[]{:S(2)}, u32[]{:S(2)}) collective-permute-start(f32[24,1,128]{2,1,0:T(1,128)} %les_ref.1), channel_id=1, source_target_pairs={{16,32},{48,64},{80,96},{112,0},{32,16},{64,48},{96,80},{0,112},{1... | collective-permute-start | bytes 36872 | tf_op jit(solution)/shard_map/ppermute | solution.py:400
  8.9 0.0 collective-permute-start
  9.0 1.7 %collective-permute-start.3 = (f32[24,1,128]{2,1,0:T(1,128)}, f32[24,1,128]{2,1,0:T(1,128)S(1)}, u32[]{:S(2)}, u32[]{:S(2)}) collective-permute-start(f32[24,1,128]{2,1,0:T(1,128)} %les_ref.1), channel_id=1, source_target_pairs={{0,16},{32,48},{64,80},{96,112},{16,0},{48,32},{80,64},{112,96},{1... | collective-permute-start | bytes 36872 | tf_op jit(solution)/shard_map/ppermute | solution.py:400
  10.6 0.0 copy-start.5
  10.6 0.0 copy-start.6
  10.7 3.2 %shard_map.149 = (f32[24,128,128]{2,1,0:T(8,128)S(1)}, bf16[192,192]{1,0:T(8,128)(2,1)S(1)}, bf16[192,192]{1,0:T(8,128)(2,1)S(1)}, f32[24,128]{1,0:T(8,128)S(1)}) custom-call(f32[128,24,128]{2,1,0:T(8,128)} %bitcast.13, s32[2,1,1,128]{3,2,1,0:T(1,128)} %start_ref.1, f32[1,24]{1,0:T(1,128)} %bitcast.14, f32[1,128]{1,0:T(1,128)} %constant.8.clone.eigen_hbm, ...), custom_call_target="tpu_custom_call" | custom-call | flops 4000000000 | bytes 3573856 | tf_op jit(solution)/shard_map/pallas_call | solution.py:383
  13.9 0.0 collective-permute-done.2.line_odd_ref
  13.9 0.0 collective-permute-done.1.grid_odd_ref
  13.9 0.0 collective-permute-done.line_even_ref
  13.9 0.0 collective-permute-done.3.grid_even_ref
  13.9 0.0 copy-done
  13.9 0.0 copy-done.1
  13.9 0.0 copy-done.2
  13.9 0.0 copy-done.4
  13.9 0.0 copy-done.5
  14.0 5.7 %shard_map.150 = (f32[24,128,128]{2,1,0:T(8,128)S(1)}, f32[896,128]{1,0:T(8,128)S(1)}, f32[24,128]{1,0:T(8,128)S(1)}, f32[128,128]{1,0:T(8,128)S(1)}, bf16[2,128,256]{2,1,0:T(8,128)(2,1)S(1)}) custom-call(f32[24,128,128]{2,1,0:T(8,128)S(1)} %get-tuple-element.23.mixed_ref, f32[24,1,128]{2,1,0:T(1,128)S(1)} %copy-done, ...), custom_call_target="tpu_custom_call" | custom-call | flops 6000000000 | bytes 4026880 | tf_op jit(solution)/shard_map/pallas_call | solution.py:383
  19.6 17.6 %all_to_all.10 = f32[128,1,896]{2,1,0:T(1,128)S(1)} all-to-all(f32[128,1,896]{2,1,0:T(1,128)S(1)} %bitcast.8), channel_id=1, replica_groups=mesh['grid'=8,'line'=16] {'grid','line'}, dimensions={0} | all-to-all | bytes 917504 | tf_op jit(solution)/shard_map/all_to_all | solution.py:433
  37.2 1.9 %shard_map.151 = (f32[24,1,128]{2,1,0:T(1,128)S(1)}, f32[24,128,128]{2,1,0:T(8,128)S(1)}, f32[8,128]{1,0:T(8,128)S(1)}) custom-call(f32[896,128]{1,0:T(8,128)S(1)} %bitcast.9, f32[24,128,128]{2,1,0:T(8,128)S(1)} %get-tuple-element.27.state_ref, f32[24,128]{1,0:T(8,128)S(1)} %get-tuple-element.28.mid_ref), custom_call_target="tpu_custom_call" | custom-call | flops 3000000000 | bytes 3633152 | tf_op jit(solution)/shard_map/pallas_call | solution.py:383
  39.1 1.8 %collective-permute-start.7 = (f32[24,1,128]{2,1,0:T(1,128)S(1)}, f32[24,1,128]{2,1,0:T(1,128)S(1)}, u32[]{:S(2)}, u32[]{:S(2)}) collective-permute-start(f32[24,1,128]{2,1,0:T(1,128)S(1)} %get-tuple-element.33.les_ref), channel_id=1, source_target_pairs={{1,2},{3,4},{5,6},{7,8},{9,10},{11,12},{13,14},{15,0},{2,1},{4,3},... | collective-permute-start | bytes 36872 | tf_op jit(solution)/shard_map/ppermute | solution.py:400
  40.9 0.5 collective-permute-start.6
  41.4 0.1 collective-permute-start.5
  41.4 0.9 %collective-permute-start.4 = (f32[24,1,128]{2,1,0:T(1,128)S(1)}, f32[24,1,128]{2,1,0:T(1,128)S(1)}, u32[]{:S(2)}, u32[]{:S(2)}) collective-permute-start(f32[24,1,128]{2,1,0:T(1,128)S(1)} %get-tuple-element.33.les_ref), channel_id=1, source_target_pairs={{0,16},{32,48},{64,80},{96,112},{16,0},{48,32},{80,64},{112,96},{1... | collective-permute-start | bytes 36872 | tf_op jit(solution)/shard_map/ppermute | solution.py:400
  42.3 0.0 copy-done.7
  42.3 1.6 %shard_map.152 = (f32[24,128,128]{2,1,0:T(8,128)S(1)}, s32[128,128]{1,0:T(8,128)S(1)}, s32[128,128]{1,0:T(8,128)S(1)}, bf16[1024,512]{1,0:T(8,128)(2,1)S(1)}) custom-call(f32[24,128,128]{2,1,0:T(8,128)S(1)} %get-tuple-element.29.state_ref, s32[2,1,1,128]{3,2,1,0:T(1,128)S(1)} %copy-done.3, f32[24,128]{1,0:T(8,128)S(1)} %get-tuple-element.30.scale_ref, ...), custom_call_target="tpu_custom_call" | custom-call | flops 3000000000 | bytes 4606976 | tf_op jit(solution)/shard_map/pallas_call | solution.py:383
  44.0 1.1 %collective-permute-done.7.line_odd_ref = f32[24,1,128]{2,1,0:T(1,128)S(1)} collective-permute-done((f32[24,1,128]{2,1,0:T(1,128)S(1)}, f32[24,1,128]{2,1,0:T(1,128)S(1)}, u32[]{:S(2)}, u32[]{:S(2)}) %collective-permute-start.7) | collective-permute-done | bytes 12320 | tf_op jit(solution)/shard_map/ppermute | solution.py:400
  45.1 0.0 collective-permute-done.6.grid_odd_ref
  45.1 0.0 collective-permute-done.5.line_even_ref
  45.1 0.0 collective-permute-done.4.grid_even_ref
  45.1 5.5 %shard_map.153 = (f32[24,128,128]{2,1,0:T(8,128)S(1)}, f32[768,128]{1,0:T(8,128)S(1)}, f32[24,128]{1,0:T(8,128)S(1)}) custom-call(f32[24,128,128]{2,1,0:T(8,128)S(1)} %get-tuple-element.32.mixed_ref, f32[24,1,128]{2,1,0:T(1,128)S(1)} %get-tuple-element.33.les_ref, f32[24,1,128]{2,1,0:T(1,128)S(1)} %collective-permute-done.4.grid_even_ref, ...), custom_call_target="tpu_custom_call" | custom-call | flops 6000000000 | bytes 4087808 | tf_op jit(solution)/shard_map/pallas_call | solution.py:383
  50.6 19.1 %all_to_all.11 = f32[128,1,768]{2,1,0:T(1,128)S(1)} all-to-all(f32[128,1,768]{2,1,0:T(1,128)S(1)} %bitcast.10), channel_id=1, replica_groups=mesh['grid'=8,'line'=16] {'grid','line'}, dimensions={0} | all-to-all | bytes 786432 | tf_op jit(solution)/shard_map/all_to_all | solution.py:433
  69.7 2.8 %shard_map.154 = (f32[24,1,128]{2,1,0:T(1,128)}, f32[3072,128]{1,0:T(8,128)}) custom-call(f32[768,128]{1,0:T(8,128)S(1)} %bitcast.11, f32[24,128,128]{2,1,0:T(8,128)S(1)} %get-tuple-element.39.state_ref, f32[24,128]{1,0:T(8,128)S(1)} %get-tuple-element.40.mid_ref, bf16[1024,512]{1,0:T(8,128)(2,1)S(1)} %get-tuple-element.41.hits_ref), custom_call_target="tpu_custom_call" | custom-call | flops 3000000000 | bytes 4612096 | tf_op jit(solution)/shard_map/pallas_call | solution.py:383
  (10 shorter events, 0.0 us)
Async XLA Ops:
  0.6 13.2 %collective-permute-start.2 = (f32[24,1,128]{2,1,0:T(1,128)}, f32[24,1,128]{2,1,0:T(1,128)S(1)}, u32[]{:S(2)}, u32[]{:S(2)}) collective-permute-start(f32[24,1,128]{2,1,0:T(1,128)} %les_ref.1), channel_id=1, source_target_pairs={{1,2},{3,4},{5,6},{7,8},{9,10},{11,12},{13,14},{15,0},{2,1},{4,3},... | collective-permute-start | bytes 36872 | tf_op jit(solution)/shard_map/ppermute | solution.py:400
  6.5 7.4 %collective-permute-start.1 = (f32[24,1,128]{2,1,0:T(1,128)}, f32[24,1,128]{2,1,0:T(1,128)S(1)}, u32[]{:S(2)}, u32[]{:S(2)}) collective-permute-start(f32[24,1,128]{2,1,0:T(1,128)} %les_ref.1), channel_id=1, source_target_pairs={{16,32},{48,64},{80,96},{112,0},{32,16},{64,48},{96,80},{0,112},{1... | collective-permute-start | bytes 36872 | tf_op jit(solution)/shard_map/ppermute | solution.py:400
  8.9 4.9 %collective-permute-start = (f32[24,1,128]{2,1,0:T(1,128)}, f32[24,1,128]{2,1,0:T(1,128)S(1)}, u32[]{:S(2)}, u32[]{:S(2)}) collective-permute-start(f32[24,1,128]{2,1,0:T(1,128)} %les_ref.1), channel_id=1, source_target_pairs={{0,1},{2,3},{4,5},{6,7},{8,9},{10,11},{12,13},{14,15},{1,0},{3,2},... | collective-permute-start | bytes 36872 | tf_op jit(solution)/shard_map/ppermute | solution.py:400
  9.0 4.9 %collective-permute-start.3 = (f32[24,1,128]{2,1,0:T(1,128)}, f32[24,1,128]{2,1,0:T(1,128)S(1)}, u32[]{:S(2)}, u32[]{:S(2)}) collective-permute-start(f32[24,1,128]{2,1,0:T(1,128)} %les_ref.1), channel_id=1, source_target_pairs={{0,16},{32,48},{64,80},{96,112},{16,0},{48,32},{80,64},{112,96},{1... | collective-permute-start | bytes 36872 | tf_op jit(solution)/shard_map/ppermute | solution.py:400
  10.6 3.3 %copy-start = (f32[24,1,128]{2,1,0:T(1,128)S(1)}, f32[24,1,128]{2,1,0:T(1,128)}, u32[]{:S(2)}) copy-start(f32[24,1,128]{2,1,0:T(1,128)} %les_ref.1) | copy-start | bytes 36868
  10.6 3.3 %copy-start.1 = (s32[2,1,1,128,1]{3,4,2,1,0:T(1,128)S(1)}, s32[2,1,1,128,1]{3,4,2,1,0:T(1,128)}, u32[]{:S(2)}) copy-start(s32[2,1,1,128,1]{3,4,2,1,0:T(1,128)} %param.17) | copy-start | bytes 3076
  10.6 3.3 %copy-start.2 = (s32[2,1,1,128]{3,2,1,0:T(1,128)S(1)}, s32[2,1,1,128]{3,2,1,0:T(1,128)}, u32[]{:S(2)}) copy-start(s32[2,1,1,128]{3,2,1,0:T(1,128)} %line_ref.1) | copy-start | bytes 3076
  10.6 3.3 %copy-start.4 = (s32[2,1,1,128]{3,2,1,0:T(1,128)S(1)}, s32[2,1,1,128]{3,2,1,0:T(1,128)}, u32[]{:S(2)}) copy-start(s32[2,1,1,128]{3,2,1,0:T(1,128)} %from_ref.3) | copy-start | bytes 3076
  10.6 3.3 %copy-start.5 = (s32[2,1,1,128]{3,2,1,0:T(1,128)S(1)}, s32[2,1,1,128]{3,2,1,0:T(1,128)}, u32[]{:S(2)}) copy-start(s32[2,1,1,128]{3,2,1,0:T(1,128)} %to_ref.3) | copy-start | bytes 3076
  10.6 3.3 %copy-start.6 = (s32[1,1,128]{2,1,0:T(1,128)S(1)}, s32[1,1,128]{2,1,0:T(1,128)}, u32[]{:S(2)}) copy-start(s32[1,1,128]{2,1,0:T(1,128)} %counts_ref.1) | copy-start | bytes 1540
  37.2 5.1 %copy-start.3 = (s32[2,1,1,128]{3,2,1,0:T(1,128)S(1)}, s32[2,1,1,128]{3,2,1,0:T(1,128)}, u32[]{:S(2)}) copy-start(s32[2,1,1,128]{3,2,1,0:T(1,128)} %start_ref.1) | copy-start | bytes 3076
  37.2 5.1 %copy-start.7 = (bf16[256,256]{1,0:T(8,128)(2,1)S(1)}, bf16[256,256]{1,0:T(8,128)(2,1)}, u32[]{:S(2)}) copy-start(bf16[256,256]{1,0:T(8,128)(2,1)} %constant.7.clone.second_hbm.second_ref) | copy-start | bytes 393220
  37.2 5.1 %copy-start.8 = (bf16[256,256]{1,0:T(8,128)(2,1)S(1)}, bf16[256,256]{1,0:T(8,128)(2,1)}, u32[]{:S(2)}) copy-start(bf16[256,256]{1,0:T(8,128)(2,1)} %constant.6.clone.first_hbm.first_ref) | copy-start | bytes 393220
  39.1 5.9 %collective-permute-start.7 = (f32[24,1,128]{2,1,0:T(1,128)S(1)}, f32[24,1,128]{2,1,0:T(1,128)S(1)}, u32[]{:S(2)}, u32[]{:S(2)}) collective-permute-start(f32[24,1,128]{2,1,0:T(1,128)S(1)} %get-tuple-element.33.les_ref), channel_id=1, source_target_pairs={{1,2},{3,4},{5,6},{7,8},{9,10},{11,12},{13,14},{15,0},{2,1},{4,3},... | collective-permute-start | bytes 36872 | tf_op jit(solution)/shard_map/ppermute | solution.py:400
  40.9 4.2 %collective-permute-start.6 = (f32[24,1,128]{2,1,0:T(1,128)S(1)}, f32[24,1,128]{2,1,0:T(1,128)S(1)}, u32[]{:S(2)}, u32[]{:S(2)}) collective-permute-start(f32[24,1,128]{2,1,0:T(1,128)S(1)} %get-tuple-element.33.les_ref), channel_id=1, source_target_pairs={{16,32},{48,64},{80,96},{112,0},{32,16},{64,48},{96,80},{0,112},{1... | collective-permute-start | bytes 36872 | tf_op jit(solution)/shard_map/ppermute | solution.py:400
  41.4 3.7 %collective-permute-start.5 = (f32[24,1,128]{2,1,0:T(1,128)S(1)}, f32[24,1,128]{2,1,0:T(1,128)S(1)}, u32[]{:S(2)}, u32[]{:S(2)}) collective-permute-start(f32[24,1,128]{2,1,0:T(1,128)S(1)} %get-tuple-element.33.les_ref), channel_id=1, source_target_pairs={{0,1},{2,3},{4,5},{6,7},{8,9},{10,11},{12,13},{14,15},{1,0},{3,2},... | collective-permute-start | bytes 36872 | tf_op jit(solution)/shard_map/ppermute | solution.py:400
  41.4 3.6 %collective-permute-start.4 = (f32[24,1,128]{2,1,0:T(1,128)S(1)}, f32[24,1,128]{2,1,0:T(1,128)S(1)}, u32[]{:S(2)}, u32[]{:S(2)}) collective-permute-start(f32[24,1,128]{2,1,0:T(1,128)S(1)} %get-tuple-element.33.les_ref), channel_id=1, source_target_pairs={{0,16},{32,48},{64,80},{96,112},{16,0},{48,32},{80,64},{112,96},{1... | collective-permute-start | bytes 36872 | tf_op jit(solution)/shard_map/ppermute | solution.py:400

commit v6 on v5

--- a/solution.py
+++ b/solution.py
@@ -328,7 +328,7 @@
 
 
 def next_react_kernel(
-    mixed_ref, les_ref, grid_even_ref, line_even_ref, grid_odd_ref, line_odd_ref, high_ref, low_ref, pick_ref, group_ref,
+    mixed_ref, les_ref, grid_odd_ref, line_odd_ref, grid_even_ref, line_even_ref, high_ref, low_ref, pick_ref, group_ref,
     turns_ref, placing_ref, state_ref, send_ref, mid_ref, out_ref,
 ):
     rim = (grid_even_ref, grid_odd_ref, line_even_ref, line_odd_ref)
@@ -456,7 +456,7 @@
         next_mix_kernel, inputs, [STATE, index, index, hits], [scratch_of(index)], 3
     )
 
-    inputs = [mixed, field, grid_even, line_even, grid_odd, line_odd, high, low, pick, group, turns, later]
+    inputs = [mixed, field, grid_odd, line_odd, grid_even, line_even, high, low, pick, group, turns, later]
     outputs = [STATE, shaped((OWNERS * ROWS, POINTS)), plane]
     state, sending, mid = call(next_react_kernel, inputs, outputs, [outgoing], 6)
 

time: 72.8 us -> 72.3 us (level)
  blocking collectives: 36.7 us -> 34.2 us
  waiting for transfers between devices: 1.12 us -> 2.56 us
    all_to_all x2, blocking collectives: 36.7 us -> 34.2 us  [exchange(): lax.all_to_all(sending, ('grid', 'line'), split_axis=0, concat_axis=0, ti...]
    ppermute x8, waiting for transfers between devices: 1.12 us -> 2.56 us  [beside(): around.append(lax.ppermute(field, axis, pairs + [(b, a) for a, b in pairs]))]
where the time goes in v6:
time: 72.3 us; the launch traced here: 72.2 us
  blocking collectives  34.2 us (47%)
  Pallas kernels  20.6 us (28%)
  starting transfers between devices  13.7 us (19%)
  waiting for transfers between devices  2.56 us (4%)
  between operations  0.95 us (1%)
    all_to_all x2, blocking collectives, exchange(): lax.all_to_all(sending, ('grid', 'line'), split_axis=0, concat_axis=0, ti...  34.2 us
    pallas_call x6, Pallas kernels, call(): pl.pallas_call(kernel, out_shape=outputs, in_specs=[in_space] * len(input...  20.6 us
    ppermute x8, starting transfers between devices, beside(): around.append(lax.ppermute(field, axis, pairs + [(b, a) for a, b in pairs]))  13.7 us
    ppermute x8, waiting for transfers between devices, beside(): around.append(lax.ppermute(field, axis, pairs + [(b, a) for a, b in pairs]))  2.56 us
  transfers between devices with their start and end apart: 8, of which 1 were waited for; matrix products, arithmetic and copies ran while one was open for 0% of the time, Pallas kernels for 7%

profile of v6, /device:TPU:1, one launch (start us, length us, event | category | flops | bytes accessed | tf_op | source)
XLA Modules:
  0.0 72.2 jit_solution(8792221533242470224)
XLA Ops:
  0.6 5.8 %collective-permute-start.2 = (f32[24,1,128]{2,1,0:T(1,128)}, f32[24,1,128]{2,1,0:T(1,128)S(1)}, u32[]{:S(2)}, u32[]{:S(2)}) collective-permute-start(f32[24,1,128]{2,1,0:T(1,128)} %les_ref.1), channel_id=1, source_target_pairs={{1,2},{3,4},{5,6},{7,8},{9,10},{11,12},{13,14},{15,0},{2,1},{4,3},... | collective-permute-start | bytes 36872 | tf_op jit(solution)/shard_map/ppermute | solution.py:400
  6.5 2.5 %collective-permute-start.1 = (f32[24,1,128]{2,1,0:T(1,128)}, f32[24,1,128]{2,1,0:T(1,128)S(1)}, u32[]{:S(2)}, u32[]{:S(2)}) collective-permute-start(f32[24,1,128]{2,1,0:T(1,128)} %les_ref.1), channel_id=1, source_target_pairs={{16,32},{48,64},{80,96},{112,0},{32,16},{64,48},{96,80},{0,112},{1... | collective-permute-start | bytes 36872 | tf_op jit(solution)/shard_map/ppermute | solution.py:400
  8.9 0.0 collective-permute-start
  9.0 1.7 %collective-permute-start.3 = (f32[24,1,128]{2,1,0:T(1,128)}, f32[24,1,128]{2,1,0:T(1,128)S(1)}, u32[]{:S(2)}, u32[]{:S(2)}) collective-permute-start(f32[24,1,128]{2,1,0:T(1,128)} %les_ref.1), channel_id=1, source_target_pairs={{0,16},{32,48},{64,80},{96,112},{16,0},{48,32},{80,64},{112,96},{1... | collective-permute-start | bytes 36872 | tf_op jit(solution)/shard_map/ppermute | solution.py:400
  10.6 0.0 copy-start.5
  10.6 0.0 copy-start.6
  10.7 3.2 %shard_map.149 = (f32[24,128,128]{2,1,0:T(8,128)S(1)}, bf16[192,192]{1,0:T(8,128)(2,1)S(1)}, bf16[192,192]{1,0:T(8,128)(2,1)S(1)}, f32[24,128]{1,0:T(8,128)S(1)}) custom-call(f32[128,24,128]{2,1,0:T(8,128)} %bitcast.13, s32[2,1,1,128]{3,2,1,0:T(1,128)} %start_ref.1, f32[1,24]{1,0:T(1,128)} %bitcast.14, f32[1,128]{1,0:T(1,128)} %constant.8.clone.eigen_hbm, ...), custom_call_target="tpu_custom_call" | custom-call | flops 4000000000 | bytes 3573856 | tf_op jit(solution)/shard_map/pallas_call | solution.py:383
  13.9 0.0 collective-permute-done.2.line_odd_ref
  13.9 0.0 collective-permute-done.1.grid_odd_ref
  13.9 0.0 collective-permute-done.line_even_ref
  13.9 0.0 collective-permute-done.3.grid_even_ref
  13.9 0.0 copy-done
  13.9 0.0 copy-done.1
  13.9 0.0 copy-done.2
  13.9 0.0 copy-done.4
  13.9 0.0 copy-done.5
  14.0 0.0 copy-done.6
  14.0 5.7 %shard_map.150 = (f32[24,128,128]{2,1,0:T(8,128)S(1)}, f32[896,128]{1,0:T(8,128)S(1)}, f32[24,128]{1,0:T(8,128)S(1)}, f32[128,128]{1,0:T(8,128)S(1)}, bf16[2,128,256]{2,1,0:T(8,128)(2,1)S(1)}) custom-call(f32[24,128,128]{2,1,0:T(8,128)S(1)} %get-tuple-element.23.mixed_ref, f32[24,1,128]{2,1,0:T(1,128)S(1)} %copy-done, ...), custom_call_target="tpu_custom_call" | custom-call | flops 6000000000 | bytes 4026880 | tf_op jit(solution)/shard_map/pallas_call | solution.py:383
  19.6 17.6 %all_to_all.10 = f32[128,1,896]{2,1,0:T(1,128)S(1)} all-to-all(f32[128,1,896]{2,1,0:T(1,128)S(1)} %bitcast.8), channel_id=1, replica_groups=mesh['grid'=8,'line'=16] {'grid','line'}, dimensions={0} | all-to-all | bytes 917504 | tf_op jit(solution)/shard_map/all_to_all | solution.py:433
  37.2 1.9 %shard_map.151 = (f32[24,1,128]{2,1,0:T(1,128)S(1)}, f32[24,128,128]{2,1,0:T(8,128)S(1)}, f32[8,128]{1,0:T(8,128)S(1)}) custom-call(f32[896,128]{1,0:T(8,128)S(1)} %bitcast.9, f32[24,128,128]{2,1,0:T(8,128)S(1)} %get-tuple-element.27.state_ref, f32[24,128]{1,0:T(8,128)S(1)} %get-tuple-element.28.mid_ref), custom_call_target="tpu_custom_call" | custom-call | flops 3000000000 | bytes 3633152 | tf_op jit(solution)/shard_map/pallas_call | solution.py:383
  39.1 0.5 collective-permute-start.7
  39.6 1.6 %collective-permute-start.6 = (f32[24,1,128]{2,1,0:T(1,128)S(1)}, f32[24,1,128]{2,1,0:T(1,128)S(1)}, u32[]{:S(2)}, u32[]{:S(2)}) collective-permute-start(f32[24,1,128]{2,1,0:T(1,128)S(1)} %get-tuple-element.33.les_ref), channel_id=1, source_target_pairs={{0,16},{32,48},{64,80},{96,112},{16,0},{48,32},{80,64},{112,96},{1... | collective-permute-start | bytes 36872 | tf_op jit(solution)/shard_map/ppermute | solution.py:400
  41.2 1.0 %collective-permute-start.5 = (f32[24,1,128]{2,1,0:T(1,128)S(1)}, f32[24,1,128]{2,1,0:T(1,128)S(1)}, u32[]{:S(2)}, u32[]{:S(2)}) collective-permute-start(f32[24,1,128]{2,1,0:T(1,128)S(1)} %get-tuple-element.33.les_ref), channel_id=1, source_target_pairs={{1,2},{3,4},{5,6},{7,8},{9,10},{11,12},{13,14},{15,0},{2,1},{4,3},... | collective-permute-start | bytes 36872 | tf_op jit(solution)/shard_map/ppermute | solution.py:400
  42.2 0.7 collective-permute-start.4
  42.9 1.6 %shard_map.152 = (f32[24,128,128]{2,1,0:T(8,128)S(1)}, s32[128,128]{1,0:T(8,128)S(1)}, s32[128,128]{1,0:T(8,128)S(1)}, bf16[1024,512]{1,0:T(8,128)(2,1)S(1)}) custom-call(f32[24,128,128]{2,1,0:T(8,128)S(1)} %get-tuple-element.29.state_ref, s32[2,1,1,128]{3,2,1,0:T(1,128)S(1)} %copy-done.3, f32[24,128]{1,0:T(8,128)S(1)} %get-tuple-element.30.scale_ref, ...), custom_call_target="tpu_custom_call" | custom-call | flops 3000000000 | bytes 4606976 | tf_op jit(solution)/shard_map/pallas_call | solution.py:383
  44.5 0.0 collective-permute-done.7.line_even_ref
  44.5 0.0 collective-permute-done.6.grid_even_ref
  44.5 2.5 %collective-permute-done.5.line_odd_ref = f32[24,1,128]{2,1,0:T(1,128)S(1)} collective-permute-done((f32[24,1,128]{2,1,0:T(1,128)S(1)}, f32[24,1,128]{2,1,0:T(1,128)S(1)}, u32[]{:S(2)}, u32[]{:S(2)}) %collective-permute-start.5) | collective-permute-done | bytes 12320 | tf_op jit(solution)/shard_map/ppermute | solution.py:400
  47.0 0.0 collective-permute-done.4.grid_odd_ref
  47.1 5.5 %shard_map.153 = (f32[24,128,128]{2,1,0:T(8,128)S(1)}, f32[768,128]{1,0:T(8,128)S(1)}, f32[24,128]{1,0:T(8,128)S(1)}) custom-call(f32[24,128,128]{2,1,0:T(8,128)S(1)} %get-tuple-element.32.mixed_ref, f32[24,1,128]{2,1,0:T(1,128)S(1)} %get-tuple-element.33.les_ref, f32[24,1,128]{2,1,0:T(1,128)S(1)} %collective-permute-done.4.grid_odd_ref, ...), custom_call_target="tpu_custom_call" | custom-call | flops 6000000000 | bytes 4087808 | tf_op jit(solution)/shard_map/pallas_call | solution.py:383
  52.5 16.7 %all_to_all.11 = f32[128,1,768]{2,1,0:T(1,128)S(1)} all-to-all(f32[128,1,768]{2,1,0:T(1,128)S(1)} %bitcast.10), channel_id=1, replica_groups=mesh['grid'=8,'line'=16] {'grid','line'}, dimensions={0} | all-to-all | bytes 786432 | tf_op jit(solution)/shard_map/all_to_all | solution.py:433
  69.2 2.8 %shard_map.154 = (f32[24,1,128]{2,1,0:T(1,128)}, f32[3072,128]{1,0:T(8,128)}) custom-call(f32[768,128]{1,0:T(8,128)S(1)} %bitcast.11, f32[24,128,128]{2,1,0:T(8,128)S(1)} %get-tuple-element.39.state_ref, f32[24,128]{1,0:T(8,128)S(1)} %get-tuple-element.40.mid_ref, bf16[1024,512]{1,0:T(8,128)(2,1)S(1)} %get-tuple-element.41.hits_ref), custom_call_target="tpu_custom_call" | custom-call | flops 3000000000 | bytes 4612096 | tf_op jit(solution)/shard_map/pallas_call | solution.py:383
  (10 shorter events, 0.0 us)
Async XLA Ops:
  0.6 13.2 %collective-permute-start.2 = (f32[24,1,128]{2,1,0:T(1,128)}, f32[24,1,128]{2,1,0:T(1,128)S(1)}, u32[]{:S(2)}, u32[]{:S(2)}) collective-permute-start(f32[24,1,128]{2,1,0:T(1,128)} %les_ref.1), channel_id=1, source_target_pairs={{1,2},{3,4},{5,6},{7,8},{9,10},{11,12},{13,14},{15,0},{2,1},{4,3},... | collective-permute-start | bytes 36872 | tf_op jit(solution)/shard_map/ppermute | solution.py:400
  6.5 7.4 %collective-permute-start.1 = (f32[24,1,128]{2,1,0:T(1,128)}, f32[24,1,128]{2,1,0:T(1,128)S(1)}, u32[]{:S(2)}, u32[]{:S(2)}) collective-permute-start(f32[24,1,128]{2,1,0:T(1,128)} %les_ref.1), channel_id=1, source_target_pairs={{16,32},{48,64},{80,96},{112,0},{32,16},{64,48},{96,80},{0,112},{1... | collective-permute-start | bytes 36872 | tf_op jit(solution)/shard_map/ppermute | solution.py:400
  8.9 4.9 %collective-permute-start = (f32[24,1,128]{2,1,0:T(1,128)}, f32[24,1,128]{2,1,0:T(1,128)S(1)}, u32[]{:S(2)}, u32[]{:S(2)}) collective-permute-start(f32[24,1,128]{2,1,0:T(1,128)} %les_ref.1), channel_id=1, source_target_pairs={{0,1},{2,3},{4,5},{6,7},{8,9},{10,11},{12,13},{14,15},{1,0},{3,2},... | collective-permute-start | bytes 36872 | tf_op jit(solution)/shard_map/ppermute | solution.py:400
  9.0 4.9 %collective-permute-start.3 = (f32[24,1,128]{2,1,0:T(1,128)}, f32[24,1,128]{2,1,0:T(1,128)S(1)}, u32[]{:S(2)}, u32[]{:S(2)}) collective-permute-start(f32[24,1,128]{2,1,0:T(1,128)} %les_ref.1), channel_id=1, source_target_pairs={{0,16},{32,48},{64,80},{96,112},{16,0},{48,32},{80,64},{112,96},{1... | collective-permute-start | bytes 36872 | tf_op jit(solution)/shard_map/ppermute | solution.py:400
  10.6 3.3 %copy-start = (f32[24,1,128]{2,1,0:T(1,128)S(1)}, f32[24,1,128]{2,1,0:T(1,128)}, u32[]{:S(2)}) copy-start(f32[24,1,128]{2,1,0:T(1,128)} %les_ref.1) | copy-start | bytes 36868
  10.6 3.3 %copy-start.1 = (s32[2,1,1,128,1]{3,4,2,1,0:T(1,128)S(1)}, s32[2,1,1,128,1]{3,4,2,1,0:T(1,128)}, u32[]{:S(2)}) copy-start(s32[2,1,1,128,1]{3,4,2,1,0:T(1,128)} %param.17) | copy-start | bytes 3076
  10.6 3.3 %copy-start.2 = (s32[2,1,1,128]{3,2,1,0:T(1,128)S(1)}, s32[2,1,1,128]{3,2,1,0:T(1,128)}, u32[]{:S(2)}) copy-start(s32[2,1,1,128]{3,2,1,0:T(1,128)} %line_ref.1) | copy-start | bytes 3076
  10.6 3.3 %copy-start.4 = (s32[2,1,1,128]{3,2,1,0:T(1,128)S(1)}, s32[2,1,1,128]{3,2,1,0:T(1,128)}, u32[]{:S(2)}) copy-start(s32[2,1,1,128]{3,2,1,0:T(1,128)} %from_ref.3) | copy-start | bytes 3076
  10.6 3.3 %copy-start.5 = (s32[2,1,1,128]{3,2,1,0:T(1,128)S(1)}, s32[2,1,1,128]{3,2,1,0:T(1,128)}, u32[]{:S(2)}) copy-start(s32[2,1,1,128]{3,2,1,0:T(1,128)} %to_ref.3) | copy-start | bytes 3076
  10.6 3.3 %copy-start.6 = (s32[1,1,128]{2,1,0:T(1,128)S(1)}, s32[1,1,128]{2,1,0:T(1,128)}, u32[]{:S(2)}) copy-start(s32[1,1,128]{2,1,0:T(1,128)} %counts_ref.1) | copy-start | bytes 1540
  37.2 5.6 %copy-start.3 = (s32[2,1,1,128]{3,2,1,0:T(1,128)S(1)}, s32[2,1,1,128]{3,2,1,0:T(1,128)}, u32[]{:S(2)}) copy-start(s32[2,1,1,128]{3,2,1,0:T(1,128)} %start_ref.1) | copy-start | bytes 3076
  37.2 5.6 %copy-start.7 = (bf16[256,256]{1,0:T(8,128)(2,1)S(1)}, bf16[256,256]{1,0:T(8,128)(2,1)}, u32[]{:S(2)}) copy-start(bf16[256,256]{1,0:T(8,128)(2,1)} %constant.7.clone.second_hbm.second_ref) | copy-start | bytes 393220
  37.2 5.6 %copy-start.8 = (bf16[256,256]{1,0:T(8,128)(2,1)S(1)}, bf16[256,256]{1,0:T(8,128)(2,1)}, u32[]{:S(2)}) copy-start(bf16[256,256]{1,0:T(8,128)(2,1)} %constant.6.clone.first_hbm.first_ref) | copy-start | bytes 393220
  39.1 5.4 %collective-permute-start.7 = (f32[24,1,128]{2,1,0:T(1,128)S(1)}, f32[24,1,128]{2,1,0:T(1,128)S(1)}, u32[]{:S(2)}, u32[]{:S(2)}) collective-permute-start(f32[24,1,128]{2,1,0:T(1,128)S(1)} %get-tuple-element.33.les_ref), channel_id=1, source_target_pairs={{0,1},{2,3},{4,5},{6,7},{8,9},{10,11},{12,13},{14,15},{1,0},{3,2},... | collective-permute-start | bytes 36872 | tf_op jit(solution)/shard_map/ppermute | solution.py:400
  39.6 4.9 %collective-permute-start.6 = (f32[24,1,128]{2,1,0:T(1,128)S(1)}, f32[24,1,128]{2,1,0:T(1,128)S(1)}, u32[]{:S(2)}, u32[]{:S(2)}) collective-permute-start(f32[24,1,128]{2,1,0:T(1,128)S(1)} %get-tuple-element.33.les_ref), channel_id=1, source_target_pairs={{0,16},{32,48},{64,80},{96,112},{16,0},{48,32},{80,64},{112,96},{1... | collective-permute-start | bytes 36872 | tf_op jit(solution)/shard_map/ppermute | solution.py:400
  41.2 5.9 %collective-permute-start.5 = (f32[24,1,128]{2,1,0:T(1,128)S(1)}, f32[24,1,128]{2,1,0:T(1,128)S(1)}, u32[]{:S(2)}, u32[]{:S(2)}) collective-permute-start(f32[24,1,128]{2,1,0:T(1,128)S(1)} %get-tuple-element.33.les_ref), channel_id=1, source_target_pairs={{1,2},{3,4},{5,6},{7,8},{9,10},{11,12},{13,14},{15,0},{2,1},{4,3},... | collective-permute-start | bytes 36872 | tf_op jit(solution)/shard_map/ppermute | solution.py:400
  42.2 4.9 %collective-permute-start.4 = (f32[24,1,128]{2,1,0:T(1,128)S(1)}, f32[24,1,128]{2,1,0:T(1,128)S(1)}, u32[]{:S(2)}, u32[]{:S(2)}) collective-permute-start(f32[24,1,128]{2,1,0:T(1,128)S(1)} %get-tuple-element.33.les_ref), channel_id=1, source_target_pairs={{16,32},{48,64},{80,96},{112,0},{32,16},{64,48},{96,80},{0,112},{1... | collective-permute-start | bytes 36872 | tf_op jit(solution)/shard_map/ppermute | solution.py:400

commit v7 on v5

--- a/solution.py
+++ b/solution.py
@@ -206,11 +206,11 @@
 
 
 def sending_rows(placing_ref, out_ref, send_ref, rows):
+    sending = dot(placing_ref[...].reshape(2 * OWNERS, 2 * LINES), out_ref[...])
     for slot in range(2):
-        sending = dot(placing_ref[slot], out_ref[...])
         for third in range(3):
             send_ref[pl.ds(3 * slot + third, OWNERS, stride=rows), :] = sending[
-                :, third * POINTS : (third + 1) * POINTS
+                slot * OWNERS : (slot + 1) * OWNERS, third * POINTS : (third + 1) * POINTS
             ]
 
 

time: 72.8 us -> 72.8 us (level)
  no operation moved by 1% of the time
where the time goes in v7:
time: 72.8 us; the launch traced here: 72.6 us
  blocking collectives  36.7 us (50%)
  Pallas kernels  20.6 us (28%)
  starting transfers between devices  13.2 us (18%)
  waiting for transfers between devices  1.13 us (2%)
  between operations  0.94 us (1%)
    all_to_all x2, blocking collectives, exchange(): lax.all_to_all(sending, ('grid', 'line'), split_axis=0, concat_axis=0, ti...  36.7 us
    pallas_call x6, Pallas kernels, call(): pl.pallas_call(kernel, out_shape=outputs, in_specs=[in_space] * len(input...  20.6 us
    ppermute x8, starting transfers between devices, beside(): around.append(lax.ppermute(field, axis, pairs + [(b, a) for a, b in pairs]))  13.2 us
  transfers between devices with their start and end apart: 8, of which 1 were waited for; matrix products, arithmetic and copies ran while one was open for 0% of the time, Pallas kernels for 7%

profile of v7, /device:TPU:1, one launch (start us, length us, event | category | flops | bytes accessed | tf_op | source)
XLA Modules:
  0.0 72.6 jit_solution(3378036338866175731)
XLA Ops:
  0.6 5.8 %collective-permute-start.2 = (f32[24,1,128]{2,1,0:T(1,128)}, f32[24,1,128]{2,1,0:T(1,128)S(1)}, u32[]{:S(2)}, u32[]{:S(2)}) collective-permute-start(f32[24,1,128]{2,1,0:T(1,128)} %les_ref.1), channel_id=1, source_target_pairs={{1,2},{3,4},{5,6},{7,8},{9,10},{11,12},{13,14},{15,0},{2,1},{4,3},... | collective-permute-start | bytes 36872 | tf_op jit(solution)/shard_map/ppermute | solution.py:400
  6.5 2.5 %collective-permute-start.1 = (f32[24,1,128]{2,1,0:T(1,128)}, f32[24,1,128]{2,1,0:T(1,128)S(1)}, u32[]{:S(2)}, u32[]{:S(2)}) collective-permute-start(f32[24,1,128]{2,1,0:T(1,128)} %les_ref.1), channel_id=1, source_target_pairs={{16,32},{48,64},{80,96},{112,0},{32,16},{64,48},{96,80},{0,112},{1... | collective-permute-start | bytes 36872 | tf_op jit(solution)/shard_map/ppermute | solution.py:400
  8.9 0.0 collective-permute-start
  9.0 1.7 %collective-permute-start.3 = (f32[24,1,128]{2,1,0:T(1,128)}, f32[24,1,128]{2,1,0:T(1,128)S(1)}, u32[]{:S(2)}, u32[]{:S(2)}) collective-permute-start(f32[24,1,128]{2,1,0:T(1,128)} %les_ref.1), channel_id=1, source_target_pairs={{0,16},{32,48},{64,80},{96,112},{16,0},{48,32},{80,64},{112,96},{1... | collective-permute-start | bytes 36872 | tf_op jit(solution)/shard_map/ppermute | solution.py:400
  10.6 0.0 copy-start.5
  10.6 0.0 copy-start.6
  10.7 3.2 %shard_map.149 = (f32[24,128,128]{2,1,0:T(8,128)S(1)}, bf16[192,192]{1,0:T(8,128)(2,1)S(1)}, bf16[192,192]{1,0:T(8,128)(2,1)S(1)}, f32[24,128]{1,0:T(8,128)S(1)}) custom-call(f32[128,24,128]{2,1,0:T(8,128)} %bitcast.13, s32[2,1,1,128]{3,2,1,0:T(1,128)} %start_ref.1, f32[1,24]{1,0:T(1,128)} %bitcast.14, f32[1,128]{1,0:T(1,128)} %constant.8.clone.eigen_hbm, ...), custom_call_target="tpu_custom_call" | custom-call | flops 4000000000 | bytes 3573856 | tf_op jit(solution)/shard_map/pallas_call | solution.py:383
  13.9 0.0 collective-permute-done.2.line_odd_ref
  13.9 0.0 collective-permute-done.1.grid_odd_ref
  13.9 0.0 collective-permute-done.line_even_ref
  13.9 0.0 collective-permute-done.3.grid_even_ref
  13.9 0.0 copy-done
  13.9 0.0 copy-done.1
  13.9 0.0 copy-done.2
  13.9 0.0 copy-done.4
  13.9 0.0 copy-done.5
  14.0 0.0 copy-done.6
  14.0 5.7 %shard_map.150 = (f32[24,128,128]{2,1,0:T(8,128)S(1)}, f32[896,128]{1,0:T(8,128)S(1)}, f32[24,128]{1,0:T(8,128)S(1)}, f32[128,128]{1,0:T(8,128)S(1)}, bf16[2,128,256]{2,1,0:T(8,128)(2,1)S(1)}) custom-call(f32[24,128,128]{2,1,0:T(8,128)S(1)} %get-tuple-element.23.mixed_ref, f32[24,1,128]{2,1,0:T(1,128)S(1)} %copy-done, ...), custom_call_target="tpu_custom_call" | custom-call | flops 6000000000 | bytes 4026880 | tf_op jit(solution)/shard_map/pallas_call | solution.py:383
  19.6 17.6 %all_to_all.10 = f32[128,1,896]{2,1,0:T(1,128)S(1)} all-to-all(f32[128,1,896]{2,1,0:T(1,128)S(1)} %bitcast.8), channel_id=1, replica_groups=mesh['grid'=8,'line'=16] {'grid','line'}, dimensions={0} | all-to-all | bytes 917504 | tf_op jit(solution)/shard_map/all_to_all | solution.py:433
  37.2 1.9 %shard_map.151 = (f32[24,1,128]{2,1,0:T(1,128)S(1)}, f32[24,128,128]{2,1,0:T(8,128)S(1)}, f32[8,128]{1,0:T(8,128)S(1)}) custom-call(f32[896,128]{1,0:T(8,128)S(1)} %bitcast.9, f32[24,128,128]{2,1,0:T(8,128)S(1)} %get-tuple-element.27.state_ref, f32[24,128]{1,0:T(8,128)S(1)} %get-tuple-element.28.mid_ref), custom_call_target="tpu_custom_call" | custom-call | flops 3000000000 | bytes 3633152 | tf_op jit(solution)/shard_map/pallas_call | solution.py:383
  39.1 1.8 %collective-permute-start.7 = (f32[24,1,128]{2,1,0:T(1,128)S(1)}, f32[24,1,128]{2,1,0:T(1,128)S(1)}, u32[]{:S(2)}, u32[]{:S(2)}) collective-permute-start(f32[24,1,128]{2,1,0:T(1,128)S(1)} %get-tuple-element.33.les_ref), channel_id=1, source_target_pairs={{1,2},{3,4},{5,6},{7,8},{9,10},{11,12},{13,14},{15,0},{2,1},{4,3},... | collective-permute-start | bytes 36872 | tf_op jit(solution)/shard_map/ppermute | solution.py:400
  40.9 0.5 collective-permute-start.6
  41.4 0.1 collective-permute-start.5
  41.4 0.9 %collective-permute-start.4 = (f32[24,1,128]{2,1,0:T(1,128)S(1)}, f32[24,1,128]{2,1,0:T(1,128)S(1)}, u32[]{:S(2)}, u32[]{:S(2)}) collective-permute-start(f32[24,1,128]{2,1,0:T(1,128)S(1)} %get-tuple-element.33.les_ref), channel_id=1, source_target_pairs={{0,16},{32,48},{64,80},{96,112},{16,0},{48,32},{80,64},{112,96},{1... | collective-permute-start | bytes 36872 | tf_op jit(solution)/shard_map/ppermute | solution.py:400
  42.3 1.6 %shard_map.152 = (f32[24,128,128]{2,1,0:T(8,128)S(1)}, s32[128,128]{1,0:T(8,128)S(1)}, s32[128,128]{1,0:T(8,128)S(1)}, bf16[1024,512]{1,0:T(8,128)(2,1)S(1)}) custom-call(f32[24,128,128]{2,1,0:T(8,128)S(1)} %get-tuple-element.29.state_ref, s32[2,1,1,128]{3,2,1,0:T(1,128)S(1)} %copy-done.3, f32[24,128]{1,0:T(8,128)S(1)} %get-tuple-element.30.scale_ref, ...), custom_call_target="tpu_custom_call" | custom-call | flops 3000000000 | bytes 4606976 | tf_op jit(solution)/shard_map/pallas_call | solution.py:383
  43.9 1.1 %collective-permute-done.7.line_odd_ref = f32[24,1,128]{2,1,0:T(1,128)S(1)} collective-permute-done((f32[24,1,128]{2,1,0:T(1,128)S(1)}, f32[24,1,128]{2,1,0:T(1,128)S(1)}, u32[]{:S(2)}, u32[]{:S(2)}) %collective-permute-start.7) | collective-permute-done | bytes 12320 | tf_op jit(solution)/shard_map/ppermute | solution.py:400
  45.1 0.0 collective-permute-done.6.grid_odd_ref
  45.1 0.0 collective-permute-done.5.line_even_ref
  45.1 0.0 collective-permute-done.4.grid_even_ref
  45.1 5.5 %shard_map.153 = (f32[24,128,128]{2,1,0:T(8,128)S(1)}, f32[768,128]{1,0:T(8,128)S(1)}, f32[24,128]{1,0:T(8,128)S(1)}) custom-call(f32[24,128,128]{2,1,0:T(8,128)S(1)} %get-tuple-element.32.mixed_ref, f32[24,1,128]{2,1,0:T(1,128)S(1)} %get-tuple-element.33.les_ref, f32[24,1,128]{2,1,0:T(1,128)S(1)} %collective-permute-done.4.grid_even_ref, ...), custom_call_target="tpu_custom_call" | custom-call | flops 6000000000 | bytes 4087808 | tf_op jit(solution)/shard_map/pallas_call | solution.py:383
  50.6 19.1 %all_to_all.11 = f32[128,1,768]{2,1,0:T(1,128)S(1)} all-to-all(f32[128,1,768]{2,1,0:T(1,128)S(1)} %bitcast.10), channel_id=1, replica_groups=mesh['grid'=8,'line'=16] {'grid','line'}, dimensions={0} | all-to-all | bytes 786432 | tf_op jit(solution)/shard_map/all_to_all | solution.py:433
  69.7 2.8 %shard_map.154 = (f32[24,1,128]{2,1,0:T(1,128)}, f32[3072,128]{1,0:T(8,128)}) custom-call(f32[768,128]{1,0:T(8,128)S(1)} %bitcast.11, f32[24,128,128]{2,1,0:T(8,128)S(1)} %get-tuple-element.39.state_ref, f32[24,128]{1,0:T(8,128)S(1)} %get-tuple-element.40.mid_ref, bf16[1024,512]{1,0:T(8,128)(2,1)S(1)} %get-tuple-element.41.hits_ref), custom_call_target="tpu_custom_call" | custom-call | flops 3000000000 | bytes 4612096 | tf_op jit(solution)/shard_map/pallas_call | solution.py:383
  (10 shorter events, 0.0 us)
Async XLA Ops:
  0.6 13.2 %collective-permute-start.2 = (f32[24,1,128]{2,1,0:T(1,128)}, f32[24,1,128]{2,1,0:T(1,128)S(1)}, u32[]{:S(2)}, u32[]{:S(2)}) collective-permute-start(f32[24,1,128]{2,1,0:T(1,128)} %les_ref.1), channel_id=1, source_target_pairs={{1,2},{3,4},{5,6},{7,8},{9,10},{11,12},{13,14},{15,0},{2,1},{4,3},... | collective-permute-start | bytes 36872 | tf_op jit(solution)/shard_map/ppermute | solution.py:400
  6.5 7.4 %collective-permute-start.1 = (f32[24,1,128]{2,1,0:T(1,128)}, f32[24,1,128]{2,1,0:T(1,128)S(1)}, u32[]{:S(2)}, u32[]{:S(2)}) collective-permute-start(f32[24,1,128]{2,1,0:T(1,128)} %les_ref.1), channel_id=1, source_target_pairs={{16,32},{48,64},{80,96},{112,0},{32,16},{64,48},{96,80},{0,112},{1... | collective-permute-start | bytes 36872 | tf_op jit(solution)/shard_map/ppermute | solution.py:400
  8.9 4.9 %collective-permute-start = (f32[24,1,128]{2,1,0:T(1,128)}, f32[24,1,128]{2,1,0:T(1,128)S(1)}, u32[]{:S(2)}, u32[]{:S(2)}) collective-permute-start(f32[24,1,128]{2,1,0:T(1,128)} %les_ref.1), channel_id=1, source_target_pairs={{0,1},{2,3},{4,5},{6,7},{8,9},{10,11},{12,13},{14,15},{1,0},{3,2},... | collective-permute-start | bytes 36872 | tf_op jit(solution)/shard_map/ppermute | solution.py:400
  9.0 4.9 %collective-permute-start.3 = (f32[24,1,128]{2,1,0:T(1,128)}, f32[24,1,128]{2,1,0:T(1,128)S(1)}, u32[]{:S(2)}, u32[]{:S(2)}) collective-permute-start(f32[24,1,128]{2,1,0:T(1,128)} %les_ref.1), channel_id=1, source_target_pairs={{0,16},{32,48},{64,80},{96,112},{16,0},{48,32},{80,64},{112,96},{1... | collective-permute-start | bytes 36872 | tf_op jit(solution)/shard_map/ppermute | solution.py:400
  10.6 3.3 %copy-start = (f32[24,1,128]{2,1,0:T(1,128)S(1)}, f32[24,1,128]{2,1,0:T(1,128)}, u32[]{:S(2)}) copy-start(f32[24,1,128]{2,1,0:T(1,128)} %les_ref.1) | copy-start | bytes 36868
  10.6 3.3 %copy-start.1 = (s32[2,1,1,128,1]{3,4,2,1,0:T(1,128)S(1)}, s32[2,1,1,128,1]{3,4,2,1,0:T(1,128)}, u32[]{:S(2)}) copy-start(s32[2,1,1,128,1]{3,4,2,1,0:T(1,128)} %param.17) | copy-start | bytes 3076
  10.6 3.3 %copy-start.2 = (s32[2,1,1,128]{3,2,1,0:T(1,128)S(1)}, s32[2,1,1,128]{3,2,1,0:T(1,128)}, u32[]{:S(2)}) copy-start(s32[2,1,1,128]{3,2,1,0:T(1,128)} %line_ref.1) | copy-start | bytes 3076
  10.6 3.3 %copy-start.4 = (s32[2,1,1,128]{3,2,1,0:T(1,128)S(1)}, s32[2,1,1,128]{3,2,1,0:T(1,128)}, u32[]{:S(2)}) copy-start(s32[2,1,1,128]{3,2,1,0:T(1,128)} %from_ref.3) | copy-start | bytes 3076
  10.6 3.3 %copy-start.5 = (s32[2,1,1,128]{3,2,1,0:T(1,128)S(1)}, s32[2,1,1,128]{3,2,1,0:T(1,128)}, u32[]{:S(2)}) copy-start(s32[2,1,1,128]{3,2,1,0:T(1,128)} %to_ref.3) | copy-start | bytes 3076
  10.6 3.3 %copy-start.6 = (s32[1,1,128]{2,1,0:T(1,128)S(1)}, s32[1,1,128]{2,1,0:T(1,128)}, u32[]{:S(2)}) copy-start(s32[1,1,128]{2,1,0:T(1,128)} %counts_ref.1) | copy-start | bytes 1540
  37.2 5.1 %copy-start.3 = (s32[2,1,1,128]{3,2,1,0:T(1,128)S(1)}, s32[2,1,1,128]{3,2,1,0:T(1,128)}, u32[]{:S(2)}) copy-start(s32[2,1,1,128]{3,2,1,0:T(1,128)} %start_ref.1) | copy-start | bytes 3076
  37.2 5.1 %copy-start.7 = (bf16[256,256]{1,0:T(8,128)(2,1)S(1)}, bf16[256,256]{1,0:T(8,128)(2,1)}, u32[]{:S(2)}) copy-start(bf16[256,256]{1,0:T(8,128)(2,1)} %constant.7.clone.second_hbm.second_ref) | copy-start | bytes 393220
  37.2 5.1 %copy-start.8 = (bf16[256,256]{1,0:T(8,128)(2,1)S(1)}, bf16[256,256]{1,0:T(8,128)(2,1)}, u32[]{:S(2)}) copy-start(bf16[256,256]{1,0:T(8,128)(2,1)} %constant.6.clone.first_hbm.first_ref) | copy-start | bytes 393220
  39.1 5.9 %collective-permute-start.7 = (f32[24,1,128]{2,1,0:T(1,128)S(1)}, f32[24,1,128]{2,1,0:T(1,128)S(1)}, u32[]{:S(2)}, u32[]{:S(2)}) collective-permute-start(f32[24,1,128]{2,1,0:T(1,128)S(1)} %get-tuple-element.33.les_ref), channel_id=1, source_target_pairs={{1,2},{3,4},{5,6},{7,8},{9,10},{11,12},{13,14},{15,0},{2,1},{4,3},... | collective-permute-start | bytes 36872 | tf_op jit(solution)/shard_map/ppermute | solution.py:400
  40.9 4.2 %collective-permute-start.6 = (f32[24,1,128]{2,1,0:T(1,128)S(1)}, f32[24,1,128]{2,1,0:T(1,128)S(1)}, u32[]{:S(2)}, u32[]{:S(2)}) collective-permute-start(f32[24,1,128]{2,1,0:T(1,128)S(1)} %get-tuple-element.33.les_ref), channel_id=1, source_target_pairs={{16,32},{48,64},{80,96},{112,0},{32,16},{64,48},{96,80},{0,112},{1... | collective-permute-start | bytes 36872 | tf_op jit(solution)/shard_map/ppermute | solution.py:400
  41.4 3.7 %collective-permute-start.5 = (f32[24,1,128]{2,1,0:T(1,128)S(1)}, f32[24,1,128]{2,1,0:T(1,128)S(1)}, u32[]{:S(2)}, u32[]{:S(2)}) collective-permute-start(f32[24,1,128]{2,1,0:T(1,128)S(1)} %get-tuple-element.33.les_ref), channel_id=1, source_target_pairs={{0,1},{2,3},{4,5},{6,7},{8,9},{10,11},{12,13},{14,15},{1,0},{3,2},... | collective-permute-start | bytes 36872 | tf_op jit(solution)/shard_map/ppermute | solution.py:400
  41.4 3.6 %collective-permute-start.4 = (f32[24,1,128]{2,1,0:T(1,128)S(1)}, f32[24,1,128]{2,1,0:T(1,128)S(1)}, u32[]{:S(2)}, u32[]{:S(2)}) collective-permute-start(f32[24,1,128]{2,1,0:T(1,128)S(1)} %get-tuple-element.33.les_ref), channel_id=1, source_target_pairs={{0,16},{32,48},{64,80},{96,112},{16,0},{48,32},{80,64},{112,96},{1... | collective-permute-start | bytes 36872 | tf_op jit(solution)/shard_map/ppermute | solution.py:400
